TPU v7x, 32 devices: a whole 2x2x4 slice. The times are simulated.
32 devices in a mesh: batch: 4 (over y, core), own: 8 (over z, x).
Axes of the slice: x: 2, y: 2, z: 4, core: 2. Of those that a mesh axis runs over, the one named last changes fastest.
Arguments:
- hidden_in: bfloat16 [4, 1024, 2048], P('batch', 'own'), may hold values from -6 to 6
- norm_gain: float32 [2048], replicated, may hold values from 0.5 to 1.5
- input_proj: bfloat16 [3, 2048, 2, 4096], P(None, None, None, 'own'), may hold values from -0.125 to 0.125
- conv_weight: float32 [4, 4096], replicated, may hold values from -3 to 3
- conv_bias: float32 [4096], replicated, may hold values from -0.5 to 0.5
- state_proj: bfloat16 [3, 4096, 160], P(None, 'own'), may hold values from -0.09375 to 0.09375
- step_proj: bfloat16 [3, 128, 4096], P(None, None, 'own'), may hold values from -0.5 to 0.5
- step_bias: float32 [3, 4096], P(None, 'own'), may hold values from -9 to -3
- log_decay: float32 [16, 4096], replicated, may hold values from 0 to 2.8
- skip_gain: float32 [4096], replicated, may hold values from 0.5 to 1.5
- output_proj: bfloat16 [3, 4096, 2048], P(None, 'own'), may hold values from -0.5 to 0.5
- modality: int32 [4, 1024], P('batch'), may hold values from 0 to 2, as said below
- grad_out: bfloat16 [4, 1024, 2048], P('batch', 'own'), may hold values from -6 to 6
Outputs:
- block_out: bfloat16 [4, 1024, 2048], P('batch', 'own')
- grad_hidden: float32 [4, 1024, 2048], P('batch', 'own')
- grad_gain: float32 [2048], replicated
- grad_input_proj: float32 [3, 2048, 2, 4096], P(None, None, None, 'own')
- grad_conv_weight: float32 [4, 4096], replicated
- grad_conv_bias: float32 [4096], replicated
- grad_state_proj: float32 [3, 4096, 160], P(None, 'own')
- grad_step_proj: float32 [3, 128, 4096], P(None, None, 'own')
- grad_step_bias: float32 [3, 4096], P(None, 'own')
- grad_log_decay: float32 [16, 4096], replicated
- grad_skip_gain: float32 [4096], replicated
- grad_output_proj: float32 [3, 4096, 2048], P(None, 'own')
Inputs may be any that keep to these rules, and one draw needn't show every extreme that they name: Among the 1 sequence of one batch index (an aligned block of rows), each modality has at most 448 tokens, and one modality has exactly 448.
All inputs are finite; a program needn't handle non-finite values.
Results may differ from a plain program's by a relative error of at most 0.011.
The roundings to bfloat16 on the way count: a program that leaves them out, or rounds other values in their place, can miss the bound.
Values may be sent and summed in bfloat16 or wider, within the bound.
No kernel may reach another device: no remote copies, remote signals or barrier semaphores. Data moves between devices by JAX's collectives and lax.ppermute only.
A program may use at most 320 MiB of HBM per device.

v0:
```python
import jax
import jax.numpy as jnp
from jax import lax
from jax.sharding import PartitionSpec as P

M = 3


epsilon = 1e-05
time_block = 64
highest = lax.Precision.HIGHEST


def carried_in(value, axis, join, neutral, backward):
    count, mine = (lax.axis_size(axis), lax.axis_index(axis))
    pieces = jax.tree.map(lambda part: lax.all_gather(part, axis), value)
    if backward:
        pieces = jax.tree.map(lambda part: part[::-1], pieces)
        mine = count - 1 - mine
    subtotal = jax.tree.map(
        lambda part, zero: jnp.full_like(part, 0) + jnp.asarray(zero, part.dtype), value, neutral
    )

    def step(position, subtotal):
        longer = join(subtotal, jax.tree.map(lambda part: part[position], pieces))
        return jax.tree.map(lambda new, old: jnp.where(position < mine, new, old), longer, subtotal)

    return lax.fori_loop(0, count - 1, step, subtotal)


def group_plan(modal_rows, capacity):
    row_count = modal_rows.shape[0]
    positions = lax.iota(jnp.int32, row_count)
    sort_keys = modal_rows * row_count + positions
    sorted_ids = jnp.argsort(sort_keys)
    modal_ids = lax.iota(jnp.int32, M)
    counts = jnp.sum((modal_rows[:, None] == modal_ids[None, :]).astype(jnp.int32), axis=0)
    starts = jnp.cumsum(counts) - counts
    slot_ids = lax.iota(jnp.int32, M * capacity)
    slot_modal = slot_ids // capacity
    within = slot_ids - slot_modal * capacity
    slot_count = jnp.take(counts, slot_modal)
    slot_start = jnp.take(starts, slot_modal)
    source_pos = jnp.minimum(slot_start + within, row_count - 1)
    token_of_slot = jnp.where(within < slot_count, jnp.take(sorted_ids, source_pos), row_count)
    rank_of_token = jnp.zeros((row_count,), jnp.int32).at[sorted_ids].set(positions)
    slot_of_token = modal_rows * capacity + rank_of_token - jnp.take(starts, modal_rows)
    return (token_of_slot, slot_of_token)


def run_scan(act_vec, step_vec, b_state, c_state, rates, skip_vec, initial):
    seq_count, length, chans = act_vec.shape
    block_len = min(time_block, length)

    def advance(carried, inputs):
        act_t, step_t, write_t, read_t = inputs
        decays = jnp.exp(step_t[:, None, :] * rates[None])
        carried = decays * carried + (step_t * act_t)[:, None, :] * write_t[:, :, None]
        emitted = jnp.sum(carried * read_t[:, :, None], axis=1) + skip_vec * act_t
        return (carried, emitted)

    def run_block(carried, inputs):
        return lax.scan(advance, carried, inputs, unroll=8)

    def by_time(series):
        return jnp.transpose(series, (1, 0, 2)).reshape(
            length // block_len, block_len, seq_count, series.shape[2]
        )

    final, emitted = lax.scan(
        jax.checkpoint(run_block),
        initial,
        (by_time(act_vec), by_time(step_vec), by_time(b_state), by_time(c_state)),
    )
    return (jnp.transpose(emitted.reshape(length, seq_count, chans), (1, 0, 2)), final)


def zero_start_scan(act_vec, step_vec, b_state, c_state, log_part, skip_vec):
    initial = jnp.zeros((act_vec.shape[0], log_part.shape[0], act_vec.shape[2]), jnp.float32)
    return run_scan(act_vec, step_vec, b_state, c_state, -jnp.exp(log_part), skip_vec, initial)


def start_effect(step_vec, c_state, log_part, initial):
    rates = -jnp.exp(log_part)

    def one_seq(inputs):
        step_one, read_one, start_one = inputs
        running = jnp.cumsum(step_one, axis=0)
        decayed = jnp.exp(rates[None] * running[:, None, :]) * start_one[None]
        return jnp.einsum("ln,lne->le", read_one, decayed, precision=highest)

    return lax.map(jax.checkpoint(one_seq), (step_vec, c_state, initial))


def carried_start(step_vec, log_part, initial):
    rates = -jnp.exp(log_part)
    return jnp.exp(rates[None] * jnp.sum(step_vec, axis=1)[:, None, :]) * initial


def gate_apply(scanned, gate_vec):
    return scanned * jax.nn.silu(gate_vec)


def norm_rows(rows, gain):
    mean_sq = jnp.mean(rows * rows, axis=-1, keepdims=True)
    return rows * lax.rsqrt(mean_sq + epsilon) * gain


def chain_fwd(earlier, later):
    return (earlier[0] * later[0], later[0] * earlier[1] + later[1])


def chain_back(earlier, later):
    return (later[0] * earlier[0], later[1] + later[0] * earlier[1])


def per_device(
    hidden_in,
    norm_gain,
    input_proj,
    conv_weight,
    conv_bias,
    state_proj,
    step_proj,
    step_bias,
    log_decay,
    skip_gain,
    output_proj,
    modality,
    grad_out,
):
    seq_count, span_len, model_width = hidden_in.shape
    own_index = lax.axis_index("own")
    zero_index = own_index * 0
    seq_len = modality.shape[1]
    group_rows = seq_count * seq_len
    capacity = 7 * group_rows // 16
    channels = input_proj.shape[3]
    full_width = conv_weight.shape[1]
    rank_width = step_proj.shape[1]
    state_width = log_decay.shape[0]
    kernel = conv_weight.shape[0]
    chan_at = own_index * channels
    rows_at = own_index * span_len
    token_of_slot, slot_of_token = group_plan(modality.reshape(group_rows), capacity)

    def dispatch(series):
        flat = series.reshape(group_rows, series.shape[-1])
        return jnp.take(flat, token_of_slot, axis=0, mode="fill", fill_value=0).reshape(
            M, capacity, series.shape[-1]
        )

    def combine(buffer):
        flat = buffer.reshape(M * capacity, buffer.shape[-1])
        return jnp.take(flat, slot_of_token, axis=0).reshape(seq_count, seq_len, buffer.shape[-1])

    resid = hidden_in.astype(jnp.float32)
    normed, norm_pull = jax.vjp(norm_rows, resid, norm_gain)
    normed_q = normed.astype(jnp.bfloat16)
    gathered = lax.all_gather(normed_q, "own", axis=1, tiled=True)
    normed_buf = dispatch(gathered)
    in_flat = input_proj.reshape(M, model_width, 2 * channels)
    mixed = combine(
        jnp.einsum("mcd,mdf->mcf", normed_buf, in_flat, preferred_element_type=jnp.float32)
    ).astype(jnp.bfloat16)
    conv_in = mixed[..., :channels]
    gate_in = mixed[..., channels:]
    conv_w_part = lax.dynamic_slice_in_dim(conv_weight, chan_at, channels, 1)
    conv_b_part = lax.dynamic_slice_in_dim(conv_bias, chan_at, channels, 0)

    def conv_fn(source, weight, offset_vec):
        padded = jnp.pad(source, ((0, 0), (kernel - 1, 0), (0, 0)))
        summed = offset_vec + jnp.zeros_like(source)
        for offset in range(kernel):
            summed = summed + weight[offset] * padded[:, offset : offset + seq_len]
        return jax.nn.silu(summed)

    conv_out, conv_pull = jax.vjp(conv_fn, conv_in.astype(jnp.float32), conv_w_part, conv_b_part)
    act_q = conv_out.astype(jnp.bfloat16)
    act_buf = dispatch(act_q)
    proj_part = combine(
        jnp.einsum("mce,mep->mcp", act_buf, state_proj, preferred_element_type=jnp.float32)
    )
    proj_full = lax.psum(proj_part, "own")
    step_in = proj_full[..., :rank_width].astype(jnp.bfloat16)
    b_state = proj_full[..., rank_width : rank_width + state_width]
    c_state = proj_full[..., rank_width + state_width :]
    step_buf = dispatch(step_in)
    step_lin = combine(
        jnp.einsum("mcr,mre->mce", step_buf, step_proj, preferred_element_type=jnp.float32)
    )
    bias_rows = jnp.zeros((seq_count, seq_len, channels), jnp.float32)
    for modal_id in range(M):
        bias_rows = jnp.where(modality[..., None] == modal_id, step_bias[modal_id], bias_rows)
    pre_step = step_lin + bias_rows
    step_q = jax.nn.softplus(pre_step).astype(jnp.bfloat16)
    act_k, gate_k, step_k = (
        lax.all_to_all(act_q, "own", split_axis=1, concat_axis=2, tiled=True),
        lax.all_to_all(gate_in, "own", split_axis=1, concat_axis=2, tiled=True),
        lax.all_to_all(step_q, "own", split_axis=1, concat_axis=2, tiled=True),
    )
    act_f = act_k.astype(jnp.float32)
    step_f = step_k.astype(jnp.float32)
    gate_f = gate_k.astype(jnp.float32)
    b_rows = lax.dynamic_slice_in_dim(b_state, rows_at, span_len, 1)
    c_rows = lax.dynamic_slice_in_dim(c_state, rows_at, span_len, 1)
    rates_full = -jnp.exp(log_decay)
    (emitted_zero, final_local), scan_pull = jax.vjp(
        zero_start_scan, act_f, step_f, b_rows, c_rows, log_decay, skip_gain
    )
    total_decay = jnp.exp(rates_full[None] * jnp.sum(step_f, axis=1)[:, None, :])
    initial = carried_in(
        (total_decay, final_local),
        "own",
        chain_fwd,
        (jnp.ones_like(total_decay), jnp.zeros_like(final_local)),
        False,
    )[1]
    extra, effect_pull = jax.vjp(start_effect, step_f, c_rows, log_decay, initial)
    scanned_k = emitted_zero + extra
    gated_k, gate_pull = jax.vjp(gate_apply, scanned_k, gate_f)
    gated_c = lax.all_to_all(
        gated_k.astype(jnp.bfloat16), "own", split_axis=2, concat_axis=1, tiled=True
    )
    gated_buf = dispatch(gated_c)
    out_term = combine(
        jnp.einsum("mce,med->mcd", gated_buf, output_proj, preferred_element_type=jnp.float32)
    )
    branch = lax.psum_scatter(out_term, "own", scatter_dimension=1, tiled=True)
    block_out = (resid + branch).astype(jnp.bfloat16)
    cot_all = lax.all_gather(grad_out, "own", axis=1, tiled=True)
    cot_buf = dispatch(cot_all)
    grad_out_proj = jnp.einsum(
        "mce,mcd->med", gated_buf, cot_buf, preferred_element_type=jnp.float32
    )
    grad_gated = combine(
        jnp.einsum("mcd,med->mce", cot_buf, output_proj, preferred_element_type=jnp.float32)
    ).astype(jnp.bfloat16)
    grad_gated_k = lax.all_to_all(grad_gated, "own", split_axis=1, concat_axis=2, tiled=True)
    grad_scanned_k, grad_gate_k = gate_pull(grad_gated_k.astype(jnp.float32))
    effect_grads = effect_pull(grad_scanned_k)
    end_grad = carried_in(
        (total_decay, effect_grads[3]),
        "own",
        chain_back,
        (jnp.ones_like(total_decay), jnp.zeros_like(final_local)),
        True,
    )[1]
    carried_out, carry_pull = jax.vjp(carried_start, step_f, log_decay, initial)
    carry_grads = carry_pull(end_grad)
    scan_grads = scan_pull((grad_scanned_k, end_grad))
    grad_step_k = scan_grads[1] + effect_grads[0] + carry_grads[0]
    grad_act_scan, grad_gate, grad_step = (
        lax.all_to_all(
            scan_grads[0].astype(jnp.bfloat16), "own", split_axis=2, concat_axis=1, tiled=True
        ),
        lax.all_to_all(
            grad_gate_k.astype(jnp.bfloat16), "own", split_axis=2, concat_axis=1, tiled=True
        ),
        lax.all_to_all(
            grad_step_k.astype(jnp.bfloat16), "own", split_axis=2, concat_axis=1, tiled=True
        ),
    )
    bc_rows = jnp.concatenate([scan_grads[2], scan_grads[3] + effect_grads[1]], axis=-1)
    grad_bc = lax.dynamic_update_slice(
        jnp.zeros((seq_count, seq_len, 2 * state_width), jnp.float32),
        bc_rows,
        (zero_index, rows_at, zero_index),
    )
    grad_logd = scan_grads[4] + effect_grads[2] + carry_grads[1]
    grad_skip = scan_grads[5]
    grad_pre = grad_step.astype(jnp.float32) * jax.nn.sigmoid(pre_step)
    grad_bias_part = jnp.sum(dispatch(grad_pre), axis=1)
    grad_lin_buf = dispatch(grad_pre.astype(jnp.bfloat16))
    grad_step_part = jnp.einsum(
        "mcr,mce->mre", step_buf, grad_lin_buf, preferred_element_type=jnp.float32
    )
    grad_step_in = combine(
        jnp.einsum("mce,mre->mcr", grad_lin_buf, step_proj, preferred_element_type=jnp.float32)
    )
    grad_proj_part = jnp.concatenate([grad_step_in, grad_bc], axis=-1)
    grad_proj = lax.psum(grad_proj_part.astype(jnp.bfloat16), "own")
    grad_proj_buf = dispatch(grad_proj)
    grad_state_part = jnp.einsum(
        "mce,mcp->mep", act_buf, grad_proj_buf, preferred_element_type=jnp.float32
    )
    grad_act = combine(
        jnp.einsum("mcp,mep->mce", grad_proj_buf, state_proj, preferred_element_type=jnp.float32)
    ) + grad_act_scan.astype(jnp.float32)
    grad_conv_in, grad_conv_w_part, grad_conv_b_part = conv_pull(grad_act)
    grad_mixed = jnp.concatenate([grad_conv_in, grad_gate.astype(jnp.float32)], axis=-1).astype(
        jnp.bfloat16
    )
    grad_mixed_buf = dispatch(grad_mixed)
    grad_in_part = jnp.einsum(
        "mcd,mcf->mdf", normed_buf, grad_mixed_buf, preferred_element_type=jnp.float32
    ).reshape(M, model_width, 2, channels)
    grad_normed_term = combine(
        jnp.einsum("mcf,mdf->mcd", grad_mixed_buf, in_flat, preferred_element_type=jnp.float32)
    )
    grad_normed = lax.psum_scatter(grad_normed_term, "own", scatter_dimension=1, tiled=True)
    grad_resid, grad_gain_part = norm_pull(grad_normed)
    grad_hidden = grad_resid + grad_out.astype(jnp.float32)
    grad_conv_w_full = lax.dynamic_update_slice(
        jnp.zeros((kernel, full_width), jnp.float32), grad_conv_w_part, (zero_index, chan_at)
    )
    grad_conv_b_full = lax.dynamic_update_slice(
        jnp.zeros((full_width,), jnp.float32), grad_conv_b_part, (chan_at,)
    )
    shared = lax.psum(
        (grad_gain_part, grad_conv_w_full, grad_conv_b_full, grad_logd, grad_skip), ("batch", "own")
    )
    summed = lax.psum(
        (grad_in_part, grad_state_part, grad_step_part, grad_bias_part, grad_out_proj), "batch"
    )
    return (
        block_out,
        grad_hidden,
        shared[0],
        summed[0],
        shared[1],
        shared[2],
        summed[1],
        summed[2],
        summed[3],
        shared[3],
        shared[4],
        summed[4],
    )


def solution(mesh):
    placed = (
        P("batch", "own", None),
        P(),
        P(None, None, None, "own"),
        P(),
        P(),
        P(None, "own", None),
        P(None, None, "own"),
        P(None, "own"),
        P(),
        P(),
        P(None, "own", None),
        P("batch", None),
        P("batch", "own", None),
    )
    return jax.shard_map(
        per_device,
        mesh=mesh,
        in_specs=placed,
        out_specs=(
            P("batch", "own", None),
            P("batch", "own", None),
            P(),
            P(None, None, None, "own"),
            P(),
            P(),
            P(None, "own", None),
            P(None, None, "own"),
            P(None, "own"),
            P(),
            P(),
            P(None, "own", None),
        ),
        check_vma=False,
    )
```

profile of v0, /device:TPU:0, one launch (start us, length us, event | category | flops | bytes accessed | tf_op | source)
XLA Modules:
  0.0 2811.2 jit_solution(9358457438066097852)
XLA Ops:
  11.7 21.0 reshape.5724
  57.5 29.4 %all-gather.9.cloned.1.call-done = bf16[1,1024,2048]{2,1,0:T(8,128)(2,1)} async-done(((bf16[1,128,2048]{2,1,0:T(8,128)(2,1)}), bf16[1,1024,2048]{2,1,0:T(8,128)(2,1)}) %all-gather.9.cloned.1.call-update) | async-done | bytes 4194320 | tf_op jit(solution)/shard_map/all_gather | solution.py:160
  86.9 15.4 gather_fusion.8
  102.2 58.4 %all-gather.11.cloned.1.call-done = bf16[1,1024,2048]{2,1,0:T(8,128)(2,1)} async-done(((bf16[1,128,2048]{2,1,0:T(8,128)(2,1)}), bf16[1,1024,2048]{2,1,0:T(8,128)(2,1)}) %all-gather.11.cloned.1.call-update) | async-done | bytes 4194320 | tf_op jit(solution)/shard_map/all_gather | solution.py:231
  160.7 15.2 gather_fusion.13
  175.8 7.7 broadcast_select_fusion
  183.6 11.0 fusion.232
  194.6 5.3 gather_fusion.1
  220.3 8.1 reduce.183
  235.7 92.2 %all-reduce.17.cloned.1.call-done = f32[1,1024,160]{2,1,0:T(8,128)} async-done(((f32[1,1024,160]{2,1,0:T(8,128)}), f32[1,1024,160]{2,1,0:T(8,128)}) %all-reduce.17.cloned.1.call-update) | async-done | bytes 655376 | tf_op jit(solution)/shard_map/psum | solution.py:184
  345.3 8.1 reduce.182
  360.4 7.5 fusion.235
  373.8 8.1 reduce.181
  398.4 6.0 all-to-all-start.4
  404.5 5.8 reshape.6024
  430.6 66.2 %while.217 = (s32[]{:T(128)}, f32[1,16,4096]{2,1,0:T(8,128)S(1)}, f32[2,64,1,4096]{3,1,2,0:T(8,128)}, f32[2,1,16,4096]{3,2,1,0:T(8,128)}, f32[2,64,1,4096]{3,2,1...) while((s32[]{:T(128)}, f32[1,16,4096]{2,1,0:T(8,128)S(1)}, ...), condition=%wide.region_17.22_spmd, body=%wide.region_6.21_spmd.sunk | while | flops 4784138 | bytes 11227194 | solution.py:70
  434.8 26.1 while.223
  467.9 26.1 while.223
  501.7 9.0 reduce.180
  513.3 6.0 all-to-all-start.2
  519.4 5.9 reshape.6032
  534.6 25.9 all-to-all-done.2
  560.5 5.8 reshape.6028
  584.8 8.9 while.218
  593.8 23.9 fusion.151
  626.7 19.9 multiply_reduce_fusion.32
  666.9 5.5 copy.285
  672.4 24.8 reduce.184
  703.6 5.5 copy.262
  709.2 24.4 reduce.187
  735.9 39.0 %reduce_window_sum.44 = f32[1,128,4096]{2,1,0:T(8,128)} reduce-window(f32[1,128,4096]{2,1,0:T(8,128)} %bitcast.1686, f32[]{:T(128)} %constant.472.clone.1), window={size=1x128x1 pad=0_0x0_127x0_0}, to_apply=%region_66.72 | reduce-window | flops 66584576 | bytes 4194308 | tf_op jit(solution)/shard_map/transpose(jvp())/while/body/eval_jaxpr/checkpoint/jit(cumsum)/reduce_window_sum | solution.py:88
  778.0 8.9 while.219
  787.0 5.9 all-to-all-start.3
  796.1 569.0 %while.222 = (s32[]{:T(128)}, f32[16,4096]{1,0:T(8,128)}, f32[4096]{0:T(1024)}, f32[1,16,4096]{2,1,0:T(8,128)S(1)}, bf16[2,64,1,4096]{3,1,0,2:T(8,128)(2,1)}, /*...) while((s32[]{:T(128)}, f32[16,4096]{1,0:T(8,128)}, ...), condition=%wide.region_64.70_spmd.clone, body=%wide.region_27.69_spmd.clone.sunk | while | flops 12366611 | bytes 83280304 | solution.py:70
  806.5 107.9 %while.224 = (s32[]{:T(128)}, f32[1,16,4096]{2,1,0:T(8,128)S(1)}, f32[8,8,1,1,4096]{4,3,2,1,0:T(1,128)}, f32[8,8,1,16,4096]{4,3,1,2,0:T(8,128)}, f32[8,8,1,16,40...) while((s32[]{:T(128)}, f32[1,16,4096]{2,1,0:T(8,128)S(1)}, ...), condition=%wide.region_29.34_spmd, body=%wide.region_28.33_spmd.sunk | while | flops 3735558 | bytes 27557512 | solution.py:63
  916.4 157.0 %while.225 = (s32[]{:T(128)}, f32[16,4096]{1,0:T(8,128)S(1)}, f32[4096]{0:T(1024)S(1)}, f32[1,16,4096]{2,1,0:T(8,128)S(1)}, bf16[8,8,1,4096]{3,2,1,0:T(2,128)(2,...) while((s32[]{:T(128)}, f32[16,4096]{1,0:T(8,128)S(1)}, ...), condition=%wide.region_63.68_spmd.clone, body=%wide.region_30.67_spmd.clone.sunk | while | flops 8228617 | bytes 19550056 | solution.py:63
  1090.5 107.9 %while.224 = (s32[]{:T(128)}, f32[1,16,4096]{2,1,0:T(8,128)S(1)}, f32[8,8,1,1,4096]{4,3,2,1,0:T(1,128)}, f32[8,8,1,16,4096]{4,3,1,2,0:T(8,128)}, f32[8,8,1,16,40...) while((s32[]{:T(128)}, f32[1,16,4096]{2,1,0:T(8,128)S(1)}, ...), condition=%wide.region_29.34_spmd, body=%wide.region_28.33_spmd.sunk | while | flops 3735558 | bytes 27557512 | solution.py:63
  1200.5 157.0 %while.225 = (s32[]{:T(128)}, f32[16,4096]{1,0:T(8,128)S(1)}, f32[4096]{0:T(1024)S(1)}, f32[1,16,4096]{2,1,0:T(8,128)S(1)}, bf16[8,8,1,4096]{3,2,1,0:T(2,128)(2,...) while((s32[]{:T(128)}, f32[16,4096]{1,0:T(8,128)S(1)}, ...), condition=%wide.region_63.68_spmd.clone, body=%wide.region_30.67_spmd.clone.sunk | while | flops 8228617 | bytes 19550056 | solution.py:63
  1374.9 23.8 reduce.186
  1401.0 6.0 all-to-all-start.5
  1407.0 42.3 %fusion.149 = f32[128,1,16]{2,1,0:T(1,128)S(1)} fusion(f32[16,4096]{1,0:T(8,128)S(1)} %bitcast.1631, f32[128,4096]{1,0:T(8,128)S(1)} %copy-done.33, f32[16,4096]{1,0:T(8,128)S(1)} %get-tuple-element.3690, f32[128,4096,1]{1,0,2:T(8,128)} %bitcast.1688), kind=kOutput, calls=%fused_computation.534 | convolution fusion | flops 117440512 | bytes 4726784 | tf_op jit(solution)/shard_map/transpose(jvp())/while/body/eval_jaxpr/checkpoint/ln,lne->le/dot_general | solution.py:90
  1464.0 5.5 gather_fusion.11
  1474.8 23.4 reduce.185
  1500.5 6.0 all-to-all-start.6
  1521.9 5.3 gather_fusion.15
  1535.4 8.9 fusion.234
  1550.7 13.2 gather_fusion.12
  1563.8 45.4 %all-reduce.19.cloned.1.call-done = bf16[1024,160]{1,0:T(8,128)(2,1)} async-done(((bf16[1024,160]{1,0:T(8,128)(2,1)}), bf16[1024,160]{1,0:T(8,128)(2,1)}) %all-reduce.19.cloned.1.call-update) | async-done | bytes 327696 | tf_op jit(solution)/shard_map/psum | solution.py:282
  1621.6 6.8 multiply_reduce_fusion.36
  1631.2 5.6 gather_fusion.6
  1636.9 15.9 fusion.163
  1652.8 13.0 gather_fusion.17
  1665.8 11.3 select_bitcast_fusion
  1683.2 9.7 fusion.237
  1692.9 15.1 fusion.162
  1708.0 37.3 %copy.287 = f32[3,2048,2,512]{3,2,1,0:T(2,128)} copy(f32[3,2048,2,512]{1,3,2,0:T(8,128)} %bitcast.1622) | data formatting | bytes 50331648 | tf_op jit(solution)/shard_map/reshape | solution.py:297
  1756.3 6.7 psum.92
  1763.3 62.4 %reduce-scatter.5.cloned.1.call-done = f32[1,128,2048]{2,1,0:T(8,128)} async-done(((f32[1,1024,2048]{2,1,0:T(8,128)}), f32[1,128,2048]{2,1,0:T(8,128)}) %reduce-scatter.5.cloned.1.call-update) | async-done | bytes 1048592 | tf_op jit(solution)/shard_map/reduce_scatter | solution.py:301
  1827.3 43.2 %all-reduce.9 = (f32[2048]{0:T(1024)}, f32[4096]{0:T(1024)}, f32[4096]{0:T(1024)}) all-reduce(f32[2048]{0:T(1024)S(1)} %get-tuple-element.1726, f32[4096]{0:T(1024)S(1)} %dynamic_update_slice.136, f32[4096]{0:T(1024)S(1)} %copy-done.42), channel_id=1, replica_groups=mesh['batch'=4,'own'=8] {'batch','own'}, use_global_device_ids=true, to_apply=%region_72.78 | all-reduce | flops 10240 | bytes 81920 | tf_op jit(solution)/shard_map/psum | solution.py:310
  1870.6 108.2 %reduce-scatter.3.cloned.1.call-done = f32[1,128,2048]{2,1,0:T(8,128)} async-done(((f32[1,1024,2048]{2,1,0:T(8,128)}), f32[1,128,2048]{2,1,0:T(8,128)}) %reduce-scatter.3.cloned.1.call-update) | async-done | bytes 1048592 | tf_op jit(solution)/shard_map/reduce_scatter | solution.py:229
  1981.5 128.6 %all-reduce.21.cloned.1.call-done = (f32[4,4096]{1,0:T(4,128)}, f32[16,4096]{1,0:T(8,128)}) async-done(((f32[4,4096]{1,0:T(4,128)}, f32[16,4096]{1,0:T(8,128)}), (f32[4,4096]{1,0:T(4,128)}, f32[16,4096]{1,0:T(8,128)})) %all-reduce.21.cloned.1.call-update) | async-done | bytes 327696 | tf_op jit(solution)/shard_map/psum | solution.py:310
  2110.2 662.0 %all-reduce.23.cloned.1.call-done = (f32[3,2048,2,512]{3,2,1,0:T(2,128)}, f32[3,512,160]{1,2,0:T(8,128)}, f32[3,128,512]{2,1,0:T(8,128)}, f32[3,512,2048]{2,1,0:T(8,128)}) async-done(((f32[3,2048,2,512]{3,2,1,0:T(2,128)}, f32[3,512,160]{1,2,0:T(8,128)}, f32[3,128,512]{2,1,0:T(8,128)}, f32[3,512,2048]{2,1,0:T(8,128)}), (f32[3,2048,2,512]{3,2,1,0:T(2,128)}, f32[3,512,160]{1,2,0:T(8,128)}, ...) | async-done | bytes 39518224 | tf_op jit(solution)/shard_map/psum | solution.py:313
  2772.2 17.3 copy.619
  2792.7 11.5 copy.624
  (2363 shorter events, 952.7 us)
Async XLA Ops:
  7.2 208.6 %copy-start = (bf16[3,512,160]{1,2,0:T(8,128)(2,1)S(1)}, bf16[3,512,160]{1,2,0:T(8,128)(2,1)}, u32[]{:S(2)}) copy-start(bf16[3,512,160]{1,2,0:T(8,128)(2,1)} %param.42) | copy-start | bytes 1474564
  7.2 79.7 %all-gather.9.cloned.1.call-start = ((), (), s32[]{:S(2)}) async-start(), calls=%async_computation.10 | async-start | bytes 4718592 | tf_op jit(solution)/shard_map/all_gather | solution.py:160
  8.5 24.1 copy-start.85
  8.5 24.1 copy-start.83
  10.6 150.1 %all-gather.11.cloned.1.call-start = ((), (), s32[]{:S(2)}) async-start(), calls=%async_computation.13 | async-start | bytes 4718592 | tf_op jit(solution)/shard_map/all_gather | solution.py:231
  54.5 181.1 %copy-start.60 = (pred[1344]{0:T(1024)(128)(4,1)}, pred[1344]{0:T(1024)(128)(4,1)S(1)}, u32[]{:S(2)}) copy-start(pred[1344]{0:T(1024)(128)(4,1)S(1)} %get-tuple-element.1968) | copy-start | bytes 4036
  54.5 274.4 %copy-start.37 = (s32[2048]{0:T(1024)}, s32[2048]{0:T(1024)S(1)}, u32[]{:S(2)}) copy-start(s32[2048]{0:T(1024)S(1)} %pad_clamp_fusion) | copy-start | bytes 24580
  55.4 148.2 %copy-start.62 = (f32[1,512]{1,0:T(1,128)}, f32[1,512]{1,0:T(1,128)S(1)}, u32[]{:S(2)}) copy-start(f32[1,512]{1,0:T(1,128)S(1)} %get-tuple-element.2130) | copy-start | bytes 6148
  55.4 148.2 %copy-start.64 = (f32[1,512]{1,0:T(1,128)}, f32[1,512]{1,0:T(1,128)S(1)}, u32[]{:S(2)}) copy-start(f32[1,512]{1,0:T(1,128)S(1)} %get-tuple-element.2131) | copy-start | bytes 6148
  55.4 148.2 %copy-start.66 = (f32[1,512]{1,0:T(1,128)}, f32[1,512]{1,0:T(1,128)S(1)}, u32[]{:S(2)}) copy-start(f32[1,512]{1,0:T(1,128)S(1)} %get-tuple-element.2132) | copy-start | bytes 6148
  55.5 148.2 %copy-start.68 = (f32[1,512]{1,0:T(1,128)}, f32[1,512]{1,0:T(1,128)S(1)}, u32[]{:S(2)}) copy-start(f32[1,512]{1,0:T(1,128)S(1)} %get-tuple-element.2133) | copy-start | bytes 6148
  57.4 282.6 %copy-start.76 = (pred[1024]{0:T(1024)(128)(4,1)}, pred[1024]{0:T(1024)(128)(4,1)S(1)}, u32[]{:S(2)}) copy-start(pred[1024]{0:T(1024)(128)(4,1)S(1)} %get-tuple-element.2137) | copy-start | bytes 3076
  57.5 282.6 %copy-start.78 = (pred[1024]{0:T(1024)(128)(4,1)}, pred[1024]{0:T(1024)(128)(4,1)S(1)}, u32[]{:S(2)}) copy-start(pred[1024]{0:T(1024)(128)(4,1)S(1)} %get-tuple-element.2138) | copy-start | bytes 3076
  57.5 282.6 %copy-start.80 = (pred[1024]{0:T(1024)(128)(4,1)}, pred[1024]{0:T(1024)(128)(4,1)S(1)}, u32[]{:S(2)}) copy-start(pred[1024]{0:T(1024)(128)(4,1)S(1)} %get-tuple-element.2139) | copy-start | bytes 3076
  57.5 314.4 %copy-start.53 = (pred[1024]{0:T(1024)(128)(4,1)}, pred[1024]{0:T(1024)(128)(4,1)S(1)}, u32[]{:S(2)}) copy-start(pred[1024]{0:T(1024)(128)(4,1)S(1)} %get-tuple-element.2140) | copy-start | bytes 3076
  57.5 310.4 %copy-start.46 = (s32[1024]{0:T(1024)}, s32[1024]{0:T(1024)S(1)}, u32[]{:S(2)}) copy-start(s32[1024]{0:T(1024)S(1)} %broadcast_clamp_fusion) | copy-start | bytes 12292
  183.6 11.0 copy-start.24
  230.0 126.0 %all-to-all-start = ((bf16[8,2,32768]{2,1,0:T(2,128)(2,1)}), bf16[8,2,32768]{2,1,0:T(2,128)(2,1)}, u32[]{:S(2)}, u32[]{:S(2)}) async-start(bf16[8,2,32768]{2,1,0:T(2,128)(2,1)} %reshape.6025), calls=%async_computation | async-start | bytes 2097152 | tf_op jit(solution)/shard_map/all_to_all | solution.py:198
  234.3 93.6 %all-reduce.17.cloned.1.call-start = ((), (), s32[]{:S(2)}) async-start(), calls=%async_computation.11 | async-start | bytes 2097152 | tf_op jit(solution)/shard_map/psum | solution.py:184
  235.6 99.5 %copy-start.56 = (pred[3,448]{1,0:T(4,128)(4,1)}, pred[3,448]{1,0:T(4,128)(4,1)S(1)}, u32[]{:S(2)}) copy-start(pred[3,448]{1,0:T(4,128)(4,1)S(1)} %broadcast_in_dim.627) | copy-start | bytes 4036
  235.6 104.4 %copy-start.70 = (f32[1,512]{1,0:T(1,128)}, f32[1,512]{1,0:T(1,128)S(1)}, u32[]{:S(2)}) copy-start(f32[1,512]{1,0:T(1,128)S(1)} %get-tuple-element.2134) | copy-start | bytes 6148
  235.6 104.4 %copy-start.72 = (f32[1,512]{1,0:T(1,128)}, f32[1,512]{1,0:T(1,128)S(1)}, u32[]{:S(2)}) copy-start(f32[1,512]{1,0:T(1,128)S(1)} %get-tuple-element.2135) | copy-start | bytes 6148
  235.7 104.4 %copy-start.74 = (f32[1,512]{1,0:T(1,128)}, f32[1,512]{1,0:T(1,128)S(1)}, u32[]{:S(2)}) copy-start(f32[1,512]{1,0:T(1,128)S(1)} %get-tuple-element.2136) | copy-start | bytes 6148
  356.0 42.4 %all-to-all-start.1 = ((bf16[8,2,32768]{2,1,0:T(2,128)(2,1)}), bf16[8,2,32768]{2,1,0:T(2,128)(2,1)}, u32[]{:S(2)}, u32[]{:S(2)}) async-start(bf16[8,2,32768]{2,1,0:T(2,128)(2,1)} %reshape.6023), calls=%async_computation.1 | async-start | bytes 2097152 | tf_op jit(solution)/shard_map/all_to_all | solution.py:200
  398.4 114.9 %all-to-all-start.4 = ((bf16[8,2,32768]{2,1,0:T(2,128)(2,1)}), bf16[8,2,32768]{2,1,0:T(2,128)(2,1)}, u32[]{:S(2)}, u32[]{:S(2)}) async-start(bf16[8,2,32768]{2,1,0:T(2,128)(2,1)} %reshape.6031), calls=%async_computation.5 | async-start | bytes 2097152 | tf_op jit(solution)/shard_map/all_to_all | solution.py:239
  404.4 180.4 %all-gather.13.cloned.1.call-start = ((), (), s32[]{:S(2)}) async-start(), calls=%async_computation.16 | async-start | bytes 2359296 | tf_op jit(solution)/shard_map/all_gather | solution.py:16
  419.7 165.2 %all-gather.15.cloned.1.call-start = ((), (), s32[]{:S(2)}) async-start(), calls=%async_computation.17 | async-start | bytes 2359296 | tf_op jit(solution)/shard_map/all_gather | solution.py:16
  513.3 47.2 %all-to-all-start.2 = ((bf16[8,2,32768]{2,1,0:T(2,128)(2,1)}), bf16[8,2,32768]{2,1,0:T(2,128)(2,1)}, u32[]{:S(2)}, u32[]{:S(2)}) async-start(bf16[8,2,32768]{2,1,0:T(2,128)(2,1)} %reshape.6027), calls=%async_computation.2 | async-start | bytes 2097152 | tf_op jit(solution)/shard_map/all_to_all | solution.py:199
  519.3 255.6 %all-gather.17.cloned.1.call-start = ((), (), s32[]{:S(2)}) async-start(), calls=%async_computation.18 | async-start | bytes 2359296 | tf_op jit(solution)/shard_map/all_gather | solution.py:16
  593.7 32.9 %copy-start.13 = (f32[1,16,4096]{2,1,0:T(8,128)}, f32[1,16,4096]{2,1,0:T(8,128)S(1)}, u32[]{:S(2)}) copy-start(f32[1,16,4096]{2,1,0:T(8,128)S(1)} %get-tuple-element.1257) | copy-start | bytes 786436
  593.7 23.9 copy-start.20
  593.7 23.9 copy-start.21
  593.8 23.9 copy-start.22
  699.4 87.6 %all-to-all-start.7 = ((bf16[8,2,32768]{2,1,0:T(2,128)(2,1)}), bf16[8,2,32768]{2,1,0:T(2,128)(2,1)}, u32[]{:S(2)}, u32[]{:S(2)}) async-start(bf16[8,2,32768]{2,1,0:T(2,128)(2,1)} %reshape.6033), calls=%async_computation.8 | async-start | bytes 2097152 | tf_op jit(solution)/shard_map/all_to_all | solution.py:257
  786.9 9.2 copy-start.10
  787.0 614.0 %all-to-all-start.3 = ((bf16[8,2,32768]{2,1,0:T(2,128)(2,1)}), bf16[8,2,32768]{2,1,0:T(2,128)(2,1)}, u32[]{:S(2)}, u32[]{:S(2)}) async-start(bf16[8,2,32768]{2,1,0:T(2,128)(2,1)} %reshape.6029), calls=%async_computation.3 | async-start | bytes 2097152 | tf_op jit(solution)/shard_map/all_to_all | solution.py:222
  916.4 157.0 %copy-start.40 = (f32[4096]{0:T(1024)S(1)}, f32[4096]{0:T(1024)}, u32[]{:S(2)}) copy-start(f32[4096]{0:T(1024)} %get-tuple-element.3581) | copy-start | bytes 49156 | tf_op jit(solution)/shard_map/transpose(jvp())/while
  1200.5 157.0 %copy-start.40 = (f32[4096]{0:T(1024)S(1)}, f32[4096]{0:T(1024)}, u32[]{:S(2)}) copy-start(f32[4096]{0:T(1024)} %get-tuple-element.3581) | copy-start | bytes 49156 | tf_op jit(solution)/shard_map/transpose(jvp())/while
  1398.7 8.3 copy-start.14
  1398.7 8.3 copy-start.33
  1401.0 99.5 %all-to-all-start.5 = ((bf16[8,2,32768]{2,1,0:T(2,128)(2,1)}), bf16[8,2,32768]{2,1,0:T(2,128)(2,1)}, u32[]{:S(2)}, u32[]{:S(2)}) async-start(bf16[8,2,32768]{2,1,0:T(2,128)(2,1)} %reshape.6037), calls=%async_computation.6 | async-start | bytes 2097152 | tf_op jit(solution)/shard_map/all_to_all | solution.py:260
  1500.5 43.8 %all-to-all-start.6 = ((bf16[8,2,32768]{2,1,0:T(2,128)(2,1)}), bf16[8,2,32768]{2,1,0:T(2,128)(2,1)}, u32[]{:S(2)}, u32[]{:S(2)}) async-start(bf16[8,2,32768]{2,1,0:T(2,128)(2,1)} %reshape.6035), calls=%async_computation.7 | async-start | bytes 2097152 | tf_op jit(solution)/shard_map/all_to_all | solution.py:254
  1506.5 102.7 %all-reduce.19.cloned.1.call-start = ((), (), s32[]{:S(2)}) async-start(), calls=%async_computation.14 | async-start | bytes 1048576 | tf_op jit(solution)/shard_map/psum | solution.py:282
  1535.3 290.3 %reduce-scatter.5.cloned.1.call-start = ((), (), s32[]{:S(2)}) async-start(), calls=%async_computation.15 | async-start | bytes 9437184 | tf_op jit(solution)/shard_map/reduce_scatter | solution.py:301
  1563.8 51.3 %copy-start.57 = (pred[3,448]{1,0:T(4,128)(4,1)S(1)}, pred[3,448]{1,0:T(4,128)(4,1)}, u32[]{:S(2)}) copy-start(pred[3,448]{1,0:T(4,128)(4,1)} %copy-done.56) | copy-start | bytes 4036
  1621.6 6.8 copy-start.63
  1621.6 6.8 copy-start.65
  1621.6 6.8 copy-start.67
  1621.6 6.8 copy-start.69
  1677.1 301.7 %reduce-scatter.3.cloned.1.call-start = ((), (), s32[]{:S(2)}) async-start(), calls=%async_computation.12 | async-start | bytes 9437184 | tf_op jit(solution)/shard_map/reduce_scatter | solution.py:229
  1677.9 432.3 %all-reduce.21.cloned.1.call-start = ((), (), s32[]{:S(2)}) async-start(), calls=%async_computation.19 | async-start | bytes 655360 | tf_op jit(solution)/shard_map/psum | solution.py:310
  1683.2 9.7 copy-start.30
  1708.0 38.3 %copy-start.17 = (bf16[1344,512]{1,0:T(8,128)(2,1)S(1)}, bf16[1344,512]{1,0:T(8,128)(2,1)}, u32[]{:S(2)}) copy-start(bf16[1344,512]{1,0:T(8,128)(2,1)} %copy-done.16) | copy-start | bytes 4128772
  1708.0 38.3 %copy-start.26 = (bf16[3,448,160]{1,2,0:T(8,128)(2,1)S(1)}, bf16[3,448,160]{1,2,0:T(8,128)(2,1)}, u32[]{:S(2)}) copy-start(bf16[3,448,160]{1,2,0:T(8,128)(2,1)} %copy.278) | copy-start | bytes 1290244
  1746.0 1026.2 %all-reduce.23.cloned.1.call-start = ((), (), s32[]{:S(2)}) async-start(), calls=%async_computation.20 | async-start | bytes 79036416 | tf_op jit(solution)/shard_map/psum | solution.py:313
  1754.1 71.5 %copy-start.23 = (bf16[1,128,2048]{2,1,0:T(8,128)(2,1)S(1)}, bf16[1,128,2048]{2,1,0:T(8,128)(2,1)}, u32[]{:S(2)}) copy-start(bf16[1,128,2048]{2,1,0:T(8,128)(2,1)} %param.37) | copy-start | bytes 1572868
  1754.1 71.5 %copy-start.55 = (f32[2048]{0:T(1024)S(1)}, f32[2048]{0:T(1024)}, u32[]{:S(2)}) copy-start(f32[2048]{0:T(1024)} %param.38) | copy-start | bytes 24580
  1754.1 71.5 %copy-start.84 = (f32[128]{0:T(128)S(1)}, f32[128]{0:T(128)}, u32[]{:S(2)}) copy-start(f32[128]{0:T(128)} %copy-done.83) | copy-start | bytes 1540
  1754.1 73.2 %copy-start.42 = (f32[4096]{0:T(1024)S(1)}, f32[4096]{0:T(1024)}, u32[]{:S(2)}) copy-start(f32[4096]{0:T(1024)} %get-tuple-element.1270) | copy-start | bytes 49156
  1754.1 116.4 %copy-start.86 = (f32[128]{0:T(128)S(1)}, f32[128]{0:T(128)}, u32[]{:S(2)}) copy-start(f32[128]{0:T(128)} %copy-done.85) | copy-start | bytes 1540
  1754.2 224.6 %copy-start.34 = (bf16[1,128,2048]{2,1,0:T(8,128)(2,1)S(1)}, bf16[1,128,2048]{2,1,0:T(8,128)(2,1)}, u32[]{:S(2)}) copy-start(bf16[1,128,2048]{2,1,0:T(8,128)(2,1)} %param.49) | copy-start | bytes 1572868
  1825.6 153.2 %copy-start.28 = (f32[1,128,2048]{2,1,0:T(8,128)S(1)}, f32[1,128,2048]{2,1,0:T(8,128)}, u32[]{:S(2)}) copy-start(f32[1,128,2048]{2,1,0:T(8,128)} %reduce-scatter.5.cloned.1.call-done) | copy-start | bytes 3145732
  2772.2 17.3 copy-start.59
  2772.2 18.0 copy-start.36
  (47 other events, 131.2 us)
Sparse Core Ops, SparseCore 0:
  10.7 76.0 all-gather.8
  89.0 71.6 all-gather.10
  238.6 89.1 all-reduce.16
  419.8 50.6 all-gather.12
  497.6 63.3 all-gather.14
  646.7 48.1 all-gather.16
  1535.4 73.7 all-reduce.18
  1677.3 148.3 reduce-scatter.4
  1829.7 149.0 reduce-scatter.2
  1985.2 124.9 all-reduce.20
  2114.4 657.7 all-reduce.22
where the time goes:
time: 2850 us; the launch traced here: 2810 us
  waiting for transfers between devices  1210 us (42%)
  other arithmetic  686 us (24%)
  local copies, waits for them, and re-layouts  652 us (23%)
  matrix products  143 us (5%)
  blocking collectives  50 us (2%)
  starting transfers between devices  43.5 us (2%)
    psum x1, waiting for transfers between devices, per_device(): lax.psum((grad_in_part, grad_state_part, grad_step_part, grad_bias_part,...  662 us
    while x440, other arithmetic  193 us
    unnamed x13, other arithmetic  130 us
    psum x1, waiting for transfers between devices, per_device(): lax.psum((grad_gain_part, grad_conv_w_full, grad_conv_b_full, grad_logd,...  129 us
    dynamic_update_slice x160, local copies, waits for them, and re-layouts, run_block(): return lax.scan(advance, carried, inputs, unroll=8)  126 us
    reduce_scatter x1, waiting for transfers between devices, per_device(): branch = lax.psum_scatter(out_term, 'own', scatter_dimension=1, tiled=True)  108 us
    unnamed x193, local copies, waits for them, and re-layouts  105 us
    psum x1, waiting for transfers between devices, per_device(): proj_full = lax.psum(proj_part, 'own')  92.2 us
  transfers between devices with their start and end apart: 19, of which 9 were waited for; matrix products, arithmetic and copies ran while one was open for 44% of the time, Pallas kernels for 0%

commit v1 on v0

v1 whole, which is shorter than its diff:
```python
import functools

import jax
import jax.numpy as jnp
from jax import lax
from jax.experimental import pallas as pl
from jax.experimental.pallas import tpu as pltpu
from jax.sharding import PartitionSpec as P

M = 3
epsilon = 1e-05
LANES = 128
log2e = 1.4426950408889634
bf16 = jnp.bfloat16
f32 = jnp.float32


def contract(a, b, ca, cb):
    return lax.dot_general(a, b, (((ca,), (cb,)), ((), ())), preferred_element_type=f32)


def pick(mod, parts):
    out = parts[-1]
    for m in reversed(range(len(parts) - 1)):
        out = jnp.where(mod == m, parts[m], out)
    return out


def sigmoid(v):
    return 1.0 / (1.0 + jnp.exp(-v))


def fold_rows(vs):
    sub = lax.broadcasted_iota(jnp.int32, vs[0].shape, 0)
    for shift in (1, 2, 4):
        mask = (sub & shift) == 0
        vs = [
            jnp.where(mask, a, b) + pltpu.roll(jnp.where(mask, b, a), shift, 0)
            for a, b in zip(vs[0::2], vs[1::2])
        ]
    return vs[0]


def lane_total(v):
    width = v.shape[1] // LANES
    total = v[:, :LANES]
    for k in range(1, width):
        total = total + v[:, k * LANES : (k + 1) * LANES]
    return jnp.sum(total, axis=1, keepdims=True)


def cost(flops, nbytes):
    return pl.CostEstimate(flops=int(flops), bytes_accessed=int(nbytes), transcendentals=0)


def in_body(x_ref, wc_ref, wg_ref, cw_ref, cb_ref, sp_ref, modc_ref, modr_ref,
            ci_ref, gate_ref, act_ref, proj_ref, pad, *, rows, block):
    tile = pl.program_id(0)
    pad[0:8, :] = jnp.zeros((8, pad.shape[1]), f32)

    def matmul(r, _):
        at = pl.multiple_of(r * block, block)
        x = x_ref[pl.ds(at, block), :]
        mc = modc_ref[pl.ds(at, block), :]
        conv = pick(mc, [contract(x, wc_ref[m], 1, 0) for m in range(M)]).astype(bf16)
        ci_ref[pl.ds(at, block), :] = conv
        pad[pl.ds(at + 8, block), :] = conv.astype(f32)
        gate_ref[pl.ds(at, block), :] = pick(
            mc, [contract(x, wg_ref[m], 1, 0) for m in range(M)]
        ).astype(bf16)
        return 0

    lax.fori_loop(0, rows // block, matmul, 0)
    taps = cw_ref[...]
    base = cb_ref[...]

    def convolve(r, _):
        at = pl.multiple_of(r * LANES, LANES)
        v = pad[pl.ds(at, LANES + 8), :]
        s = base
        for k in range(4):
            s = s + taps[k : k + 1, :] * v[5 + k : 5 + k + LANES, :]
        act = (s * sigmoid(s)).astype(bf16)
        act_ref[pl.ds(at, LANES), :] = act
        part = pick(modr_ref[r], [contract(sp_ref[m], act, 1, 1) for m in range(M)])

        @pl.when(tile == 0)
        def _():
            proj_ref[r] = part

        @pl.when(tile != 0)
        def _():
            proj_ref[r] += part

        return 0

    lax.fori_loop(0, rows // LANES, convolve, 0)


def input_stage(x, w, cw, cb, sp, modc, modr):
    rows, width = x.shape
    chans = cw.shape[1]
    psize = sp.shape[1]
    tc = min(256, chans)
    tiles = chans // tc
    full = lambda shape: pl.BlockSpec(shape, lambda j: (0,) * len(shape))
    col = lambda r: pl.BlockSpec((r, tc), lambda j: (0, j))
    return pl.pallas_call(
        functools.partial(in_body, rows=rows, block=256),
        grid=(tiles,),
        in_specs=[
            full((rows, width)),
            pl.BlockSpec((M, width, tc), lambda j: (0, 0, j)),
            pl.BlockSpec((M, width, tc), lambda j: (0, 0, j + tiles)),
            col(4),
            col(1),
            pl.BlockSpec((M, psize, tc), lambda j: (0, 0, j)),
            full((rows, 1)),
            full(modr.shape),
        ],
        out_specs=[col(rows), col(rows), col(rows), full((rows // LANES, psize, LANES))],
        out_shape=[
            jax.ShapeDtypeStruct((rows, chans), bf16),
            jax.ShapeDtypeStruct((rows, chans), bf16),
            jax.ShapeDtypeStruct((rows, chans), bf16),
            jax.ShapeDtypeStruct((rows // LANES, psize, LANES), f32),
        ],
        scratch_shapes=[pltpu.VMEM((rows + 8, tc), f32)],
        cost_estimate=cost(2 * M * rows * width * 2 * chans, 2 * (rows * width + M * width * 2 * chans)),
        name="input_stage",
    )(x, w, w, cw, cb, sp, modc, modr)


def mm_body(x_ref, w_ref, modc_ref, o_ref, *, rows, block, rhs_dim):
    def step(r, _):
        at = pl.multiple_of(r * block, block)
        x = x_ref[pl.ds(at, block), :]
        mc = modc_ref[pl.ds(at, block), :]
        o_ref[pl.ds(at, block), :] = pick(
            mc, [contract(x, w_ref[m], 1, rhs_dim) for m in range(M)]
        ).astype(o_ref.dtype)
        return 0

    lax.fori_loop(0, rows // block, step, 0)


def select_matmul(x, w, modc, transposed, dtype, name):
    rows, depth = x.shape
    cols = w.shape[1] if transposed else w.shape[2]
    tn = min(256, cols)
    wspec = (
        pl.BlockSpec((M, tn, depth), lambda j: (0, j, 0))
        if transposed
        else pl.BlockSpec((M, depth, tn), lambda j: (0, 0, j))
    )
    return pl.pallas_call(
        functools.partial(mm_body, rows=rows, block=256, rhs_dim=1 if transposed else 0),
        grid=(cols // tn,),
        in_specs=[
            pl.BlockSpec((rows, depth), lambda j: (0, 0)),
            wspec,
            pl.BlockSpec((rows, 1), lambda j: (0, 0)),
        ],
        out_specs=pl.BlockSpec((rows, tn), lambda j: (0, j)),
        out_shape=jax.ShapeDtypeStruct((rows, cols), dtype),
        cost_estimate=cost(2 * M * rows * depth * cols, 2 * (rows * depth + M * depth * cols + rows * cols)),
        name=name,
    )(x, w, modc)


def dgrad_body(gc_ref, gg_ref, wc_ref, modc_ref, o_ref, *, rows, block, chans):
    def step(r, _):
        at = pl.multiple_of(r * block, block)
        gc = gc_ref[pl.ds(at, block), :]
        gg = gg_ref[pl.ds(at, block), :]
        mc = modc_ref[pl.ds(at, block), :]
        o_ref[pl.ds(at, block), :] = pick(
            mc,
            [
                contract(gc, wc_ref[m, :, :chans], 1, 1) + contract(gg, wc_ref[m, :, chans:], 1, 1)
                for m in range(M)
            ],
        ).astype(o_ref.dtype)
        return 0

    lax.fori_loop(0, rows // block, step, 0)


def input_dgrad(gc, gg, w, modc):
    rows, chans = gc.shape
    width = w.shape[1]
    tn = 256
    return pl.pallas_call(
        functools.partial(dgrad_body, rows=rows, block=256, chans=chans),
        grid=(width // tn,),
        in_specs=[
            pl.BlockSpec((rows, chans), lambda j: (0, 0)),
            pl.BlockSpec((rows, chans), lambda j: (0, 0)),
            pl.BlockSpec((M, tn, 2 * chans), lambda j: (0, j, 0)),
            pl.BlockSpec((rows, 1), lambda j: (0, 0)),
        ],
        out_specs=pl.BlockSpec((rows, tn), lambda j: (0, j)),
        out_shape=jax.ShapeDtypeStruct((rows, width), bf16),
        cost_estimate=cost(4 * M * rows * chans * width, 2 * (2 * rows * chans + 2 * M * chans * width + rows * width)),
        name="input_dgrad",
    )(gc, gg, w, modc)


def wgrad_body(pos_ref, xt_ref, g_ref, modl_ref, o_ref):
    g = g_ref[...]
    xt = xt_ref[...]
    for m in range(M):
        o_ref[m] = contract(jnp.where(modl_ref[...] == m, xt, jnp.zeros_like(xt)), g, 1, 0).astype(o_ref.dtype)


def half_wgrad(half, xt, g, modl, dtype, name):
    width, rows = xt.shape
    cols = g.shape[1]
    td = min(256, width // 2)
    steps = width // 2 // td
    return pl.pallas_call(
        wgrad_body,
        grid_spec=pltpu.PrefetchScalarGridSpec(
            num_scalar_prefetch=1,
            grid=(steps,),
            in_specs=[
                pl.BlockSpec((td, rows), lambda i, pos: (i + pos[0] * steps, 0)),
                pl.BlockSpec((rows, cols), lambda i, pos: (0, 0)),
                pl.BlockSpec((1, rows), lambda i, pos: (0, 0)),
            ],
            out_specs=pl.BlockSpec((M, td, cols), lambda i, pos: (0, i, 0)),
        ),
        out_shape=jax.ShapeDtypeStruct((M, width // 2, cols), dtype),
        cost_estimate=cost(M * rows * width * cols, rows * width + 2 * rows * cols + 2 * M * width * cols),
        name=name,
    )(half, xt, g, modl)


def row_of(ref, t):
    return jnp.broadcast_to(ref[pl.ds(t, 1), :], (8, ref.shape[1]))


def scan_fwd_body(pj_ref, act_ref, gate_ref, gg_ref, sp_ref, sb_ref, ld_ref, skip_ref, modc_ref,
                  delta_ref, sig_ref, gated_ref, ggate_ref, prev_ref, gct_ref,
                  state, d_s, u_s, y_s, gs_s, r_s):
    span, chans = act_ref.shape
    rank = sp_ref.shape[1]

    @pl.when(pl.program_id(0) == 0)
    def _():
        state[...] = jnp.zeros_like(state)

    mc = modc_ref[...]
    step_in = pj_ref[0, :rank, :]
    pre = pick(mc, [contract(step_in, sp_ref[m], 0, 0) + sb_ref[m : m + 1, :] for m in range(M)])
    z = jnp.exp(-jnp.abs(pre))
    delta = (jnp.maximum(pre, 0.0) + jnp.log1p(z)).astype(bf16)
    delta_ref[...] = delta
    inv = 1.0 / (1.0 + z)
    sig_ref[...] = jnp.where(pre >= 0, inv, z * inv)
    act = act_ref[...].astype(f32)
    d = delta.astype(f32)
    d_s[...] = d
    u_s[...] = d * act
    gate = gate_ref[...].astype(f32)
    s = sigmoid(gate)
    ggf = gg_ref[...].astype(f32)
    gs_s[...] = ggf * (gate * s)
    r_s[...] = -jnp.exp(ld_ref[...]) * log2e
    b = pj_ref[0, rank : rank + 16, :].astype(f32) + pj_ref[0, rank + 32 : rank + 48, :].astype(f32)
    c = pj_ref[0, rank + 16 : rank + 32, :].astype(f32) + pj_ref[0, rank + 48 : rank + 64, :].astype(f32)
    lane = lax.broadcasted_iota(jnp.int32, (8, LANES), 1)

    def eight(i, carry):
        st0, st1, gc0, gc1 = carry
        back = lax.rem(span - i * 8, span)
        bb = pltpu.roll(b, back, 1)
        cc = pltpu.roll(c, back, 1)
        ys = []
        for j in range(8):
            t = i * 8 + j
            db, ub, gsb = row_of(d_s, t), row_of(u_s, t), row_of(gs_s, t)
            at = pl.multiple_of(t * 16, 16)
            prev_ref[pl.ds(at, 8), :] = st0
            prev_ref[pl.ds(at + 8, 8), :] = st1
            st0 = jnp.exp2(db * r_s[0:8, :]) * st0 + ub * bb[0:8, j : j + 1]
            st1 = jnp.exp2(db * r_s[8:16, :]) * st1 + ub * bb[8:16, j : j + 1]
            ys.append(st0 * cc[0:8, j : j + 1] + st1 * cc[8:16, j : j + 1])
            gc0 = jnp.where(lane == t, lane_total(st0 * gsb), gc0)
            gc1 = jnp.where(lane == t, lane_total(st1 * gsb), gc1)
        y_s[pl.ds(pl.multiple_of(i * 8, 8), 8), :] = fold_rows(ys)
        return st0, st1, gc0, gc1

    none = jnp.zeros((8, LANES), f32)
    st0, st1, gc0, gc1 = lax.fori_loop(0, span // 8, eight, (state[0:8, :], state[8:16, :], none, none))
    state[0:8, :] = st0
    state[8:16, :] = st1
    gct_ref[0, 0:8, :] = gc0
    gct_ref[0, 8:16, :] = gc1
    scanned = y_s[...] + skip_ref[...] * act
    gated_ref[...] = (scanned * (gate * s)).astype(bf16)
    ggate_ref[...] = (ggf * scanned * (s * (1.0 + gate * (1.0 - s)))).astype(bf16)


def scan_forward(pj, act, gate, gg, step_proj, step_bias, log_decay, skip, modc):
    rows, chans = act.shape
    blocks = rows // LANES
    rank = step_proj.shape[1]
    row = pl.BlockSpec((LANES, chans), lambda i: (i, 0))
    full = lambda shape: pl.BlockSpec(shape, lambda i: (0,) * len(shape))
    return pl.pallas_call(
        scan_fwd_body,
        grid=(blocks,),
        in_specs=[
            pl.BlockSpec((1,) + pj.shape[1:], lambda i: (i, 0, 0)),
            row, row, row,
            full((M, rank, chans)),
            full((M, chans)),
            full((16, chans)),
            full((1, chans)),
            pl.BlockSpec((LANES, 1), lambda i: (i, 0)),
        ],
        out_specs=[
            row, row, row, row,
            pl.BlockSpec((LANES * 16, chans), lambda i: (i, 0)),
            pl.BlockSpec((1, 16, LANES), lambda i: (i, 0, 0)),
        ],
        out_shape=[
            jax.ShapeDtypeStruct((rows, chans), bf16),
            jax.ShapeDtypeStruct((rows, chans), f32),
            jax.ShapeDtypeStruct((rows, chans), bf16),
            jax.ShapeDtypeStruct((rows, chans), bf16),
            jax.ShapeDtypeStruct((rows * 16, chans), f32),
            jax.ShapeDtypeStruct((blocks, 16, LANES), f32),
        ],
        scratch_shapes=[pltpu.VMEM((16, chans), f32)] + [pltpu.VMEM((LANES, chans), f32)] * 4 + [pltpu.VMEM((16, chans), f32)],
        cost_estimate=cost(40e9, 64 * rows * chans + 20 * rows * chans),
        name="scan_forward",
    )(pj, act, gate, gg, step_proj, step_bias, log_decay, skip, modc)


def scan_bwd_body(pj_ref, act_ref, gate_ref, gg_ref, delta_ref, sig_ref, prev_ref, gct_ref,
                  sp_ref, ld_ref, skip_ref, modc_ref, modr_ref,
                  gas_ref, gpt_ref, glogd_ref, gskip_ref, gbias_ref, gstep_ref,
                  carry_w, acc, d_s, u_s, gs_s, g_s, h_s, r_s, n_s):
    span, chans = act_ref.shape
    rank = sp_ref.shape[1]
    first = pl.program_id(0) == 0

    @pl.when(first)
    def _():
        carry_w[...] = jnp.zeros_like(carry_w)
        acc[...] = jnp.zeros_like(acc)
        gskip_ref[...] = jnp.zeros_like(gskip_ref)
        gbias_ref[...] = jnp.zeros_like(gbias_ref)
        gstep_ref[...] = jnp.zeros_like(gstep_ref)

    act = act_ref[...].astype(f32)
    d = delta_ref[...].astype(f32)
    gate = gate_ref[...].astype(f32)
    gs = gg_ref[...].astype(f32) * (gate * sigmoid(gate))
    d_s[...] = d
    u_s[...] = d * act
    gs_s[...] = gs
    rates = -jnp.exp(ld_ref[...])
    n_s[...] = rates
    r_s[...] = rates * log2e
    b = pj_ref[0, rank : rank + 16, :].astype(f32) + pj_ref[0, rank + 32 : rank + 48, :].astype(f32)
    c = pj_ref[0, rank + 16 : rank + 32, :].astype(f32) + pj_ref[0, rank + 48 : rank + 64, :].astype(f32)
    lane = lax.broadcasted_iota(jnp.int32, (8, LANES), 1)

    def eight(k, carry):
        w0, w1, gb0, gb1 = carry
        i = span // 8 - 1 - k
        back = lax.rem(span - i * 8, span)
        bb = pltpu.roll(b, back, 1)
        cc = pltpu.roll(c, back, 1)
        gl = [None] * 8
        hl = [None] * 8
        for j in reversed(range(8)):
            t = i * 8 + j
            db, ub, gsb = row_of(d_s, t), row_of(u_s, t), row_of(gs_s, t)
            at = pl.multiple_of(t * 16, 16)
            a0 = gsb * cc[0:8, j : j + 1] + w0
            a1 = gsb * cc[8:16, j : j + 1] + w1
            gl[j] = a0 * bb[0:8, j : j + 1] + a1 * bb[8:16, j : j + 1]
            w0 = jnp.exp2(db * r_s[0:8, :]) * a0
            w1 = jnp.exp2(db * r_s[8:16, :]) * a1
            q0 = w0 * prev_ref[pl.ds(at, 8), :]
            q1 = w1 * prev_ref[pl.ds(at + 8, 8), :]
            hl[j] = q0 * n_s[0:8, :] + q1 * n_s[8:16, :]
            acc[0:8, :] += q0 * db
            acc[8:16, :] += q1 * db
            gb0 = jnp.where(lane == t, lane_total(a0 * ub), gb0)
            gb1 = jnp.where(lane == t, lane_total(a1 * ub), gb1)
        at8 = pl.ds(pl.multiple_of(i * 8, 8), 8)
        g_s[at8, :] = fold_rows(gl)
        h_s[at8, :] = fold_rows(hl)
        return w0, w1, gb0, gb1

    none = jnp.zeros((8, LANES), f32)
    w0, w1, gb0, gb1 = lax.fori_loop(0, span // 8, eight, (carry_w[0:8, :], carry_w[8:16, :], none, none))
    carry_w[0:8, :] = w0
    carry_w[8:16, :] = w1
    g = g_s[...]
    gas_ref[...] = (g * d + skip_ref[...] * gs).astype(bf16)
    gpre = (act * g + h_s[...]).astype(bf16).astype(f32) * sig_ref[...]
    glin = gpre.astype(bf16)
    mc = modc_ref[...]
    mr = modr_ref[0]
    step_in = pj_ref[0, :rank, :]
    sums = []
    for m in range(M):
        sums.append(jnp.sum(jnp.where(mc == m, gpre, 0.0), axis=0, keepdims=True))
        gstep_ref[m] += contract(jnp.where(mr == m, step_in, jnp.zeros_like(step_in)), glin, 1, 0)
    gbias_ref[...] += jnp.concatenate(sums, axis=0)
    gskip_ref[...] += jnp.sum(gs * act, axis=0, keepdims=True)
    gpt_ref[0, :rank, :] = pick(mr, [contract(sp_ref[m], glin, 1, 1) for m in range(M)]).astype(bf16)
    gpt_ref[0, rank : rank + 16, :] = jnp.concatenate([gb0, gb1], axis=0).astype(bf16)
    gpt_ref[0, rank + 16 : rank + 32, :] = gct_ref[0].astype(bf16)
    glogd_ref[...] = acc[...] * n_s[...]


def scan_backward(pj, act, gate, gg, delta, sig, prev, gct, step_proj, log_decay, skip, modc, modr):
    rows, chans = act.shape
    blocks = rows // LANES
    rank = step_proj.shape[1]
    last = blocks - 1
    row = pl.BlockSpec((LANES, chans), lambda i: (last - i, 0))
    full = lambda shape: pl.BlockSpec(shape, lambda i: (0,) * len(shape))
    slab = lambda shape: pl.BlockSpec((1,) + shape, lambda i: (last - i, 0, 0))
    return pl.pallas_call(
        scan_bwd_body,
        grid=(blocks,),
        in_specs=[
            slab(pj.shape[1:]),
            row, row, row, row, row,
            pl.BlockSpec((LANES * 16, chans), lambda i: (last - i, 0)),
            slab((16, LANES)),
            full((M, rank, chans)),
            full((16, chans)),
            full((1, chans)),
            pl.BlockSpec((LANES, 1), lambda i: (last - i, 0)),
            slab((1, LANES)),
        ],
        out_specs=[
            row,
            slab((rank + 32, LANES)),
            full((16, chans)),
            full((1, chans)),
            full((M, chans)),
            full((M, rank, chans)),
        ],
        out_shape=[
            jax.ShapeDtypeStruct((rows, chans), bf16),
            jax.ShapeDtypeStruct((blocks, rank + 32, LANES), bf16),
            jax.ShapeDtypeStruct((16, chans), f32),
            jax.ShapeDtypeStruct((1, chans), f32),
            jax.ShapeDtypeStruct((M, chans), f32),
            jax.ShapeDtypeStruct((M, rank, chans), f32),
        ],
        scratch_shapes=[pltpu.VMEM((16, chans), f32)] * 2 + [pltpu.VMEM((LANES, chans), f32)] * 5 + [pltpu.VMEM((16, chans), f32)] * 2,
        cost_estimate=cost(60e9, 64 * rows * chans + 20 * rows * chans),
        name="scan_backward",
    )(pj, act, gate, gg, delta, sig, prev, gct, step_proj, log_decay, skip, modc, modr)


def conv_bwd_body(gp_ref, sp_ref, gas_ref, ci_ref, act_ref, cw_ref, cb_ref, modc_ref, modr_ref,
                  gci_ref, gstate_ref, gcw_ref, pad, tail, *, rows):
    cols = pad.shape[1]
    pad[0:8, :] = jnp.zeros((8, cols), f32)
    tail[rows : rows + 8, :] = jnp.zeros((8, cols), f32)
    gstate_ref[...] = jnp.zeros_like(gstate_ref)
    taps = cw_ref[...]
    base = cb_ref[...]

    def first(r, sums):
        at = pl.multiple_of(r * LANES, LANES)
        here = pl.ds(at, LANES)
        pad[pl.ds(at + 8, LANES), :] = ci_ref[here, :].astype(f32)
        v = pad[pl.ds(at, LANES + 8), :]
        shifted = [v[5 + k : 5 + k + LANES, :] for k in range(4)]
        s = base
        for k in range(4):
            s = s + taps[k : k + 1, :] * shifted[k]
        sg = sigmoid(s)
        gp = gp_ref[r]
        ga = pick(modc_ref[here, :], [contract(gp, sp_ref[m], 0, 0) for m in range(M)])
        gcp = (ga + gas_ref[here, :].astype(f32)) * (sg * (1.0 + s * (1.0 - sg)))
        tail[here, :] = gcp
        act = act_ref[here, :]
        mr = modr_ref[r]
        for m in range(M):
            gstate_ref[m] += contract(jnp.where(mr == m, gp, jnp.zeros_like(gp)), act, 1, 0)
        terms = [gcp * part for part in shifted] + [gcp]
        return tuple(
            total + jnp.sum(term.reshape(LANES // 8, 8, cols), axis=0) for total, term in zip(sums, terms)
        )

    sums = lax.fori_loop(0, rows // LANES, first, (jnp.zeros((8, cols), f32),) * 5)
    gcw_ref[...] = jnp.concatenate(
        [jnp.sum(total, axis=0, keepdims=True) for total in sums] + [jnp.zeros((3, cols), f32)], axis=0
    )

    def second(r, _):
        at = pl.multiple_of(r * LANES, LANES)
        v = tail[pl.ds(at, LANES + 8), :]
        s = taps[0:1, :] * v[3 : 3 + LANES, :]
        for k in range(1, 4):
            s = s + taps[k : k + 1, :] * v[3 - k : 3 - k + LANES, :]
        gci_ref[pl.ds(at, LANES), :] = s.astype(bf16)
        return 0

    lax.fori_loop(0, rows // LANES, second, 0)


def conv_backward(gp, sp, gas, ci, act, cw, cb, modc, modr):
    rows, chans = ci.shape
    psize = sp.shape[1]
    tc = min(256, chans)
    col = lambda r: pl.BlockSpec((r, tc), lambda j: (0, j))
    full = lambda shape: pl.BlockSpec(shape, lambda j: (0,) * len(shape))
    wide = pl.BlockSpec((M, psize, tc), lambda j: (0, 0, j))
    return pl.pallas_call(
        functools.partial(conv_bwd_body, rows=rows),
        grid=(chans // tc,),
        in_specs=[full(gp.shape), wide, col(rows), col(rows), col(rows), col(4), col(1), full((rows, 1)), full(modr.shape)],
        out_specs=[col(rows), wide, col(8)],
        out_shape=[
            jax.ShapeDtypeStruct((rows, chans), bf16),
            jax.ShapeDtypeStruct((M, psize, chans), f32),
            jax.ShapeDtypeStruct((8, chans), f32),
        ],
        scratch_shapes=[pltpu.VMEM((rows + 8, tc), f32), pltpu.VMEM((rows + 8, tc), f32)],
        cost_estimate=cost(8 * M * rows * psize * chans, 10 * rows * chans),
        name="conv_backward",
    )(gp, sp, gas, ci, act, cw, cb, modc, modr)


def assemble_body(pos_ref, mc_ref, rc_ref, mg_ref, rg_ref, o_ref, *, half_steps):
    mine = pl.program_id(1) // half_steps == pos_ref[0]

    @pl.when(mine)
    def _():
        o_ref[0, :, 0, :] = mc_ref[0].astype(f32)
        o_ref[0, :, 1, :] = mg_ref[0].astype(f32)

    @pl.when(jnp.logical_not(mine))
    def _():
        o_ref[0, :, 0, :] = rc_ref[0].astype(f32)
        o_ref[0, :, 1, :] = rg_ref[0].astype(f32)


def assemble_input_grad(core, mine_conv, recv_conv, mine_gate, recv_gate):
    _, half, chans = mine_conv.shape
    td = 256
    steps = half // td
    own_map = lambda m, i, pos: (m, jnp.where(i // steps == pos[0], lax.rem(i, steps), 0), 0)
    other_map = lambda m, i, pos: (m, jnp.where(i // steps != pos[0], lax.rem(i, steps), 0), 0)
    mine = pl.BlockSpec((1, td, chans), own_map)
    recv = pl.BlockSpec((1, td, chans), other_map)
    return pl.pallas_call(
        functools.partial(assemble_body, half_steps=steps),
        grid_spec=pltpu.PrefetchScalarGridSpec(
            num_scalar_prefetch=1,
            grid=(M, 2 * steps),
            in_specs=[mine, recv, mine, recv],
            out_specs=pl.BlockSpec((1, td, 2, chans), lambda m, i, pos: (m, i, 0, 0)),
        ),
        out_shape=jax.ShapeDtypeStruct((M, 2 * half, 2, chans), f32),
        cost_estimate=cost(0, 24 * M * half * chans),
        name="assemble_input_grad",
    )(core, mine_conv, recv_conv, mine_gate, recv_gate)


def swap_core(value):
    count = lax.axis_size("batch")
    return lax.ppermute(value, "batch", [(i, i ^ 1) for i in range(count)])


def y_sum(value, wide):
    count = lax.axis_size("batch")
    chips = count // 2
    if chips == 2:
        other = lax.ppermute(value, "batch", [(i, i ^ 2) for i in range(count)])
        return value.astype(f32) + other.astype(f32)
    mine = lax.axis_index("batch") // 2
    buffer = jnp.zeros((chips,) + value.shape, value.dtype)
    for shift in range(chips):
        piece = value if shift == 0 else lax.ppermute(
            value, "batch", [(i, (i + 2 * shift) % count) for i in range(count)]
        )
        buffer = lax.dynamic_update_index_in_dim(buffer, piece, (mine + chips - shift) % chips, 0)
    return jnp.sum(buffer.astype(f32), axis=0)


def batch_total(value):
    return y_sum(value + swap_core(value), True)


def to_owners(pieces):
    return lax.all_to_all(pieces, "own", split_axis=0, concat_axis=0, tiled=False)


def to_all(piece):
    return to_owners(jnp.broadcast_to(piece[None], (lax.axis_size("own"),) + piece.shape))


def split_total(mine, send):
    got = swap_core(send)
    half = (mine + got.astype(f32)).astype(bf16)
    total = y_sum(half, False).astype(bf16)
    return total, swap_core(total)


def join_halves(core, mine, recv, axis):
    low = jnp.where(core == 0, mine, recv)
    high = jnp.where(core == 0, recv, mine)
    return jnp.concatenate([low, high], axis=axis)


def per_device(
    hidden_in, norm_gain, input_proj, conv_weight, conv_bias, state_proj, step_proj, step_bias,
    log_decay, skip_gain, output_proj, modality, grad_out,
):
    own_count = lax.axis_size("own")
    own_index = lax.axis_index("own")
    core = lax.axis_index("batch") % 2
    width = hidden_in.shape[2]
    rows = modality.shape[1]
    span = rows // own_count
    chans = input_proj.shape[3]
    rank = step_proj.shape[1]
    states = log_decay.shape[0]
    psize = state_proj.shape[2]
    chan_at = own_index * chans

    core_at = core.astype(jnp.int32).reshape(1)
    other_at = (1 - core).astype(jnp.int32).reshape(1)

    modc = modality.reshape(rows, 1)
    modl = modality.reshape(1, rows)
    modr = modality.reshape(rows // LANES, 1, LANES)
    w_in = input_proj.reshape(M, width, 2 * chans)
    sp_t = jnp.swapaxes(state_proj, 1, 2)
    part = lambda table: lax.dynamic_slice_in_dim(table, chan_at, chans, table.ndim - 1)
    cw = part(conv_weight)
    cb = part(conv_bias).reshape(1, chans)
    decay = part(log_decay)
    skip = part(skip_gain).reshape(1, chans)

    resid = hidden_in[0].astype(f32)
    inverse = lax.rsqrt(jnp.mean(resid * resid, axis=-1, keepdims=True) + epsilon)
    normed = (resid * inverse * norm_gain).astype(bf16)
    x = lax.all_gather(normed, "own", axis=0, tiled=True)
    cot = lax.all_gather(grad_out[0], "own", axis=0, tiled=True)

    conv_in, gate, act, proj_part = input_stage(x, w_in, cw, cb, sp_t, modc, modr)
    blocks = rows // LANES
    per_owner = blocks // own_count
    pieces = proj_part.astype(bf16).reshape(own_count, per_owner * psize, LANES)
    proj = jnp.sum(to_owners(pieces).astype(f32), axis=0).reshape(per_owner, psize, LANES)
    high = proj.astype(bf16)
    low = (proj[:, rank:] - high[:, rank:].astype(f32)).astype(bf16)
    packed = jnp.concatenate([high, low], axis=1)
    pj = to_all(packed).reshape(blocks, psize + 2 * states, LANES)
    gg = select_matmul(cot, output_proj, modc, True, bf16, "gated_grad")
    delta, sig, gated, ggate, prev, gct = scan_forward(
        pj, act, gate, gg, step_proj, step_bias, decay, skip, modc
    )
    branch = select_matmul(gated, output_proj, modc, False, f32, "output_stage")
    branch = lax.psum_scatter(branch, "own", scatter_dimension=0, tiled=True)
    block_out = (resid + branch).astype(bf16)[None]

    xt = jnp.swapaxes(x, 0, 1)
    gated_t = jnp.swapaxes(gated, 0, 1)
    out_send = half_wgrad(other_at, gated_t, cot, modl, bf16, "output_wgrad_send")
    out_mine = half_wgrad(core_at, gated_t, cot, modl, f32, "output_wgrad_keep")
    out_mine, out_recv = split_total(out_mine, out_send)
    grad_output = join_halves(core, out_mine, out_recv, 1).astype(f32)
    gate_send = half_wgrad(other_at, xt, ggate, modl, bf16, "gate_wgrad_send")
    gate_mine = half_wgrad(core_at, xt, ggate, modl, f32, "gate_wgrad_keep")
    gate_mine, gate_recv = split_total(gate_mine, gate_send)

    gas, gpt, glogd, gskip, gbias, gstep = scan_backward(
        pj, act, gate, gg, delta, sig, prev, gct, step_proj, decay, skip, modc, modr
    )
    gp_own = jnp.sum(to_owners(gpt.reshape(own_count, per_owner * psize, LANES)).astype(f32), axis=0).astype(bf16)
    gp = to_all(gp_own).reshape(blocks, psize, LANES)
    gci, gstate, gcw = conv_backward(gp, sp_t, gas, conv_in, act, cw, cb, modc, modr)

    conv_send = half_wgrad(other_at, xt, gci, modl, bf16, "conv_wgrad_send")
    conv_mine = half_wgrad(core_at, xt, gci, modl, f32, "conv_wgrad_keep")
    conv_mine, conv_recv = split_total(conv_mine, conv_send)
    gnormed = input_dgrad(gci, ggate, w_in, modc)
    gnormed = jnp.sum(to_owners(gnormed.reshape(own_count, span, width)).astype(f32), axis=0)

    weighted = norm_gain * gnormed
    coupled = jnp.mean(resid * weighted, axis=-1, keepdims=True)
    grad_hidden = (
        grad_out[0].astype(f32) + inverse * weighted - resid * (inverse * inverse * inverse) * coupled
    )[None]
    gain_part = jnp.sum(gnormed * resid * inverse, axis=0).reshape(width // LANES, LANES)
    grad_gain = batch_total(jnp.sum(to_all(gain_part), axis=0)).reshape(width)

    grad_input = assemble_input_grad(core_at, conv_mine, conv_recv, gate_mine, gate_recv)

    both = jnp.concatenate([gstep, gstate], axis=1)
    half_width = both.shape[1] // 2
    mine = lax.dynamic_slice_in_dim(both, core * half_width, half_width, 1)
    send = lax.dynamic_slice_in_dim(both, (1 - core) * half_width, half_width, 1).astype(bf16)
    mine, recv = split_total(mine, send)
    both = join_halves(core, mine, recv, 1).astype(f32)
    grad_step = both[:, :rank]
    grad_state = jnp.swapaxes(both[:, rank:], 1, 2)

    small = batch_total(jnp.concatenate([glogd, gcw[:5], gskip, gbias], axis=0))
    grad_bias = small[states + 6 :]
    wide = jnp.swapaxes(to_all(small[: states + 6]), 0, 1).reshape(states + 6, own_count * chans)
    return (
        block_out,
        grad_hidden,
        grad_gain,
        grad_input,
        wide[states : states + 4],
        wide[states + 4],
        grad_state,
        grad_step,
        grad_bias,
        wide[:states],
        wide[states + 5],
        grad_output,
    )


def solution(mesh):
    placed = (
        P("batch", "own", None),
        P(),
        P(None, None, None, "own"),
        P(),
        P(),
        P(None, "own", None),
        P(None, None, "own"),
        P(None, "own"),
        P(),
        P(),
        P(None, "own", None),
        P("batch", None),
        P("batch", "own", None),
    )
    return jax.shard_map(
        per_device,
        mesh=mesh,
        in_specs=placed,
        out_specs=(
            P("batch", "own", None),
            P("batch", "own", None),
            P(),
            P(None, None, None, "own"),
            P(),
            P(),
            P(None, "own", None),
            P(None, None, "own"),
            P(None, "own"),
            P(),
            P(),
            P(None, "own", None),
        ),
        check_vma=False,
    )
```

time: 2850 us -> 739 us (0.26); the launches traced: 2810 us -> 736 us
  waiting for transfers between devices: 1210 us -> 280 us
  other arithmetic: 686 us -> 64 us
  local copies, waits for them, and re-layouts: 652 us -> 65.9 us
  Pallas kernels: 0 us -> 275 us
  matrix products: 143 us -> 0 us
  blocking collectives: 50 us -> 0 us
    psum x4 -> x0, waiting for transfers between devices: 928 us -> none  [the longest x1 662 us: per_device(): lax.psum((grad_in_part, grad_state_part, grad_step_part, grad_bias_part,...]
    pallas_call x0 -> x14, Pallas kernels: none -> 275 us  [the longest x1 62.1 us: scan_backward(): pl.pallas_call(scan_bwd_body, grid=(blocks,), in_specs=[slab(pj.shape[1:]...]
    while x440 -> x0, other arithmetic: 193 us -> none
    reduce_scatter x2 -> x1, waiting for transfers between devices: 171 us -> 0.01 us  [per_device(): branch = lax.psum_scatter(branch, 'own', scatter_dimension=0, tiled=True)]
    ppermute x0 -> x16, waiting for transfers between devices: none -> 170 us  [the longest x6 167 us: y_sum(): other = lax.ppermute(value, 'batch', [(i, i ^ 2) for i in range(count)])]
    reduce_sum x152 -> x6, other arithmetic: 171 us -> 6.67 us  [the longest x1 3 us: per_device(): jnp.sum(to_owners(gnormed.reshape(own_count, span, width)).astype(f32), a...]
    dynamic_update_slice x174 -> x0, local copies, waits for them, and re-layouts: 144 us -> none  [the longest x160 126 us: run_block(): return lax.scan(advance, carried, inputs, unroll=8)]
    dot_general x13 -> x0, matrix products: 142 us -> none  [the longest x2 66.1 us: one_seq(): return jnp.einsum('ln,lne->le', read_one, decayed, precision=highest)]
  transfers between devices with their start and end apart: 19 -> 26, of which waited for: 9 -> 10; matrix products, arithmetic and copies ran while one was open for 44% -> 15% of each run, Pallas kernels for 0% -> 27%
where the time goes in v1:
time: 739 us; the launch traced here: 736 us
  waiting for transfers between devices  280 us (38%)
  Pallas kernels  275 us (37%)
  local copies, waits for them, and re-layouts  65.9 us (9%)
  other arithmetic  64 us (9%)
  starting transfers between devices  37.2 us (5%)
  between operations  14.2 us (2%)
    ppermute x6, waiting for transfers between devices, y_sum(): other = lax.ppermute(value, 'batch', [(i, i ^ 2) for i in range(count)])  167 us
    pallas_call x1, Pallas kernels, scan_backward(): pl.pallas_call(scan_bwd_body, grid=(blocks,), in_specs=[slab(pj.shape[1:]...  62.1 us
    pallas_call x1, Pallas kernels, scan_forward(): pl.pallas_call(scan_fwd_body, grid=(blocks,), in_specs=[pl.BlockSpec((1,)...  58.5 us
    all_gather x1, waiting for transfers between devices, per_device(): x = lax.all_gather(normed, 'own', axis=0, tiled=True)  52.5 us
    pallas_call x6, Pallas kernels, half_wgrad(): pl.pallas_call(wgrad_body, grid_spec=pltpu.PrefetchScalarGridSpec(num_sca...  43.4 us
    all_to_all x7, waiting for transfers between devices, to_owners(): lax.all_to_all(pieces, 'own', split_axis=0, concat_axis=0, tiled=False)  33.6 us
    all_to_all x7, starting transfers between devices, to_owners(): lax.all_to_all(pieces, 'own', split_axis=0, concat_axis=0, tiled=False)  29.8 us
    pallas_call x1, Pallas kernels, input_stage(): pl.pallas_call(functools.partial(in_body, rows=rows, block=256), grid=(ti...  27.2 us
  transfers between devices with their start and end apart: 26, of which 10 were waited for; matrix products, arithmetic and copies ran while one was open for 15% of the time, Pallas kernels for 27%

profile of v1, /device:TPU:0, one launch (start us, length us, event | category | flops | bytes accessed | tf_op | source)
XLA Modules:
  0.0 735.8 jit_solution(12858064190912632213)
XLA Ops:
  7.2 1.3 copy.81
  10.0 1.8 fusion.7
  12.6 20.9 %reshape.160.wc_ref.wg_ref = bf16[3,2048,1024]{2,1,0:T(8,128)(2,1)} reshape(bf16[3,2048,2,512]{3,2,1,0:T(2,128)(2,1)} %param.15) | data formatting | bytes 25165824 | tf_op jit(solution)/shard_map/reshape | solution.py:644
  33.5 1.0 copy.83.modc_ref
  34.5 1.3 dynamic_slice.19
  35.9 1.3 constant_dynamic-slice_fusion.1.cw_ref
  37.2 52.5 %all-gather.4.cloned.1.call-done = bf16[1024,2048]{0,1:T(8,128)(2,1)} async-done(((bf16[128,2048]{0,1:T(8,128)(2,1)}), bf16[1024,2048]{0,1:T(8,128)(2,1)}) %all-gather.4.cloned.1.call-update) | async-done | bytes 4194320 | tf_op jit(solution)/shard_map/all_gather | solution.py:655
  89.7 6.4 copy.82.x_ref
  96.1 27.2 %input_stage.1 = (bf16[1024,512]{1,0:T(8,128)(2,1)}, bf16[1024,512]{1,0:T(8,128)(2,1)}, bf16[1024,512]{1,0:T(8,128)(2,1)}, f32[8,160,128]{2,1,0:T(8,128)}) custom-call(bf16[1024,2048]{1,0:T(8,128)(2,1)} %copy.82.x_ref, bf16[3,2048,1024]{2,1,0:T(8,128)(2,1)} %reshape.160.wc_ref.wg_ref, bf16[3,2048,1024]{2,1,0:T(8,128)(2,1)} %reshape.160.wc_ref.wg_ref, ...), custom_call_target="tpu_custom_call" | custom-call | flops 12884901888 | bytes 16777216 | tf_op jit(solution)/shard_map/input_stage/pallas_call | solution.py:108
  123.3 2.0 convert_element_type.119
  125.3 3.4 all-to-all-start
  128.8 1.3 dynamic_slice.21
  130.1 18.9 %all-to-all-done = bf16[8,160,128]{2,1,0:T(8,128)(2,1)S(1)} async-done(((bf16[8,160,128]{2,1,0:T(8,128)(2,1)}), bf16[8,160,128]{2,1,0:T(8,128)(2,1)S(1)}, u32[]{:S(2)}, u32[]{:S(2)}) %all-to-all-start) | async-done | bytes 327712 | tf_op jit(solution)/shard_map/all_to_all | solution.py:602
  149.9 3.5 all-to-all-start.1
  154.0 22.4 %all-gather.6.cloned.1.call-done = bf16[1,1024,2048]{2,1,0:T(8,128)(2,1)} async-done(((bf16[1,128,2048]{2,1,0:T(8,128)(2,1)}), bf16[1,1024,2048]{2,1,0:T(8,128)(2,1)}) %all-gather.6.cloned.1.call-update) | async-done | bytes 4194320 | tf_op jit(solution)/shard_map/all_gather | solution.py:656
  176.4 12.1 %gated_grad.1.gg_ref = bf16[1024,512]{1,0:T(8,128)(2,1)} custom-call(bf16[1024,2048]{1,0:T(8,128)(2,1)} %bitcast.92, bf16[3,512,2048]{2,1,0:T(8,128)(2,1)} %w_ref.3, s32[1024,1]{1,0:T(8,128)} %copy.83.modc_ref), custom_call_target="tpu_custom_call" | custom-call | flops 6442450944 | bytes 11534336 | tf_op jit(solution)/shard_map/gated_grad/pallas_call | solution.py:156
  189.3 58.5 %scan_forward.1 = (bf16[1024,512]{1,0:T(8,128)(2,1)}, f32[1024,512]{1,0:T(8,128)}, bf16[1024,512]{1,0:T(8,128)(2,1)}, bf16[1024,512]{1,0:T(8,128)(2,1)}, f32[16384,512]{1,0:T(8,128)}, /*index=5*/f32[8,16,128]{2,1,0:T(8,128)}) custom-call(bf16[8,192,128]{2,1,0:T(8,128)(2,1)} %bitcast.75, bf16[1024,512]{1,0:T(8,128)(2,1)} %get-tuple-element.32.act_ref, ...), custom_call_target="tpu_custom_call" | custom-call | flops 40000000000 | bytes 44040192 | tf_op jit(solution)/shard_map/scan_forward/pallas_call | solution.py:311
  247.8 14.9 %output_stage.1 = f32[1024,2048]{1,0:T(8,128)} custom-call(bf16[1024,512]{1,0:T(8,128)(2,1)} %get-tuple-element.34.x_ref, bf16[3,512,2048]{2,1,0:T(8,128)(2,1)} %w_ref.3, s32[1024,1]{1,0:T(8,128)} %copy.83.modc_ref), custom_call_target="tpu_custom_call" | custom-call | flops 6442450944 | bytes 11534336 | tf_op jit(solution)/shard_map/output_stage/pallas_call | solution.py:156
  262.7 9.3 %copy.87 = f32[1024,2048]{0,1:T(8,128)} copy(f32[1024,2048]{1,0:T(8,128)} %output_stage.1) | data formatting | bytes 16777216 | tf_op jit(solution)/shard_map/output_stage/pallas_call | solution.py:156
  272.1 62.1 %scan_backward.1 = (bf16[1024,512]{1,0:T(8,128)(2,1)}, bf16[8,160,128]{2,1,0:T(8,128)(2,1)}, f32[16,512]{1,0:T(8,128)}, f32[1,512]{1,0:T(1,128)}, f32[3,512]{1,0:T(4,128)}, /*index=5*/f32[3,128,512]{2,1,0:T(8,128)}) custom-call(bf16[8,192,128]{2,1,0:T(8,128)(2,1)} %bitcast.76, bf16[1024,512]{1,0:T(8,128)(2,1)} %get-tuple-element.32.act_ref, ...), custom_call_target="tpu_custom_call" | custom-call | flops 60000002048 | bytes 44040192 | tf_op jit(solution)/shard_map/scan_backward/pallas_call | solution.py:432
  334.1 4.1 all-to-all-start.2
  338.2 1.3 copy.96
  339.6 7.4 %output_wgrad_send.1 = bf16[3,256,2048]{2,1,0:T(8,128)(2,1)} custom-call(s32[1]{0:T(128)} %bitcast.17.pos_ref, bf16[512,1024]{1,0:T(8,128)(2,1)} %bitcast.72, bf16[1024,2048]{1,0:T(8,128)(2,1)} %bitcast.93, s32[1,1024]{1,0:T(1,128)} %modl_ref.11), custom_call_target="tpu_custom_call" | custom-call | flops 3221225472 | bytes 11010048 | tf_op jit(solution)/shard_map/output_wgrad_send/pallas_call | solution.py:221
  346.9 9.8 %all-to-all-done.2 = bf16[8,160,128]{2,1,0:T(8,128)(2,1)} async-done(((bf16[8,160,128]{2,1,0:T(8,128)(2,1)}), bf16[8,160,128]{2,1,0:T(8,128)(2,1)}, u32[]{:S(2)}, u32[]{:S(2)}) %all-to-all-start.2) | async-done | bytes 327712 | tf_op jit(solution)/shard_map/all_to_all | solution.py:602
  358.6 4.3 all-to-all-start.3
  362.8 6.7 gate_wgrad_send.1
  369.6 3.6 all-to-all-done.3.gp_ref
  373.2 11.6 %conv_backward.1 = (bf16[1024,512]{1,0:T(8,128)(2,1)}, f32[3,160,512]{2,1,0:T(8,128)}, f32[8,512]{1,0:T(8,128)}) custom-call(bf16[8,160,128]{2,1,0:T(8,128)(2,1)} %all-to-all-done.3.gp_ref, bf16[3,160,512]{2,1,0:T(8,128)(2,1)} %bitcast.96, bf16[1024,512]{1,0:T(8,128)(2,1)} %get-tuple-element.40.gas_ref, bf16[1024,512]{1,0:T(8,128)(2,1)} %get-tuple-element.41.ci_ref, ...), custom_call_target="tpu_custom_call" | custom-call | flops 2013265920 | bytes 5242880 | tf_op jit(solution)/shard_map/conv_backward/pallas_call | solution.py:524
  385.6 8.4 %output_wgrad_keep.1 = f32[3,256,2048]{2,1,0:T(8,128)} custom-call(s32[1]{0:T(128)} %bitcast.15.pos_ref, bf16[512,1024]{1,0:T(8,128)(2,1)} %bitcast.73, bf16[1024,2048]{1,0:T(8,128)(2,1)} %bitcast.94, s32[1,1024]{1,0:T(1,128)} %modl_ref.11), custom_call_target="tpu_custom_call" | custom-call | flops 3221225472 | bytes 11010048 | tf_op jit(solution)/shard_map/output_wgrad_keep/pallas_call | solution.py:221
  394.1 1.2 collective-permute-start.9
  395.2 6.6 conv_wgrad_send.1
  402.9 4.1 all-to-all-start.6
  407.0 22.8 %input_dgrad.1 = bf16[1024,2048]{1,0:T(8,128)(2,1)} custom-call(bf16[1024,512]{1,0:T(8,128)(2,1)} %get-tuple-element.42.gc_ref.g_ref, bf16[1024,512]{1,0:T(8,128)(2,1)} %get-tuple-element.43.gg_ref.g_ref, bf16[3,2048,1024]{2,1,0:T(8,128)(2,1)} %reshape.160.wc_ref.wg_ref, s32[1024,1]{1,0:T(8,128)} %copy.83.modc_ref), custom_call_target="tpu_custom_call" | custom-call | flops 12884901888 | bytes 18874368 | tf_op jit(solution)/shard_map/input_dgrad/pallas_call | solution.py:193
  429.8 1.2 all-to-all-done.6
  431.0 4.8 all-to-all-start.4
  435.8 5.6 add_convert_fusion.1
  442.3 7.1 gate_wgrad_keep.1
  449.4 7.1 conv_wgrad_keep.1
  456.5 5.0 add_convert_fusion.3
  461.5 1.2 collective-permute-start.6
  462.7 4.6 add_convert_fusion.5
  468.3 1.2 constant_dynamic-update-slice_fusion.1
  469.4 1.3 constant_dynamic-update-slice_fusion
  470.7 1.2 copy-done.5
  472.8 2.1 collective-permute-done.10
  474.9 2.2 add_convert_fusion.7
  477.1 1.1 collective-permute-start.11
  478.2 34.5 %collective-permute-done.14 = bf16[3,256,2048]{2,1,0:T(8,128)(2,1)} collective-permute-done((bf16[3,256,2048]{2,1,0:T(8,128)(2,1)}, bf16[3,256,2048]{2,1,0:T(8,128)(2,1)}, u32[]{:S(2)}, u32[]{:S(2)}) %collective-permute-start.14) | collective-permute-done | bytes 3145760 | tf_op jit(solution)/shard_map/ppermute | solution.py:585
  512.7 6.1 add_convert_fusion
  518.8 2.0 copy.88
  521.5 1.5 slice.57
  523.0 132.7 %collective-permute-done.11 = bf16[3,144,512]{2,1,0:T(8,128)(2,1)} collective-permute-done((bf16[3,144,512]{2,1,0:T(8,128)(2,1)}, bf16[3,144,512]{2,1,0:T(8,128)(2,1)}, u32[]{:S(2)}, u32[]{:S(2)}) %collective-permute-start.11) | collective-permute-done | bytes 442400 | tf_op jit(solution)/shard_map/ppermute | solution.py:585
  655.7 1.3 add_convert_fusion.6
  657.1 4.4 add_convert_fusion.2.mg_ref
  662.0 5.5 add_convert_fusion.4.mc_ref
  669.2 1.6 fusion.19
  673.1 3.0 convert_reduce_fusion
  676.5 6.0 broadcast_select_fusion.1
  682.5 2.3 fusion.11
  685.4 5.7 all-to-all-start.5
  691.1 9.2 %maximum_convert_fusion = f32[3,512,2048]{2,1,0:T(8,128)} fusion(bf16[3,256,2048]{2,1,0:T(8,128)(2,1)} %get-tuple-element.113, bf16[3,256,2048]{2,1,0:T(8,128)(2,1)} %get-tuple-element.112), kind=kLoop, calls=%fused_computation.1 | loop fusion | flops 12582912 | bytes 18874368 | tf_op jit(solution)/shard_map/convert_element_type | solution.py:680
  700.4 22.4 %assemble_input_grad.1 = f32[3,2048,2,512]{3,2,1,0:T(2,128)} custom-call(s32[1]{0:T(128)} %bitcast.15.pos_ref, bf16[3,1024,512]{2,1,0:T(8,128)(2,1)} %add_convert_fusion.4.mc_ref, bf16[3,1024,512]{2,1,0:T(8,128)(2,1)} %collective-permute-done.4.rc_ref, bf16[3,1024,512]{2,1,0:T(8,128)(2,1)} %add_convert_fusion.2.mg_ref, ...), custom_call_target="tpu_custom_call" | custom-call | bytes 37748736 | tf_op jit(solution)/shard_map/assemble_input_grad/pallas_call | solution.py:562
  725.3 2.0 copy.97
  727.3 1.3 copy.98
  (101 shorter events, 20.0 us)
Async XLA Ops:
  7.2 146.2 %copy-start = (f32[16,4096]{1,0:T(8,128)S(1)}, f32[16,4096]{1,0:T(8,128)}, u32[]{:S(2)}) copy-start(f32[16,4096]{1,0:T(8,128)} %param.21) | copy-start | bytes 786436
  7.2 82.5 %all-gather.4.cloned.1.call-start = ((), (), s32[]{:S(2)}) async-start(), calls=%async_computation.8 | async-start | bytes 4718592 | tf_op jit(solution)/shard_map/all_gather | solution.py:655
  8.6 24.9 %copy-start.2 = (bf16[1,128,2048]{1,2,0:T(8,128)(2,1)}, bf16[1,128,2048]{1,2,0:T(8,128)(2,1)S(1)}, u32[]{:S(2)}) copy-start(bf16[1,128,2048]{1,2,0:T(8,128)(2,1)S(1)} %copy.81) | copy-start | bytes 1572868
  9.5 0.5 copy-start.14
  11.8 164.6 %all-gather.6.cloned.1.call-start = ((), (), s32[]{:S(2)}) async-start(), calls=%async_computation.10 | async-start | bytes 4718592 | tf_op jit(solution)/shard_map/all_gather | solution.py:656
  12.6 20.9 %copy-start.16 = (s32[1,1024]{1,0:T(1,128)S(1)}, s32[1,1024]{1,0:T(1,128)}, u32[]{:S(2)}) copy-start(s32[1,1024]{1,0:T(1,128)} %modl_ref.11) | copy-start | bytes 12292
  125.3 23.7 %all-to-all-start = ((bf16[8,160,128]{2,1,0:T(8,128)(2,1)}), bf16[8,160,128]{2,1,0:T(8,128)(2,1)S(1)}, u32[]{:S(2)}, u32[]{:S(2)}) async-start(bf16[8,160,128]{2,1,0:T(8,128)(2,1)} %convert_element_type.119), calls=%async_computation | async-start | bytes 655360 | tf_op jit(solution)/shard_map/all_to_all | solution.py:602
  149.9 38.6 %all-to-all-start.1 = ((bf16[8,1,192,128]{3,2,1,0:T(8,128)(2,1)}), bf16[8,1,192,128]{3,2,1,0:T(8,128)(2,1)S(1)}, u32[]{:S(2)}, u32[]{:S(2)}) async-start(bf16[8,1,192,128]{3,2,1,0:T(8,128)(2,1)} %broadcast_in_dim.15), calls=%async_computation.1 | async-start | bytes 786432 | tf_op jit(solution)/shard_map/all_to_all | solution.py:602
  153.4 529.1 %reduce-scatter.2.cloned.1.call-start = ((), (), s32[]{:S(2)}) async-start(), calls=%async_computation.9 | async-start | bytes 9437184 | tf_op jit(solution)/shard_map/reduce_scatter | solution.py:672
  188.5 0.7 copy-start.8
  272.0 66.2 %copy-start.7 = (bf16[1024,512]{1,0:T(8,128)(2,1)S(1)}, bf16[1024,512]{1,0:T(8,128)(2,1)}, u32[]{:S(2)}) copy-start(bf16[1024,512]{1,0:T(8,128)(2,1)} %get-tuple-element.34.x_ref) | copy-start | bytes 3145732
  334.1 22.7 %all-to-all-start.2 = ((bf16[8,160,128]{2,1,0:T(8,128)(2,1)}), bf16[8,160,128]{2,1,0:T(8,128)(2,1)}, u32[]{:S(2)}, u32[]{:S(2)}) async-start(bf16[8,160,128]{2,1,0:T(8,128)(2,1)} %get-tuple-element.39), calls=%async_computation.3 | async-start | bytes 655360 | tf_op jit(solution)/shard_map/all_to_all | solution.py:602
  346.9 88.9 %collective-permute-start.13 = (bf16[3,256,2048]{2,1,0:T(8,128)(2,1)}, bf16[3,256,2048]{2,1,0:T(8,128)(2,1)S(1)}, u32[]{:S(2)}, u32[]{:S(2)}) collective-permute-start(bf16[3,256,2048]{2,1,0:T(8,128)(2,1)} %output_wgrad_send.1), channel_id=1, source_target_pairs={{0,8},{8,0},{16,24},{24,16},{1,9},{9,1},{17,25},{25,17},{2,10},{10... | collective-permute-start | bytes 9437192 | tf_op jit(solution)/shard_map/ppermute | solution.py:578
  358.6 14.6 %all-to-all-start.3 = ((bf16[8,160,128]{2,1,0:T(8,128)(2,1)}), bf16[8,160,128]{2,1,0:T(8,128)(2,1)}, u32[]{:S(2)}, u32[]{:S(2)}) async-start(bf16[8,160,128]{2,1,0:T(8,128)(2,1)} %broadcast_in_dim.17), calls=%async_computation.4 | async-start | bytes 655360 | tf_op jit(solution)/shard_map/all_to_all | solution.py:602
  369.5 87.0 %collective-permute-start.5 = (bf16[3,1024,512]{2,1,0:T(8,128)(2,1)}, bf16[3,1024,512]{2,1,0:T(8,128)(2,1)}, u32[]{:S(2)}, u32[]{:S(2)}) collective-permute-start(bf16[3,1024,512]{2,1,0:T(8,128)(2,1)} %gate_wgrad_send.1), channel_id=1, source_target_pairs={{0,8},{8,0},{16,24},{24,16},{1,9},{9,1},{17,25},{25,17},{2,10},{10... | collective-permute-start | bytes 9437192 | tf_op jit(solution)/shard_map/ppermute | solution.py:578
  373.1 11.6 %copy-start.9 = (f32[16,512]{1,0:T(8,128)S(1)}, f32[16,512]{1,0:T(8,128)}, u32[]{:S(2)}) copy-start(f32[16,512]{1,0:T(8,128)} %get-tuple-element.44) | copy-start | bytes 98308
  373.1 11.6 %copy-start.12 = (f32[3,512]{1,0:T(4,128)S(1)}, f32[3,512]{1,0:T(4,128)}, u32[]{:S(2)}) copy-start(f32[3,512]{1,0:T(4,128)} %get-tuple-element.47) | copy-start | bytes 18436
  373.2 11.6 %copy-start.13 = (f32[1,512]{1,0:T(1,128)S(1)}, f32[1,512]{1,0:T(1,128)}, u32[]{:S(2)}) copy-start(f32[1,512]{1,0:T(1,128)} %get-tuple-element.46) | copy-start | bytes 6148
  385.5 8.5 %collective-permute-start.8 = (f32[25,512]{1,0:T(8,128)S(1)}, f32[25,512]{1,0:T(8,128)S(1)}, u32[]{:S(2)}, u32[]{:S(2)}) collective-permute-start(f32[25,512]{1,0:T(8,128)S(1)} %pad_maximum_fusion), channel_id=1, source_target_pairs={{0,8},{8,0},{16,24},{24,16},{1,9},{9,1},{17,25},{25,17},{2,10},{10... | collective-permute-start | bytes 153608 | tf_op jit(solution)/shard_map/ppermute | solution.py:578
  385.6 8.5 %copy-start.11 = (f32[8,512]{1,0:T(8,128)S(1)}, f32[8,512]{1,0:T(8,128)}, u32[]{:S(2)}) copy-start(f32[8,512]{1,0:T(8,128)} %get-tuple-element.45) | copy-start | bytes 49156
  394.1 8.0 %collective-permute-start.9 = (f32[25,512]{1,0:T(8,128)S(1)}, f32[25,512]{1,0:T(8,128)S(1)}, u32[]{:S(2)}, u32[]{:S(2)}) collective-permute-start(f32[25,512]{1,0:T(8,128)S(1)} %fusion.18), channel_id=1, source_target_pairs={{0,16},{8,24},{16,0},{24,8},{1,17},{9,25},{17,1},{25,9},{2,18},{10... | collective-permute-start | bytes 153608 | tf_op jit(solution)/shard_map/ppermute | solution.py:585
  401.9 60.9 %collective-permute-start.2 = (bf16[3,1024,512]{2,1,0:T(8,128)(2,1)}, bf16[3,1024,512]{2,1,0:T(8,128)(2,1)}, u32[]{:S(2)}, u32[]{:S(2)}) collective-permute-start(bf16[3,1024,512]{2,1,0:T(8,128)(2,1)} %conv_wgrad_send.1), channel_id=1, source_target_pairs={{0,8},{8,0},{16,24},{24,16},{1,9},{9,1},{17,25},{25,17},{2,10},{10... | collective-permute-start | bytes 9437192 | tf_op jit(solution)/shard_map/ppermute | solution.py:578
  402.9 28.1 %all-to-all-start.6 = ((f32[8,22,512]{2,1,0:T(8,128)}), f32[8,22,512]{2,1,0:T(8,128)}, u32[]{:S(2)}, u32[]{:S(2)}) async-start(f32[8,22,512]{2,1,0:T(8,128)} %broadcast_in_dim.20), calls=%async_computation.7 | async-start | bytes 786432 | tf_op jit(solution)/shard_map/all_to_all | solution.py:602
  431.0 242.1 %all-to-all-start.4 = ((bf16[8,128,2048]{2,1,0:T(8,128)(2,1)}), bf16[8,128,2048]{2,1,0:T(8,128)(2,1)}, u32[]{:S(2)}, u32[]{:S(2)}) async-start(bf16[8,128,2048]{2,1,0:T(8,128)(2,1)} %bitcast.71), calls=%async_computation.5 | async-start | bytes 8388608 | tf_op jit(solution)/shard_map/all_to_all | solution.py:602
  441.4 71.3 %collective-permute-start.14 = (bf16[3,256,2048]{2,1,0:T(8,128)(2,1)}, bf16[3,256,2048]{2,1,0:T(8,128)(2,1)}, u32[]{:S(2)}, u32[]{:S(2)}) collective-permute-start(bf16[3,256,2048]{2,1,0:T(8,128)(2,1)} %add_convert_fusion.1), channel_id=1, source_target_pairs={{0,16},{8,24},{16,0},{24,8},{1,17},{9,25},{17,1},{25,9},{2,18},{10... | collective-permute-start | bytes 9437192 | tf_op jit(solution)/shard_map/ppermute | solution.py:585
  456.5 6.2 copy-start.4
  461.5 195.6 %collective-permute-start.6 = (bf16[3,1024,512]{2,1,0:T(8,128)(2,1)S(1)}, bf16[3,1024,512]{2,1,0:T(8,128)(2,1)}, u32[]{:S(2)}, u32[]{:S(2)}) collective-permute-start(bf16[3,1024,512]{2,1,0:T(8,128)(2,1)S(1)} %add_convert_fusion.3), channel_id=1, source_target_pairs={{0,16},{8,24},{16,0},{24,8},{1,17},{9,25},{17,1},{25,9},{2,18},{10... | collective-permute-start | bytes 9437192 | tf_op jit(solution)/shard_map/ppermute | solution.py:585
  467.4 194.6 %collective-permute-start.3 = (bf16[3,1024,512]{2,1,0:T(8,128)(2,1)}, bf16[3,1024,512]{2,1,0:T(8,128)(2,1)}, u32[]{:S(2)}, u32[]{:S(2)}) collective-permute-start(bf16[3,1024,512]{2,1,0:T(8,128)(2,1)} %add_convert_fusion.5), channel_id=1, source_target_pairs={{0,16},{8,24},{16,0},{24,8},{1,17},{9,25},{17,1},{25,9},{2,18},{10... | collective-permute-start | bytes 9437192 | tf_op jit(solution)/shard_map/ppermute | solution.py:585
  470.7 1.2 copy-start.5
  472.7 2.1 collective-permute-start.10
  477.1 178.6 %collective-permute-start.11 = (bf16[3,144,512]{2,1,0:T(8,128)(2,1)}, bf16[3,144,512]{2,1,0:T(8,128)(2,1)}, u32[]{:S(2)}, u32[]{:S(2)}) collective-permute-start(bf16[3,144,512]{2,1,0:T(8,128)(2,1)} %add_convert_fusion.7), channel_id=1, source_target_pairs={{0,16},{8,24},{16,0},{24,8},{1,17},{9,25},{17,1},{25,9},{2,18},{10... | collective-permute-start | bytes 1327112 | tf_op jit(solution)/shard_map/ppermute | solution.py:585
  518.8 157.7 %collective-permute-start.15 = (bf16[3,256,2048]{2,1,0:T(8,128)(2,1)}, bf16[3,256,2048]{2,1,0:T(8,128)(2,1)}, u32[]{:S(2)}, u32[]{:S(2)}) collective-permute-start(bf16[3,256,2048]{2,1,0:T(8,128)(2,1)} %add_convert_fusion), channel_id=1, source_target_pairs={{0,8},{8,0},{16,24},{24,16},{1,9},{9,1},{17,25},{25,17},{2,10},{10... | collective-permute-start | bytes 9437192 | tf_op jit(solution)/shard_map/ppermute | solution.py:578
  657.0 13.8 %collective-permute-start.12 = (bf16[3,144,512]{2,1,0:T(8,128)(2,1)S(1)}, bf16[3,144,512]{2,1,0:T(8,128)(2,1)S(1)}, u32[]{:S(2)}, u32[]{:S(2)}) collective-permute-start(bf16[3,144,512]{2,1,0:T(8,128)(2,1)S(1)} %add_convert_fusion.6), channel_id=1, source_target_pairs={{0,8},{8,0},{16,24},{24,16},{1,9},{9,1},{17,25},{25,17},{2,10},{10... | collective-permute-start | bytes 1327112 | tf_op jit(solution)/shard_map/ppermute | solution.py:578
  661.5 38.9 %collective-permute-start.7 = (bf16[3,1024,512]{2,1,0:T(8,128)(2,1)}, bf16[3,1024,512]{2,1,0:T(8,128)(2,1)}, u32[]{:S(2)}, u32[]{:S(2)}) collective-permute-start(bf16[3,1024,512]{2,1,0:T(8,128)(2,1)} %add_convert_fusion.2.mg_ref), channel_id=1, source_target_pairs={{0,8},{8,0},{16,24},{24,16},{1,9},{9,1},{17,25},{25,17},{2,10},{10... | collective-permute-start | bytes 9437192 | tf_op jit(solution)/shard_map/ppermute | solution.py:578
  667.5 32.9 %collective-permute-start.4 = (bf16[3,1024,512]{2,1,0:T(8,128)(2,1)}, bf16[3,1024,512]{2,1,0:T(8,128)(2,1)}, u32[]{:S(2)}, u32[]{:S(2)}) collective-permute-start(bf16[3,1024,512]{2,1,0:T(8,128)(2,1)} %add_convert_fusion.4.mc_ref), channel_id=1, source_target_pairs={{0,8},{8,0},{16,24},{24,16},{1,9},{9,1},{17,25},{25,17},{2,10},{10... | collective-permute-start | bytes 9437192 | tf_op jit(solution)/shard_map/ppermute | solution.py:578
  676.5 6.0 copy-start.3
  676.5 6.0 copy-start.10
  676.5 6.0 copy-start.15
  685.4 37.3 %all-to-all-start.5 = ((f32[8,16,128]{2,1,0:T(8,128)}), f32[8,16,128]{2,1,0:T(8,128)S(1)}, u32[]{:S(2)}, u32[]{:S(2)}) async-start(f32[8,16,128]{2,1,0:T(8,128)} %broadcast_in_dim.19), calls=%async_computation.6 | async-start | bytes 131072 | tf_op jit(solution)/shard_map/all_to_all | solution.py:602
  700.3 24.6 %copy-start.6 = (bf16[1,128,2048]{1,2,0:T(8,128)(2,1)S(1)}, bf16[1,128,2048]{1,2,0:T(8,128)(2,1)}, u32[]{:S(2)}) copy-start(bf16[1,128,2048]{1,2,0:T(8,128)(2,1)} %copy.88) | copy-start | bytes 1572868
  700.3 24.6 %copy-start.17 = (f32[128]{0:T(128)S(1)}, f32[128]{0:T(128)}, u32[]{:S(2)}) copy-start(f32[128]{0:T(128)} %get-tuple-element.119) | copy-start | bytes 1540
  722.8 1.2 collective-permute-start
  724.0 4.6 collective-permute-start.1
  724.9 4.3 copy-start.1
Sparse Core Ops, SparseCore 0:
  11.9 77.7 all-gather.3
  91.8 84.5 all-gather.5
  272.2 164.8 reduce-scatter.1

commit v2 on v1

v2 whole, which is shorter than its diff:
```python
import functools

import jax
import jax.numpy as jnp
from jax import lax
from jax.experimental import pallas as pl
from jax.experimental.pallas import tpu as pltpu
from jax.sharding import PartitionSpec as P

M = 3
epsilon = 1e-05
LANES = 128
log2e = 1.4426950408889634
bf16 = jnp.bfloat16
f32 = jnp.float32


def contract(a, b, ca, cb):
    return lax.dot_general(a, b, (((ca,), (cb,)), ((), ())), preferred_element_type=f32)


def pick(mod, parts):
    out = parts[-1]
    for m in reversed(range(len(parts) - 1)):
        out = jnp.where(mod == m, parts[m], out)
    return out


def sigmoid(v):
    return 1.0 / (1.0 + jnp.exp(-v))


def fold_rows(vs):
    sub = lax.broadcasted_iota(jnp.int32, vs[0].shape, 0)
    for shift in (1, 2, 4):
        mask = (sub & shift) == 0
        vs = [
            jnp.where(mask, a, b) + pltpu.roll(jnp.where(mask, b, a), shift, 0)
            for a, b in zip(vs[0::2], vs[1::2])
        ]
    return vs[0]


def fold_lanes(vs, shifts):
    lane = lax.broadcasted_iota(jnp.int32, vs[0].shape, 1)
    for shift in shifts:
        mask = (lane & shift) == 0
        vs = [
            jnp.where(mask, a, b) + pltpu.roll(jnp.where(mask, b, a), shift, 1)
            for a, b in zip(vs[0::2], vs[1::2])
        ]
    return vs[0]


def cost(flops, nbytes):
    return pl.CostEstimate(flops=int(flops), bytes_accessed=int(nbytes), transcendentals=0)


def in_body(x_ref, wc_ref, wg_ref, cw_ref, cb_ref, sp_ref, modc_ref, modr_ref,
            ci_ref, gate_ref, act_ref, proj_ref, pad, sums, *, rows, block):
    tile = pl.program_id(0)
    pad[0:8, :] = jnp.zeros((8, pad.shape[1]), f32)

    def matmul(r, _):
        at = pl.multiple_of(r * block, block)
        x = x_ref[pl.ds(at, block), :]
        mc = modc_ref[pl.ds(at, block), :]
        conv = pick(mc, [contract(x, wc_ref[m], 1, 0) for m in range(M)]).astype(bf16)
        ci_ref[pl.ds(at, block), :] = conv
        pad[pl.ds(at + 8, block), :] = conv.astype(f32)
        gate_ref[pl.ds(at, block), :] = pick(
            mc, [contract(x, wg_ref[m], 1, 0) for m in range(M)]
        ).astype(bf16)
        return 0

    lax.fori_loop(0, rows // block, matmul, 0)
    taps = cw_ref[...]
    base = cb_ref[...]

    def convolve(r, _):
        at = pl.multiple_of(r * LANES, LANES)
        v = pad[pl.ds(at, LANES + 8), :]
        s = base
        for k in range(4):
            s = s + taps[k : k + 1, :] * v[5 + k : 5 + k + LANES, :]
        act = (s * sigmoid(s)).astype(bf16)
        act_ref[pl.ds(at, LANES), :] = act
        part = pick(modr_ref[r], [contract(sp_ref[m], act, 1, 1) for m in range(M)])

        @pl.when(tile == 0)
        def _():
            sums[r] = part

        @pl.when(tile != 0)
        def _():
            sums[r] += part

        proj_ref[r] = sums[r].astype(bf16)
        return 0

    lax.fori_loop(0, rows // LANES, convolve, 0)


def input_stage(x, w, cw, cb, sp, modc, modr):
    rows, width = x.shape
    chans = cw.shape[1]
    psize = sp.shape[1]
    tc = min(256, chans)
    tiles = chans // tc
    full = lambda shape: pl.BlockSpec(shape, lambda j: (0,) * len(shape))
    col = lambda r: pl.BlockSpec((r, tc), lambda j: (0, j))
    return pl.pallas_call(
        functools.partial(in_body, rows=rows, block=min(256, rows)),
        grid=(tiles,),
        in_specs=[
            full((rows, width)),
            pl.BlockSpec((M, width, tc), lambda j: (0, 0, j)),
            pl.BlockSpec((M, width, tc), lambda j: (0, 0, j + tiles)),
            col(4),
            col(1),
            pl.BlockSpec((M, psize, tc), lambda j: (0, 0, j)),
            full((rows, 1)),
            full(modr.shape),
        ],
        out_specs=[col(rows), col(rows), col(rows), full((rows // LANES, psize, LANES))],
        out_shape=[
            jax.ShapeDtypeStruct((rows, chans), bf16),
            jax.ShapeDtypeStruct((rows, chans), bf16),
            jax.ShapeDtypeStruct((rows, chans), bf16),
            jax.ShapeDtypeStruct((rows // LANES, psize, LANES), bf16),
        ],
        scratch_shapes=[pltpu.VMEM((rows + 8, tc), f32), pltpu.VMEM((rows // LANES, psize, LANES), f32)],
        cost_estimate=cost(2 * M * rows * width * 2 * chans, 2 * (rows * width + M * width * 2 * chans)),
        name="input_stage",
    )(x, w, w, cw, cb, sp, modc, modr)


def mm_body(x_ref, w_ref, modc_ref, o_ref, *, rows, block, rhs_dim):
    def step(r, _):
        at = pl.multiple_of(r * block, block)
        x = x_ref[pl.ds(at, block), :]
        mc = modc_ref[pl.ds(at, block), :]
        o_ref[pl.ds(at, block), :] = pick(
            mc, [contract(x, w_ref[m], 1, rhs_dim) for m in range(M)]
        ).astype(o_ref.dtype)
        return 0

    lax.fori_loop(0, rows // block, step, 0)


def select_matmul(x, w, modc, transposed, dtype, name):
    rows, depth = x.shape
    cols = w.shape[1] if transposed else w.shape[2]
    tn = min(256, cols)
    wspec = (
        pl.BlockSpec((M, tn, depth), lambda j: (0, j, 0))
        if transposed
        else pl.BlockSpec((M, depth, tn), lambda j: (0, 0, j))
    )
    return pl.pallas_call(
        functools.partial(mm_body, rows=rows, block=min(512, rows), rhs_dim=1 if transposed else 0),
        grid=(cols // tn,),
        in_specs=[
            pl.BlockSpec((rows, depth), lambda j: (0, 0)),
            wspec,
            pl.BlockSpec((rows, 1), lambda j: (0, 0)),
        ],
        out_specs=pl.BlockSpec((rows, tn), lambda j: (0, j)),
        out_shape=jax.ShapeDtypeStruct((rows, cols), dtype),
        cost_estimate=cost(2 * M * rows * depth * cols, 2 * (rows * depth + M * depth * cols + rows * cols)),
        name=name,
    )(x, w, modc)


def gated_body(x_ref, w_ref, modc_ref, scanned_ref, gate_ref, gg_ref, ggate_ref):
    block = min(512, x_ref.shape[0])

    def step(r, _):
        here = pl.ds(pl.multiple_of(r * block, block), block)
        x = x_ref[here, :]
        gg = pick(modc_ref[here, :], [contract(x, w_ref[m], 1, 1) for m in range(M)]).astype(bf16)
        gg_ref[here, :] = gg
        gate = gate_ref[here, :].astype(f32)
        s = sigmoid(gate)
        ggate_ref[here, :] = (gg.astype(f32) * scanned_ref[here, :] * (s * (1.0 + gate * (1.0 - s)))).astype(bf16)
        return 0

    lax.fori_loop(0, x_ref.shape[0] // block, step, 0)


def gated_grads(cot, w, modc, scanned, gate):
    rows, depth = cot.shape
    cols = w.shape[1]
    tn = min(256, cols)
    col = pl.BlockSpec((rows, tn), lambda j: (0, j))
    return pl.pallas_call(
        gated_body,
        grid=(cols // tn,),
        in_specs=[
            pl.BlockSpec((rows, depth), lambda j: (0, 0)),
            pl.BlockSpec((M, tn, depth), lambda j: (0, j, 0)),
            pl.BlockSpec((rows, 1), lambda j: (0, 0)),
            col,
            col,
        ],
        out_specs=[col, col],
        out_shape=[jax.ShapeDtypeStruct((rows, cols), bf16)] * 2,
        cost_estimate=cost(2 * M * rows * depth * cols, 2 * (rows * depth + M * depth * cols + 5 * rows * cols)),
        name="gated_grads",
    )(cot, w, modc, scanned, gate)


def dgrad_body(gc_ref, gg_ref, w_ref, modc_ref, x_ref, gain_ref, o_ref, part_ref, *, rows, block, chans):
    sums = jnp.zeros((8, part_ref.shape[1]), f32)
    for r in range(rows // block):
        here = slice(r * block, (r + 1) * block)
        gc = gc_ref[here, :]
        gg = gg_ref[here, :]
        out = pick(
            modc_ref[here, :],
            [contract(gc, w_ref[m, :, :chans], 1, 1) + contract(gg, w_ref[m, :, chans:], 1, 1) for m in range(M)],
        )
        o_ref[here, :] = out.astype(bf16)
        terms = out * x_ref[here, :].astype(f32)
        sums = sums + jnp.sum(terms.reshape(block // 8, 8, terms.shape[1]), axis=0)
    part_ref[...] = jnp.sum(sums, axis=0, keepdims=True) / gain_ref[...]


def input_dgrad(gc, gg, w, modc, x, gain):
    rows, chans = gc.shape
    width = w.shape[1]
    tn = 256
    col = pl.BlockSpec((rows, tn), lambda j: (0, j))
    row = pl.BlockSpec((1, tn), lambda j: (0, j))
    return pl.pallas_call(
        functools.partial(dgrad_body, rows=rows, block=min(1024, rows), chans=chans),
        grid=(width // tn,),
        in_specs=[
            pl.BlockSpec((rows, chans), lambda j: (0, 0)),
            pl.BlockSpec((rows, chans), lambda j: (0, 0)),
            pl.BlockSpec((M, tn, 2 * chans), lambda j: (0, j, 0)),
            pl.BlockSpec((rows, 1), lambda j: (0, 0)),
            col,
            row,
        ],
        out_specs=[col, row],
        out_shape=[jax.ShapeDtypeStruct((rows, width), bf16), jax.ShapeDtypeStruct((1, width), f32)],
        cost_estimate=cost(4 * M * rows * chans * width, 2 * (2 * rows * chans + 2 * M * chans * width + 2 * rows * width)),
        name="input_dgrad",
    )(gc, gg, w, modc, x, gain)


def wgrad_body(*refs, sets, add):
    xs, gs, mods = refs[1 : 1 + sets], refs[1 + sets : 1 + 2 * sets], refs[1 + 2 * sets : 1 + 3 * sets]
    o_ref, masked = refs[-2], refs[-1]

    @pl.when(pl.program_id(0) == 0)
    def _():
        for n in range(sets):
            g = gs[n][...]
            for m in range(M):
                masked[n, m] = jnp.where(mods[n][...] == m, g, jnp.zeros_like(g))

    there = refs[0][0] >= 0

    def each(m, _):
        parts = [jnp.where(there, contract(xs[n][...], masked[n, m], 0, 0), 0.0) for n in range(sets)]
        total = functools.reduce(jnp.add, parts)
        if add:
            total = total + refs[1 + 3 * sets][m].astype(f32)
        o_ref[m] = total.astype(bf16)
        return 0

    lax.fori_loop(0, M, each, 0)


def half_wgrad(half, xs, gs, mods, got, name):
    sets = len(xs)
    rows, width = xs[0].shape
    cols = gs[0].shape[1]
    td = min(512, width // 2)
    steps = width // 2 // td
    full = lambda shape: pl.BlockSpec(shape, lambda i, pos: (0, 0))
    out_spec = pl.BlockSpec((M, td, cols), lambda i, pos: (0, i, 0))
    extra = () if got is None else (got,)
    return pl.pallas_call(
        functools.partial(wgrad_body, sets=sets, add=got is not None),
        grid_spec=pltpu.PrefetchScalarGridSpec(
            num_scalar_prefetch=1,
            grid=(steps,),
            in_specs=[pl.BlockSpec((rows, td), lambda i, pos: (0, i + pos[0] * steps))] * sets
            + [full((rows, cols))] * sets
            + [full((rows, 1))] * sets
            + [out_spec] * len(extra),
            out_specs=out_spec,
            scratch_shapes=[pltpu.VMEM((sets, M, rows, cols), bf16)],
        ),
        out_shape=jax.ShapeDtypeStruct((M, width // 2, cols), bf16),
        cost_estimate=cost(sets * M * rows * width * cols, sets * (rows * width + 2 * rows * cols) + 2 * M * width * cols),
        name=name,
    )(half, *xs, *gs, *mods, *extra)


def rows_wgrad_body(pos_ref, xt_ref, g_ref, modl_ref, *rest, groups):
    outs = rest[len(rest) - len(groups) :]
    xt = xt_ref[...]
    for n, group in enumerate(groups):
        for k, m in enumerate(group):
            total = contract(jnp.where(modl_ref[...] == m, xt, jnp.zeros_like(xt)), g_ref[...], 1, 0)
            if len(rest) > len(groups):
                total = total + rest[n][k].astype(f32)
            outs[n][k] = total.astype(bf16)


def rows_wgrad(half, xt, g, modl, got, groups, name):
    width, rows = xt.shape
    cols = g.shape[1]
    tn = 512
    out_specs = [pl.BlockSpec((len(group), width // 2, tn), lambda i, pos: (0, 0, i)) for group in groups]
    return pl.pallas_call(
        functools.partial(rows_wgrad_body, groups=groups),
        grid_spec=pltpu.PrefetchScalarGridSpec(
            num_scalar_prefetch=1,
            grid=(cols // tn,),
            in_specs=[
                pl.BlockSpec((width // 2, rows), lambda i, pos: (pos[0], 0)),
                pl.BlockSpec((rows, tn), lambda i, pos: (0, i)),
                pl.BlockSpec((1, rows), lambda i, pos: (0, 0)),
            ]
            + (out_specs if got else []),
            out_specs=out_specs,
        ),
        out_shape=[jax.ShapeDtypeStruct((len(group), width // 2, cols), bf16) for group in groups],
        cost_estimate=cost(M * rows * width * cols, rows * width + 2 * rows * cols + 2 * M * width * cols),
        name=name,
    )(half, xt, g, modl, *got)


UNROLL = 4


def spread(value, ref):
    for t in range(LANES):
        ref[t] = jnp.broadcast_to(value[:, t : t + 1], (16, LANES))


def fold_columns(ref):
    halves = []
    for h in range(2):
        groups = [
            fold_lanes([ref[8 * i + j, 8 * h : 8 * h + 8, :] for j in range(8)], (1, 2, 4)) for i in range(16)
        ]
        halves.append(fold_lanes(groups, (8, 16, 32, 64)))
    return jnp.concatenate(halves, axis=0)


def row_of(ref, t):
    wide = jnp.broadcast_to(ref[pl.ds(t, 1), :], (8, ref.shape[1]))
    return [wide[:, k * LANES : (k + 1) * LANES] for k in range(ref.shape[1] // LANES)]


def add_all(parts):
    while len(parts) > 1:
        parts = [functools.reduce(jnp.add, parts[k : k + 2]) for k in range(0, len(parts), 2)]
    return parts[0]


def state_vectors(pj_ref, rank):
    b = pj_ref[0, rank : rank + 16, :].astype(f32) + pj_ref[0, rank + 32 : rank + 48, :].astype(f32)
    c = pj_ref[0, rank + 16 : rank + 32, :].astype(f32) + pj_ref[0, rank + 48 : rank + 64, :].astype(f32)
    return b, c


def by_modality(mod, rows):
    return jnp.concatenate([jnp.where(mod == m, rows, jnp.zeros_like(rows)) for m in range(M)], axis=0)


def fold_all(ref):
    groups = [fold_rows([ref[8 * i + j] for j in range(8)]) for i in range(LANES // 8)]
    return jnp.concatenate(groups, axis=0)


def scan_fwd_body(pj_ref, act_ref, gate_ref, sp_ref, sb_ref, ld_ref, skip_ref, modc_ref, modr_ref,
                  delta_ref, sig_ref, gated_ref, scanned_ref, prev_ref, final_ref,
                  state, pre_s, d_s, u_s, r_s, b_s, c_s, yp_s):
    span, chans = act_ref.shape
    rank = pj_ref.shape[1] - 64
    tiles = chans // LANES

    @pl.when(pl.program_id(0) == 0)
    def _():
        state[...] = jnp.zeros_like(state)

    pre_s[...] = contract(by_modality(modr_ref[0], pj_ref[0, :rank, :]), sp_ref[...], 0, 0)
    r_s[...] = -jnp.exp(ld_ref[...]) * log2e
    b, c = state_vectors(pj_ref, rank)
    spread(b, b_s)
    spread(c, c_s)
    bias = [sb_ref[m : m + 1, :] for m in range(M)]

    pre = pre_s[...] + pick(modc_ref[...], bias)
    z = jnp.exp(-jnp.abs(pre))
    delta = (jnp.maximum(pre, 0.0) + jnp.log1p(z)).astype(bf16)
    delta_ref[...] = delta
    inv = 1.0 / (1.0 + z)
    sig_ref[...] = jnp.where(pre >= 0, inv, z * inv)
    act = act_ref[...].astype(f32)
    d = delta.astype(f32)
    d_s[...] = d
    u_s[...] = d * act

    def positions(i, carry):
        st = list(carry)
        for j in range(UNROLL):
            t = i * UNROLL + j
            at = pl.multiple_of(t * 16, 16)
            d_row, u_row = row_of(d_s, t), row_of(u_s, t)
            for k in range(tiles):
                cols = slice(k * LANES, (k + 1) * LANES)
                out = []
                for h in range(2):
                    n = 2 * k + h
                    rows = slice(8 * h, 8 * h + 8)
                    prev_ref[pl.ds(at + 8 * h, 8), cols] = st[n]
                    st[n] = jnp.exp2(d_row[k] * r_s[rows, cols]) * st[n] + u_row[k] * b_s[t, rows, :]
                    out.append(st[n] * c_s[t, rows, :])
                yp_s[t, :, cols] = out[0] + out[1]
        return tuple(st)

    first = tuple(
        state[8 * h : 8 * h + 8, k * LANES : (k + 1) * LANES] for k in range(tiles) for h in range(2)
    )
    st = lax.fori_loop(0, span // UNROLL, positions, first)
    for k in range(tiles):
        for h in range(2):
            state[8 * h : 8 * h + 8, k * LANES : (k + 1) * LANES] = st[2 * k + h]
    final_ref[...] = state[...]
    scanned = fold_all(yp_s) + skip_ref[...] * act
    scanned_ref[...] = scanned
    gate = gate_ref[...].astype(f32)
    gated_ref[...] = (scanned * (gate * sigmoid(gate))).astype(bf16)


def scan_forward(pj, act, gate, step_proj, step_bias, log_decay, skip, modc, modr):
    rows, chans = act.shape
    blocks = rows // LANES
    row = pl.BlockSpec((LANES, chans), lambda i: (i, 0))
    full = lambda shape: pl.BlockSpec(shape, lambda i: (0,) * len(shape))
    return pl.pallas_call(
        scan_fwd_body,
        grid=(blocks,),
        in_specs=[
            pl.BlockSpec((1,) + pj.shape[1:], lambda i: (i, 0, 0)),
            row, row,
            full(step_proj.shape),
            full((M, chans)),
            full((16, chans)),
            full((1, chans)),
            pl.BlockSpec((LANES, 1), lambda i: (i, 0)),
            pl.BlockSpec((1, 1, LANES), lambda i: (i, 0, 0)),
        ],
        out_specs=[
            row, row, row, row,
            pl.BlockSpec((LANES * 16, chans), lambda i: (i, 0)),
            full((16, chans)),
        ],
        out_shape=[
            jax.ShapeDtypeStruct((rows, chans), bf16),
            jax.ShapeDtypeStruct((rows, chans), f32),
            jax.ShapeDtypeStruct((rows, chans), bf16),
            jax.ShapeDtypeStruct((rows, chans), f32),
            jax.ShapeDtypeStruct((rows * 16, chans), f32),
            jax.ShapeDtypeStruct((16, chans), f32),
        ],
        scratch_shapes=[pltpu.VMEM((16, chans), f32)] + [pltpu.VMEM((LANES, chans), f32)] * 3
        + [pltpu.VMEM((16, chans), f32)]
        + [pltpu.VMEM((LANES, 16, LANES), f32)] * 2
        + [pltpu.VMEM((LANES, 8, chans), f32)],
        cost_estimate=cost(40e9, 64 * rows * chans + 20 * rows * chans),
        name="scan_forward",
    )(pj, act, gate, step_proj, step_bias, log_decay, skip, modc, modr)


def scan_bwd_body(pj_ref, act_ref, gate_ref, gg_ref, delta_ref, sig_ref, prev_ref, final_ref,
                  sp_ref, ld_ref, skip_ref, modc_ref, modr_ref,
                  gas_ref, gpt_ref, glogd_ref, gskip_ref, gbias_ref, gstep_ref,
                  carry_w, acc, later, d_s, u_s, gs_s, r_s, b_s, c_s, gp_s, hp_s, p_s, q_s):
    span, chans = act_ref.shape
    rank = pj_ref.shape[1] - 64
    tiles = chans // LANES

    @pl.when(pl.program_id(0) == 0)
    def _():
        carry_w[...] = jnp.zeros_like(carry_w)
        acc[...] = jnp.zeros_like(acc)
        later[...] = final_ref[...]
        gskip_ref[...] = jnp.zeros_like(gskip_ref)
        gbias_ref[...] = jnp.zeros_like(gbias_ref)
        gstep_ref[...] = jnp.zeros_like(gstep_ref)

    rates = -jnp.exp(ld_ref[...])
    r_s[...] = rates * log2e
    b, c = state_vectors(pj_ref, rank)
    spread(b, b_s)
    spread(c, c_s)

    act = act_ref[...].astype(f32)
    d = delta_ref[...].astype(f32)
    gate = gate_ref[...].astype(f32)
    gs = gg_ref[...].astype(f32) * (gate * sigmoid(gate))
    d_s[...] = d
    u_s[...] = d * act
    gs_s[...] = gs

    def positions(i, carry):
        w, total = list(carry[0]), list(carry[1])
        for j in range(UNROLL):
            t = span - 1 - (i * UNROLL + j)
            at = pl.multiple_of(t * 16, 16)
            grad = []
            d_row, u_row, gs_row = row_of(d_s, t), row_of(u_s, t), row_of(gs_s, t)
            for k in range(tiles):
                cols = slice(k * LANES, (k + 1) * LANES)
                gl, hl = [], []
                for h in range(2):
                    n = 2 * k + h
                    rows = slice(8 * h, 8 * h + 8)
                    rate = r_s[rows, cols]
                    adj = gs_row[k] * c_s[t, rows, :] + w[n]
                    gl.append(adj * b_s[t, rows, :])
                    w[n] = jnp.exp2(d_row[k] * rate) * adj
                    q = w[n] * prev_ref[pl.ds(at + 8 * h, 8), cols]
                    hl.append(q * rate)
                    total[n] = total[n] + q * d_row[k]
                    grad.append(adj * u_row[k])
                gp_s[t, :, cols] = gl[0] + gl[1]
                hp_s[t, :, cols] = hl[0] + hl[1]
            p_s[t, 0:8, :] = add_all(grad[0::2])
            p_s[t, 8:16, :] = add_all(grad[1::2])
        return tuple(w), tuple(total)

    places = [(slice(8 * h, 8 * h + 8), slice(k * LANES, (k + 1) * LANES)) for k in range(tiles) for h in range(2)]
    def read_grad(t, state):
        gs_row = row_of(gs_s, t)
        for h in range(2):
            rows = slice(8 * h, 8 * h + 8)
            q_s[t, rows, :] = add_all(
                [state(h)[:, k * LANES : (k + 1) * LANES] * gs_row[k] for k in range(tiles)]
            )

    def reads(i, _):
        for j in range(UNROLL):
            t = i * UNROLL + j
            at = pl.multiple_of(jnp.minimum(t + 1, span - 1) * 16, 16)
            read_grad(t, lambda h: prev_ref[pl.ds(at + 8 * h, 8), :])
        return 0

    lax.fori_loop(0, span // UNROLL, reads, 0)
    read_grad(span - 1, lambda h: later[8 * h : 8 * h + 8, :])
    later[...] = prev_ref[0:16, :]

    @pl.when(pl.program_id(0) >= 0)
    def _():
        gpt_ref[0, rank + 16 : rank + 32, :] = fold_columns(q_s).astype(bf16)

    held = (carry_w, acc)
    results = lax.fori_loop(
        0, span // UNROLL, positions, tuple(tuple(ref[at] for at in places) for ref in held)
    )
    for ref, values in zip(held, results):
        for n, at in enumerate(places):
            ref[at] = values[n]
    gb = fold_columns(p_s)
    g = fold_all(gp_s)
    gas_ref[...] = (g * d + skip_ref[...] * gs).astype(bf16)
    gpre = (act * g + fold_all(hp_s) * (1.0 / log2e)).astype(bf16).astype(f32) * sig_ref[...]
    glin = gpre.astype(bf16)
    mc = modc_ref[...]
    gbias_ref[...] += jnp.concatenate(
        [jnp.sum(jnp.where(mc == m, gpre, 0.0), axis=0, keepdims=True) for m in range(M)], axis=0
    )
    gskip_ref[...] += jnp.sum(gs * act, axis=0, keepdims=True)
    mr = modr_ref[0]
    gstep_ref[...] += contract(by_modality(mr, pj_ref[0, :rank, :]), glin, 1, 0)
    lin = contract(sp_ref[...], glin, 1, 1)
    gpt_ref[0, :rank, :] = pick(mr, [lin[m * rank : (m + 1) * rank] for m in range(M)]).astype(bf16)
    gpt_ref[0, rank : rank + 16, :] = gb.astype(bf16)
    glogd_ref[...] = acc[...] * rates


def scan_backward(pj, act, gate, gg, delta, sig, prev, final, step_proj, log_decay, skip, modc, modr):
    rows, chans = act.shape
    blocks = rows // LANES
    rank = step_proj.shape[0] // M
    last = blocks - 1
    row = pl.BlockSpec((LANES, chans), lambda i: (last - i, 0))
    full = lambda shape: pl.BlockSpec(shape, lambda i: (0,) * len(shape))
    slab = lambda shape: pl.BlockSpec((1,) + shape, lambda i: (last - i, 0, 0))
    return pl.pallas_call(
        scan_bwd_body,
        grid=(blocks,),
        in_specs=[
            slab(pj.shape[1:]),
            row, row, row, row, row,
            pl.BlockSpec((LANES * 16, chans), lambda i: (last - i, 0)),
            full((16, chans)),
            full(step_proj.shape),
            full((16, chans)),
            full((1, chans)),
            pl.BlockSpec((LANES, 1), lambda i: (last - i, 0)),
            slab((1, LANES)),
        ],
        out_specs=[
            row,
            slab((rank + 32, LANES)),
            full((16, chans)),
            full((1, chans)),
            full((M, chans)),
            full(step_proj.shape),
        ],
        out_shape=[
            jax.ShapeDtypeStruct((rows, chans), bf16),
            jax.ShapeDtypeStruct((blocks, rank + 32, LANES), bf16),
            jax.ShapeDtypeStruct((16, chans), f32),
            jax.ShapeDtypeStruct((1, chans), f32),
            jax.ShapeDtypeStruct((M, chans), f32),
            jax.ShapeDtypeStruct(step_proj.shape, f32),
        ],
        scratch_shapes=[pltpu.VMEM((16, chans), f32)] * 3
        + [pltpu.VMEM((LANES, chans), f32)] * 3
        + [pltpu.VMEM((16, chans), f32)]
        + [pltpu.VMEM((LANES, 16, LANES), f32)] * 2
        + [pltpu.VMEM((LANES, 8, chans), f32)] * 2
        + [pltpu.VMEM((LANES, 16, LANES), f32)] * 2,
        cost_estimate=cost(60e9, 64 * rows * chans + 20 * rows * chans),
        name="scan_backward",
    )(pj, act, gate, gg, delta, sig, prev, final, step_proj, log_decay, skip, modc, modr)


def conv_bwd_body(gp_ref, sp_ref, gas_ref, ci_ref, act_ref, cw_ref, cb_ref, modc_ref, modr_ref,
                  gci_ref, gstate_ref, gcw_ref, pad, tail, *, rows):
    cols = pad.shape[1]
    pad[0:8, :] = jnp.zeros((8, cols), f32)
    tail[rows : rows + 8, :] = jnp.zeros((8, cols), f32)
    gstate_ref[...] = jnp.zeros_like(gstate_ref)
    taps = cw_ref[...]
    base = cb_ref[...]

    def first(r, sums):
        at = pl.multiple_of(r * LANES, LANES)
        here = pl.ds(at, LANES)
        pad[pl.ds(at + 8, LANES), :] = ci_ref[here, :].astype(f32)
        v = pad[pl.ds(at, LANES + 8), :]
        shifted = [v[5 + k : 5 + k + LANES, :] for k in range(4)]
        s = base
        for k in range(4):
            s = s + taps[k : k + 1, :] * shifted[k]
        sg = sigmoid(s)
        gp = gp_ref[r]
        ga = pick(modc_ref[here, :], [contract(gp, sp_ref[m], 0, 0) for m in range(M)])
        gcp = (ga + gas_ref[here, :].astype(f32)) * (sg * (1.0 + s * (1.0 - sg)))
        tail[here, :] = gcp
        act = act_ref[here, :]
        mr = modr_ref[r]
        for m in range(M):
            gstate_ref[m] += contract(jnp.where(mr == m, gp, jnp.zeros_like(gp)), act, 1, 0)
        terms = [gcp * part for part in shifted] + [gcp]
        return tuple(
            total + jnp.sum(term.reshape(LANES // 8, 8, cols), axis=0) for total, term in zip(sums, terms)
        )

    sums = lax.fori_loop(0, rows // LANES, first, (jnp.zeros((8, cols), f32),) * 5)
    gcw_ref[...] = jnp.concatenate(
        [jnp.sum(total, axis=0, keepdims=True) for total in sums] + [jnp.zeros((3, cols), f32)], axis=0
    )

    def second(r, _):
        at = pl.multiple_of(r * LANES, LANES)
        v = tail[pl.ds(at, LANES + 8), :]
        s = taps[0:1, :] * v[3 : 3 + LANES, :]
        for k in range(1, 4):
            s = s + taps[k : k + 1, :] * v[3 - k : 3 - k + LANES, :]
        gci_ref[pl.ds(at, LANES), :] = s.astype(bf16)
        return 0

    lax.fori_loop(0, rows // LANES, second, 0)


def conv_backward(gp, sp, gas, ci, act, cw, cb, modc, modr):
    rows, chans = ci.shape
    psize = sp.shape[1]
    tc = min(256, chans)
    col = lambda r: pl.BlockSpec((r, tc), lambda j: (0, j))
    full = lambda shape: pl.BlockSpec(shape, lambda j: (0,) * len(shape))
    wide = pl.BlockSpec((M, psize, tc), lambda j: (0, 0, j))
    return pl.pallas_call(
        functools.partial(conv_bwd_body, rows=rows),
        grid=(chans // tc,),
        in_specs=[full(gp.shape), wide, col(rows), col(rows), col(rows), col(4), col(1), full((rows, 1)), full(modr.shape)],
        out_specs=[col(rows), wide, col(8)],
        out_shape=[
            jax.ShapeDtypeStruct((rows, chans), bf16),
            jax.ShapeDtypeStruct((M, psize, chans), f32),
            jax.ShapeDtypeStruct((8, chans), f32),
        ],
        scratch_shapes=[pltpu.VMEM((rows + 8, tc), f32), pltpu.VMEM((rows + 8, tc), f32)],
        cost_estimate=cost(8 * M * rows * psize * chans, 10 * rows * chans),
        name="conv_backward",
    )(gp, sp, gas, ci, act, cw, cb, modc, modr)


def interleave_body(pos_ref, conv_ref, gate_ref, *rest, group):
    o_ref = rest[-1]
    sub = lax.broadcasted_iota(jnp.int32, (8, LANES), 0)

    def step(r, _):
        at = pl.multiple_of(r * group, group)
        sources = [ref[0, pl.ds(at, group), :].astype(f32) for ref in (conv_ref, gate_ref)]
        for h in range(group // 8):
            vs = [
                source[8 * h : 8 * h + 8, k * LANES : (k + 1) * LANES] for k in range(4) for source in sources
            ]
            for shift in (1, 2, 4):
                mask = (sub & shift) == 0
                swapped = list(vs)
                for j in range(8):
                    if j & shift == 0:
                        a, b = vs[j], vs[j | shift]
                        swapped[j] = jnp.where(mask, a, pltpu.roll(b, shift, 0))
                        swapped[j | shift] = jnp.where(mask, pltpu.roll(a, 8 - shift, 0), b)
                vs = swapped
            for d in range(8):
                o_ref[0, pl.ds((at + 8 * h + d) * 8, 8), :] = vs[d]
        return 0

    lax.fori_loop(0, conv_ref.shape[1] // group, step, 0)


def split_body(pos_ref, conv_ref, gate_ref, *rest):
    o_ref = rest[-1]
    o_ref[0, :, 0, :] = conv_ref[0].astype(f32)
    o_ref[0, :, 1, :] = gate_ref[0].astype(f32)


def place_input_grad(half, conv, gate, target):
    _, height, chans = conv.shape
    td = min(512, height)
    steps = height // td
    packed = chans == 4 * LANES
    if packed:
        shape, block = (M, 2 * height * 8, LANES), (1, td * 8, LANES)
        where = lambda m, i, pos: (m, i + pos[0] * steps, 0)
        body = functools.partial(interleave_body, group=64)
    else:
        shape, block = (M, 2 * height, 2, chans), (1, td, 2, chans)
        where = lambda m, i, pos: (m, i + pos[0] * steps, 0, 0)
        body = split_body
    source = pl.BlockSpec((1, td, chans), lambda m, i, pos: (m, i, 0))
    extra = () if target is None else (target,)
    return pl.pallas_call(
        body,
        grid_spec=pltpu.PrefetchScalarGridSpec(
            num_scalar_prefetch=1,
            grid=(M, steps),
            in_specs=[source, source] + [pl.BlockSpec(memory_space=pl.ANY)] * len(extra),
            out_specs=pl.BlockSpec(block, where),
        ),
        out_shape=jax.ShapeDtypeStruct(shape, f32),
        input_output_aliases={} if target is None else {3: 0},
        cost_estimate=cost(0, 12 * M * height * chans),
        name="place_input_grad",
    )(half, conv, gate, *extra)


def input_grad_layout(value, width, chans):
    if value.ndim == 4:
        return value
    return value.reshape(M, width, chans // LANES, 2, LANES).transpose(0, 1, 3, 2, 4).reshape(M, width, 2, chans)


def join_body(pos_ref, mine_ref, got_ref, o_ref):
    mine = pl.program_id(1) == pos_ref[0]

    @pl.when(mine)
    def _():
        o_ref[0] = mine_ref[0].astype(f32)

    @pl.when(jnp.logical_not(mine))
    def _():
        o_ref[0] = got_ref[0].astype(f32)


def join_halves(core, mine, got):
    _, height, cols = mine.shape
    part = pl.BlockSpec((1, height, cols), lambda m, i, pos: (m, 0, 0))
    return pl.pallas_call(
        join_body,
        grid_spec=pltpu.PrefetchScalarGridSpec(
            num_scalar_prefetch=1,
            grid=(M, 2),
            in_specs=[part, part],
            out_specs=pl.BlockSpec((1, height, cols), lambda m, i, pos: (m, i, 0)),
        ),
        out_shape=jax.ShapeDtypeStruct((M, 2 * height, cols), f32),
        cost_estimate=cost(0, 12 * M * height * cols),
        name="join_halves",
    )(core, mine, got)


def after(value, *others):
    return lax.optimization_barrier((value,) + others)[0]


def swap_core(value):
    count = lax.axis_size("batch")
    return lax.ppermute(value, "batch", [(i, i ^ 1) for i in range(count)])


def y_others(value):
    count = lax.axis_size("batch")
    return [
        lax.ppermute(value, "batch", [(i, (i + shift) % count) for i in range(count)]) for shift in range(2, count, 2)
    ]


def y_sum(value, *before):
    others = [after(other, *before) for other in y_others(value)]
    if len(others) == 1:
        return value.astype(f32) + others[0].astype(f32)
    chips = len(others) + 1
    mine = lax.axis_index("batch") // 2
    buffer = jnp.zeros((chips,) + value.shape, value.dtype)
    for shift, piece in enumerate([value] + others):
        buffer = lax.dynamic_update_index_in_dim(buffer, piece, (mine + chips - shift) % chips, 0)
    return jnp.sum(buffer.astype(f32), axis=0)


def rounded(value):
    return lax.reduce_precision(value, 8, 7)


def batch_total(value, first, second):
    value = value + after(swap_core(value), first)
    return y_sum(value, second)


def batch_total_rounded(value, first, second):
    value = rounded(value)
    value = rounded(value + after(swap_core(value.astype(bf16)), first).astype(f32))
    total = value
    for other in y_others(value.astype(bf16)):
        total = total + after(other, second).astype(f32)
    return total


def to_owners(pieces):
    return lax.all_to_all(pieces, "own", split_axis=0, concat_axis=0, tiled=False)


def to_all(piece):
    return to_owners(jnp.broadcast_to(piece[None], (lax.axis_size("own"),) + piece.shape))


def gather_small(piece, *before):
    count = lax.axis_size("own")
    mine = lax.axis_index("own")
    held = piece[None]
    bit = 1
    while bit < count:
        got = lax.ppermute(held, "own", [(i, i ^ bit) for i in range(count)])
        got = after(got, before[0])
        before = before[1:] or before
        low = (mine & bit) == 0
        held = jnp.concatenate([jnp.where(low, held, got), jnp.where(low, got, held)], axis=0)
        bit *= 2
    return held


def per_device(
    hidden_in, norm_gain, input_proj, conv_weight, conv_bias, state_proj, step_proj, step_bias,
    log_decay, skip_gain, output_proj, modality, grad_out,
):
    own_count = lax.axis_size("own")
    own_index = lax.axis_index("own")
    core = lax.axis_index("batch") % 2
    width = hidden_in.shape[2]
    rows = modality.shape[1]
    span = rows // own_count
    chans = input_proj.shape[3]
    rank = step_proj.shape[1]
    states = log_decay.shape[0]
    psize = state_proj.shape[2]
    chan_at = own_index * chans

    core_at = core.astype(jnp.int32).reshape(1)
    other_at = (1 - core).astype(jnp.int32).reshape(1)

    modc = modality.reshape(rows, 1)
    modl = modality.reshape(1, rows)
    modr = modality.reshape(rows // LANES, 1, LANES)
    w_in = input_proj.reshape(M, width, 2 * chans)
    sp_t = jnp.swapaxes(state_proj, 1, 2)
    step_rows = step_proj.reshape(M * rank, chans)
    part = lambda table: lax.dynamic_slice_in_dim(table, chan_at, chans, table.ndim - 1)
    cw = part(conv_weight)
    cb = part(conv_bias).reshape(1, chans)
    decay = part(log_decay)
    skip = part(skip_gain).reshape(1, chans)

    resid = hidden_in[0].astype(f32)
    inverse = lax.rsqrt(jnp.mean(resid * resid, axis=-1, keepdims=True) + epsilon)
    normed = (resid * inverse * norm_gain).astype(bf16)
    mod_others, normed_others = y_others(modality), y_others(normed)
    x = lax.all_gather(normed, "own", axis=0, tiled=True)
    cot = lax.all_gather(after(grad_out[0], x, w_in, *mod_others, *normed_others), "own", axis=0, tiled=True)

    conv_in, gate, act, proj_part = input_stage(x, w_in, cw, cb, sp_t, modc, modr)
    modcs = [modc] + [other.reshape(rows, 1) for other in mod_others]
    blocks = rows // LANES
    per_owner = blocks // own_count
    pieces = proj_part.reshape(own_count, per_owner * psize, LANES)
    proj = jnp.sum(to_owners(pieces).astype(f32), axis=0).reshape(per_owner, psize, LANES)
    high = proj.astype(bf16)
    low = (proj[:, rank:] - high[:, rank:].astype(f32)).astype(bf16)
    packed = jnp.concatenate([high, low], axis=1)
    pj = to_all(packed).reshape(blocks, psize + 2 * states, LANES)
    xs = [x] + [lax.all_gather(after(other, pj), "own", axis=0, tiled=True) for other in normed_others]
    delta, sig, gated, scanned, prev, final = scan_forward(
        pj, act, gate, step_rows, step_bias, decay, skip, modc, modr
    )
    gg, ggate = gated_grads(cot, output_proj, modc, scanned, gate)
    ggates = [ggate] + y_others(ggate)
    branch_part = select_matmul(gated, output_proj, modc, False, bf16, "output_stage")
    branch = lax.psum_scatter(branch_part, "own", scatter_dimension=0, tiled=True)
    block_out = (resid + branch.astype(f32)).astype(bf16)[None]

    gated_t = jnp.swapaxes(gated, 0, 1)
    groups = ((0,), (1, 2))
    out_got = [
        swap_core(value) for value in rows_wgrad(other_at, gated_t, cot, modl, [], groups, "output_wgrad_send")
    ]
    out_half = rows_wgrad(core_at, gated_t, cot, modl, out_got, groups, "output_wgrad_keep")
    out_total = [y_sum(out_half[0]).astype(bf16)]

    gas, gpt, glogd, gskip, gbias, gstep = scan_backward(
        after(pj, branch_part, *out_half), act, gate, gg, delta, sig, prev, final, step_rows, decay, skip, modc, modr
    )
    gpt = after(gpt, out_total[0])
    gp_own = jnp.sum(to_owners(gpt.reshape(own_count, per_owner * psize, LANES)).astype(f32), axis=0).astype(bf16)
    gp = to_all(gp_own).reshape(blocks, psize, LANES)

    ggates = [ggate] + [after(other, gp_own) for other in ggates[1:]]
    gate_send = half_wgrad(other_at, xs, ggates, modcs, None, "gate_wgrad_send")
    gate_got = swap_core(gate_send)

    gp = after(gp, gate_send)
    gci, gstate, gcw = conv_backward(gp, sp_t, gas, conv_in, act, cw, cb, modc, modr)
    others = y_others(gci)
    gnormed, gain_part = input_dgrad(gci, ggate, w_in, modc, x, norm_gain.reshape(1, width))

    gcis = [gci] + [after(other, gnormed) for other in others]
    gnormed = to_owners(after(gnormed, *others).reshape(own_count, span, width))
    conv_send = half_wgrad(other_at, xs, gcis, modcs, None, "conv_wgrad_send")
    gate_mine = half_wgrad(core_at, xs, ggates, modcs, after(gate_got, conv_send, branch), "gate_wgrad_keep")
    gate_recv = swap_core(gate_mine)
    gain_rows = width // chans
    small = batch_total(
        jnp.concatenate([glogd, gcw[:5], gskip, gain_part.reshape(gain_rows, chans), gbias], axis=0),
        conv_send, gate_mine,
    )
    conv_got = after(swap_core(conv_send), gate_mine, small)
    conv_mine = half_wgrad(core_at, xs, gcis, modcs, conv_got, "conv_wgrad_keep")
    conv_recv = swap_core(conv_mine)
    half_placed = place_input_grad(core_at, conv_mine, gate_mine, None)
    grad_input = place_input_grad(other_at, conv_recv, gate_recv, half_placed)
    gnormed = after(gnormed, half_placed)
    out_total.append(y_sum(after(out_half[1], small), half_placed).astype(bf16))
    out_total = jnp.concatenate(out_total, axis=0)
    grad_output = join_halves(core_at, after(out_total, gnormed), swap_core(out_total))
    gnormed = jnp.sum(gnormed.astype(f32), axis=0)

    weighted = norm_gain * gnormed
    coupled = jnp.mean(resid * weighted, axis=-1, keepdims=True)
    grad_hidden = (
        grad_out[0].astype(f32) + inverse * weighted - resid * (inverse * inverse * inverse) * coupled
    )[None]

    weights = batch_total_rounded(
        jnp.concatenate([gstep, gstate.reshape(M * psize, chans)], axis=0), conv_send, grad_input
    )
    grad_step = weights[: M * rank].reshape(M, rank, chans)
    grad_state = jnp.swapaxes(weights[M * rank :].reshape(M, psize, chans), 1, 2)
    grad_bias = small[states + 6 + gain_rows :]
    wide = gather_small(small[: states + 6 + gain_rows], conv_mine, half_placed, grad_input)
    grad_gain = jnp.sum(wide[:, states + 6 :], axis=0).reshape(width)
    wide = jnp.swapaxes(wide[:, : states + 6], 0, 1).reshape(states + 6, own_count * chans)
    grad_input = input_grad_layout(grad_input, width, chans)
    return (
        block_out,
        grad_hidden,
        grad_gain,
        grad_input,
        wide[states : states + 4],
        wide[states + 4],
        grad_state,
        grad_step,
        grad_bias,
        wide[:states],
        wide[states + 5],
        grad_output,
    )


def solution(mesh):
    placed = (
        P("batch", "own", None),
        P(),
        P(None, None, None, "own"),
        P(),
        P(),
        P(None, "own", None),
        P(None, None, "own"),
        P(None, "own"),
        P(),
        P(),
        P(None, "own", None),
        P("batch", None),
        P("batch", "own", None),
    )
    return jax.shard_map(
        per_device,
        mesh=mesh,
        in_specs=placed,
        out_specs=(
            P("batch", "own", None),
            P("batch", "own", None),
            P(),
            P(None, None, None, "own"),
            P(),
            P(),
            P(None, "own", None),
            P(None, None, "own"),
            P(None, "own"),
            P(),
            P(),
            P(None, "own", None),
        ),
        check_vma=False,
    )
```

time: 739 us -> 511 us (0.69)
  waiting for transfers between devices: 280 us -> 100 us
  blocking collectives: 0 us -> 48.8 us
  other arithmetic: 64 us -> 22.1 us
  local copies, waits for them, and re-layouts: 65.9 us -> 40.3 us
  Pallas kernels: 275 us -> 253 us
  starting transfers between devices: 37.2 us -> 29.6 us
    ppermute x6 -> x11, waiting for transfers between devices: 167 us -> 29.5 us  [the longest x8 20.1 us: y_others(): lax.ppermute(value, 'batch', [(i, (i + shift) % count) for i in range(cou...]
    all_to_all x0 -> x2, blocking collectives: none -> 48.8 us  [to_owners(): lax.all_to_all(pieces, 'own', split_axis=0, concat_axis=0, tiled=False)]
    convert_element_type x11 -> x4, other arithmetic: 46.2 us -> 6.61 us  [the longest x1 3 us: per_device(): out_total.append(y_sum(after(out_half[1], small), half_placed).astype(bf16))]
    pallas_call x1, Pallas kernels: 58.5 us -> 26 us  [scan_forward(): pl.pallas_call(scan_fwd_body, grid=(blocks,), in_specs=[pl.BlockSpec((1,)...]
    all_to_all x7 -> x3, waiting for transfers between devices: 33.6 us -> 9.16 us  [to_owners(): lax.all_to_all(pieces, 'own', split_axis=0, concat_axis=0, tiled=False)]
    all_gather x1 -> x2, waiting for transfers between devices: 22.4 us -> 0.02 us  [the longest x1 0.02 us: per_device(): lax.all_gather(after(other, pj), 'own', axis=0, tiled=True)]
    pallas_call x11 -> x13, Pallas kernels: 143 us -> 164 us  [the longest x4 50.7 us: half_wgrad(): pl.pallas_call(functools.partial(wgrad_body, sets=sets, add=got is not No...]
    all_to_all x7 -> x3, starting transfers between devices: 29.8 us -> 13 us  [to_owners(): lax.all_to_all(pieces, 'own', split_axis=0, concat_axis=0, tiled=False)]
  transfers between devices with their start and end apart: 26 -> 27, of which waited for: 10 -> 8; matrix products, arithmetic and copies ran while one was open for 15% -> 11% of each run, Pallas kernels for 27% -> 48%
where the time goes in v2:
time: 511 us; the launch traced here: 508 us
  Pallas kernels  253 us (50%)
  waiting for transfers between devices  100 us (20%)
  blocking collectives  48.8 us (10%)
  local copies, waits for them, and re-layouts  40.3 us (8%)
  starting transfers between devices  29.6 us (6%)
  other arithmetic  22.1 us (4%)
  between operations  14.2 us (3%)
    all_gather x1, waiting for transfers between devices, per_device(): x = lax.all_gather(normed, 'own', axis=0, tiled=True)  52.1 us
    pallas_call x1, Pallas kernels, scan_backward(): pl.pallas_call(scan_bwd_body, grid=(blocks,), in_specs=[slab(pj.shape[1:]...  52.1 us
    pallas_call x4, Pallas kernels, half_wgrad(): pl.pallas_call(functools.partial(wgrad_body, sets=sets, add=got is not No...  50.7 us
    all_to_all x2, blocking collectives, to_owners(): lax.all_to_all(pieces, 'own', split_axis=0, concat_axis=0, tiled=False)  48.8 us
    pallas_call x1, Pallas kernels, input_stage(): pl.pallas_call(functools.partial(in_body, rows=rows, block=min(256, rows)...  27.1 us
    pallas_call x1, Pallas kernels, scan_forward(): pl.pallas_call(scan_fwd_body, grid=(blocks,), in_specs=[pl.BlockSpec((1,)...  26 us
    reshape x1, local copies, waits for them, and re-layouts, per_device(): w_in = input_proj.reshape(M, width, 2 * chans)  20.9 us
    ppermute x8, waiting for transfers between devices, y_others(): lax.ppermute(value, 'batch', [(i, (i + shift) % count) for i in range(cou...  20.1 us
  transfers between devices with their start and end apart: 27, of which 8 were waited for; matrix products, arithmetic and copies ran while one was open for 11% of the time, Pallas kernels for 48%

profile of v2, /device:TPU:0, one launch (start us, length us, event | category | flops | bytes accessed | tf_op | source)
XLA Modules:
  0.0 508.5 jit_solution(369115575319961231)
XLA Ops:
  7.3 1.2 fusion.5
  9.6 2.0 fusion.7
  11.7 3.0 collective-permute-start.1
  14.8 20.9 %reshape.183.wc_ref.wg_ref.w_ref = bf16[3,2048,1024]{2,1,0:T(8,128)(2,1)} reshape(bf16[3,2048,2,512]{3,2,1,0:T(2,128)(2,1)} %param.15) | data formatting | bytes 25165824 | tf_op jit(solution)/shard_map/reshape | solution.py:901
  35.8 52.1 %all-gather.4.cloned.1.call-done.x_ref.refs_1_ = bf16[1024,2048]{1,0:T(8,128)(2,1)} async-done(((bf16[128,2048]{1,0:T(8,128)(2,1)}), bf16[1024,2048]{1,0:T(8,128)(2,1)}) %all-gather.4.cloned.1.call-update) | async-done | bytes 4194320 | tf_op jit(solution)/shard_map/all_gather | solution.py:914
  88.0 1.0 copy.46.modc_ref.refs_5_
  89.0 1.3 dynamic_slice.13
  90.3 1.3 constant_dynamic-slice_fusion.1.cw_ref
  91.6 27.1 %input_stage.1 = (bf16[1024,512]{1,0:T(8,128)(2,1)}, bf16[1024,512]{1,0:T(8,128)(2,1)}, bf16[1024,512]{1,0:T(8,128)(2,1)}, bf16[8,160,128]{2,1,0:T(8,128)(2,1)}) custom-call(bf16[1024,2048]{1,0:T(8,128)(2,1)} %all-gather.4.cloned.1.call-done.x_ref.refs_1_, bf16[3,2048,1024]{2,1,0:T(8,128)(2,1)} %reshape.183.wc_ref.wg_ref.w_ref, ...), custom_call_target="tpu_custom_call" | custom-call | flops 12884901888 | bytes 16777216 | tf_op jit(solution)/shard_map/input_stage/pallas_call | solution.py:112
  118.7 22.8 %all_to_all.25 = bf16[8,160,128]{2,1,0:T(8,128)(2,1)S(1)} all-to-all(bf16[8,160,128]{2,1,0:T(8,128)(2,1)} %get-tuple-element.60), channel_id=1, replica_groups=mesh['batch'=4,'own'=8] {'own'}, dimensions={0} | all-to-all | bytes 655360 | tf_op jit(solution)/shard_map/all_to_all | solution.py:857
  141.6 26.0 %all_to_all.26 = bf16[8,1,192,128]{3,2,1,0:T(8,128)(2,1)} all-to-all(bf16[8,1,192,128]{3,2,1,0:T(8,128)(2,1)S(1)} %broadcast_in_dim.13), channel_id=1, replica_groups=mesh['batch'=4,'own'=8] {'own'}, dimensions={0} | all-to-all | bytes 786432 | tf_op jit(solution)/shard_map/all_to_all | solution.py:857
  167.9 1.3 dynamic_slice.15
  169.9 26.0 %scan_forward.1 = (bf16[1024,512]{1,0:T(8,128)(2,1)}, f32[1024,512]{1,0:T(8,128)}, bf16[1024,512]{1,0:T(8,128)(2,1)}, f32[1024,512]{1,0:T(8,128)}, f32[16384,512]{1,0:T(8,128)}, /*index=5*/f32[16,512]{1,0:T(8,128)}) custom-call(bf16[8,192,128]{2,1,0:T(8,128)(2,1)} %bitcast.88, bf16[1024,512]{1,0:T(8,128)(2,1)} %get-tuple-element.61.act_ref, ...), custom_call_target="tpu_custom_call" | custom-call | flops 40000000000 | bytes 44040192 | tf_op jit(solution)/shard_map/scan_forward/pallas_call | solution.py:449
  195.9 2.3 copy.49
  198.2 6.7 %output_wgrad_send.1 = (bf16[1,256,2048]{2,1,0:T(8,128)(2,1)}, bf16[2,256,2048]{2,1,0:T(8,128)(2,1)}) custom-call(s32[1]{0:T(128)} %bitcast.14.pos_ref.refs_0_, bf16[512,1024]{1,0:T(8,128)(2,1)} %bitcast.83, bf16[1024,2048]{1,0:T(8,128)(2,1)} %all-gather.6.cloned.1.call-done.g_ref.x_ref, s32[1,1024]{1,0:T(1,128)} %modl_ref.3), custom_call_target="tpu_custom_call" | custom-call | flops 3221225472 | bytes 11010048 | tf_op jit(solution)/shard_map/output_wgrad_send/pallas_call | solution.py:320
  205.4 12.4 %output_stage.1 = bf16[1024,2048]{1,0:T(8,128)(2,1)} custom-call(bf16[1024,512]{1,0:T(8,128)(2,1)} %get-tuple-element.63.x_ref, bf16[3,512,2048]{2,1,0:T(8,128)(2,1)} %w_ref.3, s32[1024,1]{1,0:T(8,128)} %copy.46.modc_ref.refs_5_), custom_call_target="tpu_custom_call" | custom-call | flops 6442450944 | bytes 11534336 | tf_op jit(solution)/shard_map/output_stage/pallas_call | solution.py:160
  217.8 12.5 %gated_grads.1 = (bf16[1024,512]{1,0:T(8,128)(2,1)}, bf16[1024,512]{1,0:T(8,128)(2,1)}) custom-call(bf16[1024,2048]{1,0:T(8,128)(2,1)} %all-gather.6.cloned.1.call-done.g_ref.x_ref, bf16[3,512,2048]{2,1,0:T(8,128)(2,1)} %w_ref.3, s32[1024,1]{1,0:T(8,128)} %copy.46.modc_ref.refs_5_, f32[1024,512]{1,0:T(8,128)} %get-tuple-element.70.scanned_ref, ...), custom_call_target="tpu_custom_call" | custom-call | flops 6442450944 | bytes 15728640 | tf_op jit(solution)/shard_map/gated_grads/pallas_call | solution.py:196
  230.4 1.5 collective-permute-start.5
  231.9 1.3 copy-done.25
  233.2 7.3 %output_wgrad_keep.1 = (bf16[1,256,2048]{2,1,0:T(8,128)(2,1)}, bf16[2,256,2048]{2,1,0:T(8,128)(2,1)}) custom-call(s32[1]{0:T(128)} %bitcast.11.pos_ref.refs_0_, bf16[512,1024]{1,0:T(8,128)(2,1)} %bitcast.84, bf16[1024,2048]{1,0:T(8,128)(2,1)} %all-gather.6.cloned.1.call-done.g_ref.x_ref, s32[1,1024]{1,0:T(1,128)} %modl_ref.3, ...), custom_call_target="tpu_custom_call" | custom-call | flops 3221225472 | bytes 11010048 | tf_op jit(solution)/shard_map/output_wgrad_keep/pallas_call | solution.py:320
  241.1 52.1 %scan_backward.1 = (bf16[1024,512]{1,0:T(8,128)(2,1)}, bf16[8,160,128]{2,1,0:T(8,128)(2,1)}, f32[16,512]{1,0:T(8,128)}, f32[1,512]{1,0:T(1,128)}, f32[3,512]{1,0:T(4,128)}, /*index=5*/f32[384,512]{1,0:T(8,128)}) custom-call(bf16[8,192,128]{2,1,0:T(8,128)(2,1)} %bitcast.89, bf16[1024,512]{1,0:T(8,128)(2,1)} %get-tuple-element.61.act_ref, ...), custom_call_target="tpu_custom_call" | custom-call | flops 60000002048 | bytes 44040192 | tf_op jit(solution)/shard_map/scan_backward/pallas_call | solution.py:599
  293.2 1.4 add_convert_fusion.1
  294.6 3.4 all-to-all-start.2
  298.0 1.0 copy.53.refs_6_
  299.1 9.2 %all-to-all-done.2 = bf16[8,160,128]{2,1,0:T(8,128)(2,1)S(1)} async-done(((bf16[8,160,128]{2,1,0:T(8,128)(2,1)}), bf16[8,160,128]{2,1,0:T(8,128)(2,1)S(1)}, u32[]{:S(2)}, u32[]{:S(2)}) %all-to-all-start.2) | async-done | bytes 327712 | tf_op jit(solution)/shard_map/all_to_all | solution.py:857
  308.3 0.8 broadcast_in_dim.30
  309.0 3.7 all-to-all-start.3
  312.7 12.3 %gate_wgrad_send.1 = bf16[3,1024,512]{2,1,0:T(8,128)(2,1)} custom-call(s32[1]{0:T(128)} %bitcast.14.pos_ref.refs_0_, bf16[1024,2048]{1,0:T(8,128)(2,1)} %all-gather.4.cloned.1.call-done.x_ref.refs_1_, bf16[1024,2048]{1,0:T(8,128)(2,1)} %all-gather.8.cloned.1.call-done.refs_2_, bf16[1024,512]{1,0:T(8,128)(2,1)} %get-tuple-element.79.refs_3_.gg_ref, ...), custom_call_target="tpu_custom_call" | custom-call | flops 6442450944 | bytes 12582912 | tf_op jit(solution)/shard_map/gate_wgrad_send/pallas_call | solution.py:286
  325.1 0.8 copy-done.14
  325.8 11.5 %conv_backward.1 = (bf16[1024,512]{1,0:T(8,128)(2,1)}, f32[3,160,512]{2,1,0:T(8,128)}, f32[8,512]{1,0:T(8,128)}) custom-call(bf16[8,160,128]{2,1,0:T(8,128)(2,1)} %copy-done.14, bf16[3,160,512]{2,1,0:T(8,128)(2,1)} %bitcast.109, bf16[1024,512]{1,0:T(8,128)(2,1)} %get-tuple-element.82.gas_ref, bf16[1024,512]{1,0:T(8,128)(2,1)} %get-tuple-element.83.ci_ref, ...), custom_call_target="tpu_custom_call" | custom-call | flops 2013265920 | bytes 5242880 | tf_op jit(solution)/shard_map/conv_backward/pallas_call | solution.py:696
  337.4 1.5 collective-permute-start.6
  338.8 18.3 %input_dgrad.1 = (bf16[1024,2048]{1,0:T(8,128)(2,1)}, f32[1,2048]{1,0:T(1,128)}) custom-call(bf16[1024,512]{1,0:T(8,128)(2,1)} %get-tuple-element.84.gc_ref.refs_3_, bf16[1024,512]{1,0:T(8,128)(2,1)} %get-tuple-element.79.refs_3_.gg_ref, bf16[3,2048,1024]{2,1,0:T(8,128)(2,1)} %reshape.183.wc_ref.wg_ref.w_ref, s32[1024,1]{1,0:T(8,128)} %copy.46.modc_ref.refs_5_, ...), custom_call_target="tpu_custom_call" | custom-call | flops 12884901888 | bytes 23068672 | tf_op jit(solution)/shard_map/input_dgrad/pallas_call | solution.py:235
  357.1 6.1 %collective-permute-done.6.refs_4_ = bf16[1024,512]{1,0:T(8,128)(2,1)S(1)} collective-permute-done((bf16[1024,512]{1,0:T(8,128)(2,1)}, bf16[1024,512]{1,0:T(8,128)(2,1)S(1)}, u32[]{:S(2)}, u32[]{:S(2)}) %collective-permute-start.6) | collective-permute-done | bytes 1048608 | tf_op jit(solution)/shard_map/ppermute | solution.py:822
  363.2 1.0 copy-done.26
  364.2 5.9 %all-to-all-start.4 = ((bf16[8,128,2048]{2,1,0:T(8,128)(2,1)}), bf16[8,128,2048]{2,1,0:T(8,128)(2,1)}, u32[]{:S(2)}, u32[]{:S(2)}) async-start(bf16[8,128,2048]{2,1,0:T(8,128)(2,1)} %bitcast.81), calls=%async_computation.5 | async-start | bytes 8388608 | tf_op jit(solution)/shard_map/all_to_all | solution.py:857
  370.1 12.3 %conv_wgrad_send.1 = bf16[3,1024,512]{2,1,0:T(8,128)(2,1)} custom-call(s32[1]{0:T(128)} %bitcast.14.pos_ref.refs_0_, bf16[1024,2048]{1,0:T(8,128)(2,1)} %all-gather.4.cloned.1.call-done.x_ref.refs_1_, bf16[1024,2048]{1,0:T(8,128)(2,1)} %all-gather.8.cloned.1.call-done.refs_2_, bf16[1024,512]{1,0:T(8,128)(2,1)} %get-tuple-element.84.gc_ref.refs_3_, ...), custom_call_target="tpu_custom_call" | custom-call | flops 6442450944 | bytes 12582912 | tf_op jit(solution)/shard_map/conv_wgrad_send/pallas_call | solution.py:286
  384.3 3.8 collective-permute-done.9
  388.1 1.4 collective-permute-start.10
  389.6 13.0 %gate_wgrad_keep.1.gate_ref = bf16[3,1024,512]{2,1,0:T(8,128)(2,1)} custom-call(s32[1]{0:T(128)} %bitcast.11.pos_ref.refs_0_, bf16[1024,2048]{1,0:T(8,128)(2,1)} %all-gather.4.cloned.1.call-done.x_ref.refs_1_, bf16[1024,2048]{1,0:T(8,128)(2,1)} %all-gather.8.cloned.1.call-done.refs_2_, bf16[1024,512]{1,0:T(8,128)(2,1)} %get-tuple-element.79.refs_3_.gg_ref, ...), custom_call_target="tpu_custom_call" | custom-call | flops 6442450944 | bytes 12582912 | tf_op jit(solution)/shard_map/gate_wgrad_keep/pallas_call | solution.py:286
  402.7 0.7 collective-permute-start.18
  403.4 13.1 %conv_wgrad_keep.1.conv_ref = bf16[3,1024,512]{2,1,0:T(8,128)(2,1)} custom-call(s32[1]{0:T(128)} %bitcast.11.pos_ref.refs_0_, bf16[1024,2048]{1,0:T(8,128)(2,1)} %all-gather.4.cloned.1.call-done.x_ref.refs_1_, bf16[1024,2048]{1,0:T(8,128)(2,1)} %all-gather.8.cloned.1.call-done.refs_2_, bf16[1024,512]{1,0:T(8,128)(2,1)} %get-tuple-element.84.gc_ref.refs_3_, ...), custom_call_target="tpu_custom_call" | custom-call | flops 6442450944 | bytes 12582912 | tf_op jit(solution)/shard_map/conv_wgrad_keep/pallas_call | solution.py:286
  416.7 1.0 fusion
  418.0 5.6 %collective-permute-done.16 = bf16[864,512]{1,0:T(8,128)(2,1)S(1)} collective-permute-done((bf16[864,512]{1,0:T(8,128)(2,1)}, bf16[864,512]{1,0:T(8,128)(2,1)S(1)}, u32[]{:S(2)}, u32[]{:S(2)}) %collective-permute-start.16) | collective-permute-done | bytes 884768 | tf_op jit(solution)/shard_map/ppermute | solution.py:816
  423.6 2.1 collective-permute-start.11
  425.7 1.2 fusion.14
  426.9 1.4 collective-permute-start.17
  428.3 9.2 %place_input_grad.2.rest_0_ = f32[3,16384,128]{2,1,0:T(8,128)} custom-call(s32[1]{0:T(128)} %bitcast.11.pos_ref.refs_0_, bf16[3,1024,512]{2,1,0:T(8,128)(2,1)} %conv_wgrad_keep.1.conv_ref, bf16[3,1024,512]{2,1,0:T(8,128)(2,1)} %gate_wgrad_keep.1.gate_ref), custom_call_target="tpu_custom_call" | custom-call | bytes 18874368 | tf_op jit(solution)/shard_map/place_input_grad/pallas_call | solution.py:760
  437.4 14.1 %collective-permute-done.18 = bf16[2,256,2048]{2,1,0:T(8,128)(2,1)} collective-permute-done((bf16[2,256,2048]{2,1,0:T(8,128)(2,1)}, bf16[2,256,2048]{2,1,0:T(8,128)(2,1)}, u32[]{:S(2)}, u32[]{:S(2)}) %collective-permute-start.18) | collective-permute-done | bytes 2097184 | tf_op jit(solution)/shard_map/ppermute | solution.py:822
  451.5 3.0 add_convert_fusion
  454.9 2.1 collective-permute-start.12
  457.6 8.4 %collective-permute-done.12 = f32[2,26,512]{2,1,0:T(8,128)} collective-permute-done((f32[2,26,512]{2,1,0:T(8,128)S(1)}, f32[2,26,512]{2,1,0:T(8,128)}, u32[]{:S(2)}, u32[]{:S(2)}) %collective-permute-start.12) | collective-permute-done | bytes 106528 | tf_op jit(solution)/shard_map/ppermute | solution.py:870
  466.0 0.9 broadcast_select_fusion.3
  467.0 0.7 pad_maximum_fusion.2
  468.0 9.2 %place_input_grad.3 = f32[3,16384,128]{2,1,0:T(8,128)} custom-call(s32[1]{0:T(128)} %bitcast.14.pos_ref.refs_0_, bf16[3,1024,512]{2,1,0:T(8,128)(2,1)} %collective-permute-done.14.conv_ref, bf16[3,1024,512]{2,1,0:T(8,128)(2,1)} %collective-permute-done.15.gate_ref, f32[3,16384,128]{2,1,0:T(8,128)} %place_input_grad.2.rest_0_), custom_call_target="tpu_custom_call", output_to_operand_aliasing={{}: (3, {})} | custom-call | bytes 18874368 | tf_op jit(solution)/shard_map/place_input_grad/pallas_call | solution.py:760
  477.2 2.4 convert_add_fusion
  479.6 1.0 slice.67
  480.6 0.9 slice.68
  481.5 0.9 collective-permute-done.13
  482.4 1.0 broadcast_select_fusion.1
  484.8 0.7 copy.64
  485.5 3.1 convert_reduce_fusion
  488.7 1.0 fusion.9
  490.4 1.4 fusion.11
  491.8 10.2 %join_halves.1 = f32[3,512,2048]{2,1,0:T(8,128)} custom-call(s32[1]{0:T(128)} %bitcast.11.pos_ref.refs_0_, bf16[3,256,2048]{2,1,0:T(8,128)(2,1)} %copy-done.2, bf16[3,256,2048]{2,1,0:T(8,128)(2,1)} %collective-permute-done.19.got_ref), custom_call_target="tpu_custom_call" | custom-call | bytes 18874368 | tf_op jit(solution)/shard_map/join_halves/pallas_call | solution.py:796
  (116 shorter events, 9.3 us)
Async XLA Ops:
  7.2 162.1 %copy-start = (f32[16,4096]{1,0:T(8,128)S(1)}, f32[16,4096]{1,0:T(8,128)}, u32[]{:S(2)}) copy-start(f32[16,4096]{1,0:T(8,128)} %param.21) | copy-start | bytes 786436
  7.2 7.5 %copy-start.20 = (s32[1,1024]{1,0:T(1,128)S(1)}, s32[1,1024]{1,0:T(1,128)}, u32[]{:S(2)}) copy-start(s32[1,1024]{1,0:T(1,128)} %modl_ref.3) | copy-start | bytes 12292
  7.2 80.7 %all-gather.4.cloned.1.call-start = ((), (), s32[]{:S(2)}) async-start(), calls=%async_computation.6 | async-start | bytes 4718592 | tf_op jit(solution)/shard_map/all_gather | solution.py:914
  9.0 0.6 copy-start.22
  11.7 186.5 %all-gather.6.cloned.1.call-start = ((), (), s32[]{:S(2)}) async-start(), calls=%async_computation.8 | async-start | bytes 4718592 | tf_op jit(solution)/shard_map/all_gather | solution.py:915
  11.7 24.0 %collective-permute-start.1 = (bf16[128,2048]{1,0:T(8,128)(2,1)}, bf16[128,2048]{1,0:T(8,128)(2,1)S(1)}, u32[]{:S(2)}, u32[]{:S(2)}) collective-permute-start(bf16[128,2048]{1,0:T(8,128)(2,1)} %fusion.7), channel_id=1, source_target_pairs={{0,16},{8,24},{16,0},{24,8},{1,17},{9,25},{17,1},{25,9},{2,18},{10... | collective-permute-start | bytes 1572872 | tf_op jit(solution)/shard_map/ppermute | solution.py:822
  14.7 21.0 %collective-permute-start = (s32[1,1024]{1,0:T(1,128)S(1)}, s32[1,1024]{1,0:T(1,128)S(1)}, u32[]{:S(2)}, u32[]{:S(2)}) collective-permute-start(s32[1,1024]{1,0:T(1,128)S(1)} %copy-done.20), channel_id=1, source_target_pairs={{0,16},{8,24},{16,0},{24,8},{1,17},{9,25},{17,1},{25,9},{2,18},{10... | collective-permute-start | bytes 12296 | tf_op jit(solution)/shard_map/ppermute | solution.py:822
  35.8 83.0 %copy-start.12 = (bf16[128,2048]{1,0:T(8,128)(2,1)}, bf16[128,2048]{1,0:T(8,128)(2,1)S(1)}, u32[]{:S(2)}) copy-start(bf16[128,2048]{1,0:T(8,128)(2,1)S(1)} %collective-permute-done.1) | copy-start | bytes 1572868
  87.9 224.8 %all-gather.8.cloned.1.call-start = ((), (), s32[]{:S(2)}) async-start(), calls=%async_computation.9 | async-start | bytes 4718592 | tf_op jit(solution)/shard_map/all_gather | solution.py:927
  167.7 221.9 %reduce-scatter.2.cloned.1.call-start = ((), (), s32[]{:S(2)}) async-start(), calls=%async_computation.7 | async-start | bytes 4718592 | tf_op jit(solution)/shard_map/reduce_scatter | solution.py:934
  204.9 27.0 %collective-permute-start.3 = (bf16[2,256,2048]{2,1,0:T(8,128)(2,1)}, bf16[2,256,2048]{2,1,0:T(8,128)(2,1)S(1)}, u32[]{:S(2)}, u32[]{:S(2)}) collective-permute-start(bf16[2,256,2048]{2,1,0:T(8,128)(2,1)} %get-tuple-element.66), channel_id=1, source_target_pairs={{0,8},{8,0},{16,24},{24,16},{1,9},{9,1},{17,25},{25,17},{2,10},{10... | collective-permute-start | bytes 6291464 | tf_op jit(solution)/shard_map/ppermute | solution.py:816
  204.9 27.0 %collective-permute-start.2 = (bf16[1,256,2048]{2,1,0:T(8,128)(2,1)}, bf16[1,256,2048]{2,1,0:T(8,128)(2,1)}, u32[]{:S(2)}, u32[]{:S(2)}) collective-permute-start(bf16[1,256,2048]{2,1,0:T(8,128)(2,1)} %get-tuple-element.65), channel_id=1, source_target_pairs={{0,8},{8,0},{16,24},{24,16},{1,9},{9,1},{17,25},{25,17},{2,10},{10... | collective-permute-start | bytes 3145736 | tf_op jit(solution)/shard_map/ppermute | solution.py:816
  230.4 82.3 %collective-permute-start.5 = (bf16[1024,512]{1,0:T(8,128)(2,1)}, bf16[1024,512]{1,0:T(8,128)(2,1)}, u32[]{:S(2)}, u32[]{:S(2)}) collective-permute-start(bf16[1024,512]{1,0:T(8,128)(2,1)} %get-tuple-element.79.refs_3_.gg_ref), channel_id=1, source_target_pairs={{0,16},{8,24},{16,0},{24,8},{1,17},{9,25},{17,1},{25,9},{2,18},{10... | collective-permute-start | bytes 3145736 | tf_op jit(solution)/shard_map/ppermute | solution.py:822
  231.9 1.3 copy-start.25
  240.6 52.6 %collective-permute-start.4 = (bf16[1,256,2048]{2,1,0:T(8,128)(2,1)}, bf16[1,256,2048]{2,1,0:T(8,128)(2,1)S(1)}, u32[]{:S(2)}, u32[]{:S(2)}) collective-permute-start(bf16[1,256,2048]{2,1,0:T(8,128)(2,1)} %get-tuple-element.67), channel_id=1, source_target_pairs={{0,16},{8,24},{16,0},{24,8},{1,17},{9,25},{17,1},{25,9},{2,18},{10... | collective-permute-start | bytes 3145736 | tf_op jit(solution)/shard_map/ppermute | solution.py:822
  241.1 52.1 %copy-start.11 = (bf16[1,256,2048]{2,1,0:T(8,128)(2,1)S(1)}, bf16[1,256,2048]{2,1,0:T(8,128)(2,1)}, u32[]{:S(2)}) copy-start(bf16[1,256,2048]{2,1,0:T(8,128)(2,1)} %get-tuple-element.67) | copy-start | bytes 3145732
  294.6 13.6 %all-to-all-start.2 = ((bf16[8,160,128]{2,1,0:T(8,128)(2,1)}), bf16[8,160,128]{2,1,0:T(8,128)(2,1)S(1)}, u32[]{:S(2)}, u32[]{:S(2)}) async-start(bf16[8,160,128]{2,1,0:T(8,128)(2,1)} %get-tuple-element.77), calls=%async_computation.3 | async-start | bytes 655360 | tf_op jit(solution)/shard_map/all_to_all | solution.py:857
  309.0 16.0 %all-to-all-start.3 = ((bf16[8,160,128]{2,1,0:T(8,128)(2,1)}), bf16[8,160,128]{2,1,0:T(8,128)(2,1)S(1)}, u32[]{:S(2)}, u32[]{:S(2)}) async-start(bf16[8,160,128]{2,1,0:T(8,128)(2,1)} %broadcast_in_dim.30), calls=%async_computation.4 | async-start | bytes 655360 | tf_op jit(solution)/shard_map/all_to_all | solution.py:857
  325.1 64.5 %collective-permute-start.8 = (bf16[3,1024,512]{2,1,0:T(8,128)(2,1)}, bf16[3,1024,512]{2,1,0:T(8,128)(2,1)}, u32[]{:S(2)}, u32[]{:S(2)}) collective-permute-start(bf16[3,1024,512]{2,1,0:T(8,128)(2,1)} %gate_wgrad_send.1), channel_id=1, source_target_pairs={{0,8},{8,0},{16,24},{24,16},{1,9},{9,1},{17,25},{25,17},{2,10},{10... | collective-permute-start | bytes 9437192 | tf_op jit(solution)/shard_map/ppermute | solution.py:816
  325.1 0.8 copy-start.14
  337.4 25.8 %collective-permute-start.6 = (bf16[1024,512]{1,0:T(8,128)(2,1)}, bf16[1024,512]{1,0:T(8,128)(2,1)S(1)}, u32[]{:S(2)}, u32[]{:S(2)}) collective-permute-start(bf16[1024,512]{1,0:T(8,128)(2,1)} %get-tuple-element.84.gc_ref.refs_3_), channel_id=1, source_target_pairs={{0,16},{8,24},{16,0},{24,8},{1,17},{9,25},{17,1},{25,9},{2,18},{10... | collective-permute-start | bytes 3145736 | tf_op jit(solution)/shard_map/ppermute | solution.py:822
  363.2 1.0 copy-start.26
  364.2 103.8 %all-to-all-start.4 = ((bf16[8,128,2048]{2,1,0:T(8,128)(2,1)}), bf16[8,128,2048]{2,1,0:T(8,128)(2,1)}, u32[]{:S(2)}, u32[]{:S(2)}) async-start(bf16[8,128,2048]{2,1,0:T(8,128)(2,1)} %bitcast.81), calls=%async_computation.5 | async-start | bytes 8388608 | tf_op jit(solution)/shard_map/all_to_all | solution.py:857
  370.0 12.8 %copy-start.19 = (f32[1,2048]{1,0:T(1,128)S(1)}, f32[1,2048]{1,0:T(1,128)}, u32[]{:S(2)}) copy-start(f32[1,2048]{1,0:T(1,128)} %get-tuple-element.92) | copy-start | bytes 24580
  370.0 13.5 %copy-start.16 = (f32[16,512]{1,0:T(8,128)S(1)}, f32[16,512]{1,0:T(8,128)}, u32[]{:S(2)}) copy-start(f32[16,512]{1,0:T(8,128)} %get-tuple-element.89) | copy-start | bytes 98308
  370.1 13.5 %copy-start.17 = (f32[8,512]{1,0:T(8,128)S(1)}, f32[8,512]{1,0:T(8,128)}, u32[]{:S(2)}) copy-start(f32[8,512]{1,0:T(8,128)} %get-tuple-element.90) | copy-start | bytes 49156
  370.1 13.5 %copy-start.18 = (f32[3,512]{1,0:T(4,128)S(1)}, f32[3,512]{1,0:T(4,128)}, u32[]{:S(2)}) copy-start(f32[3,512]{1,0:T(4,128)} %get-tuple-element.93) | copy-start | bytes 18436
  370.1 13.5 %copy-start.21 = (f32[1,512]{1,0:T(1,128)S(1)}, f32[1,512]{1,0:T(1,128)}, u32[]{:S(2)}) copy-start(f32[1,512]{1,0:T(1,128)} %get-tuple-element.91) | copy-start | bytes 6148
  382.4 21.0 %collective-permute-start.7 = (bf16[3,1024,512]{2,1,0:T(8,128)(2,1)}, bf16[3,1024,512]{2,1,0:T(8,128)(2,1)}, u32[]{:S(2)}, u32[]{:S(2)}) collective-permute-start(bf16[3,1024,512]{2,1,0:T(8,128)(2,1)} %conv_wgrad_send.1), channel_id=1, source_target_pairs={{0,8},{8,0},{16,24},{24,16},{1,9},{9,1},{17,25},{25,17},{2,10},{10... | collective-permute-start | bytes 9437192 | tf_op jit(solution)/shard_map/ppermute | solution.py:816
  383.8 4.4 collective-permute-start.9
  388.1 14.5 %collective-permute-start.10 = (f32[29,512]{1,0:T(8,128)S(1)}, f32[29,512]{1,0:T(8,128)S(1)}, u32[]{:S(2)}, u32[]{:S(2)}) collective-permute-start(f32[29,512]{1,0:T(8,128)S(1)} %add.57), channel_id=1, source_target_pairs={{0,16},{8,24},{16,0},{24,8},{1,17},{9,25},{17,1},{25,9},{2,18},{10... | collective-permute-start | bytes 178184 | tf_op jit(solution)/shard_map/ppermute | solution.py:822
  402.6 65.3 %collective-permute-start.15 = (bf16[3,1024,512]{2,1,0:T(8,128)(2,1)}, bf16[3,1024,512]{2,1,0:T(8,128)(2,1)}, u32[]{:S(2)}, u32[]{:S(2)}) collective-permute-start(bf16[3,1024,512]{2,1,0:T(8,128)(2,1)} %gate_wgrad_keep.1.gate_ref), channel_id=1, source_target_pairs={{0,8},{8,0},{16,24},{24,16},{1,9},{9,1},{17,25},{25,17},{2,10},{10... | collective-permute-start | bytes 9437192 | tf_op jit(solution)/shard_map/ppermute | solution.py:816
  402.7 14.1 %copy-start.3 = (f32[3,160,512]{2,1,0:T(8,128)S(1)}, f32[3,160,512]{2,1,0:T(8,128)}, u32[]{:S(2)}) copy-start(f32[3,160,512]{2,1,0:T(8,128)} %get-tuple-element.102) | copy-start | bytes 2949124
  402.7 14.0 %copy-start.5 = (f32[384,512]{1,0:T(8,128)S(1)}, f32[384,512]{1,0:T(8,128)}, u32[]{:S(2)}) copy-start(f32[384,512]{1,0:T(8,128)} %get-tuple-element.101) | copy-start | bytes 2359300
  402.7 48.8 %collective-permute-start.18 = (bf16[2,256,2048]{2,1,0:T(8,128)(2,1)}, bf16[2,256,2048]{2,1,0:T(8,128)(2,1)}, u32[]{:S(2)}, u32[]{:S(2)}) collective-permute-start(bf16[2,256,2048]{2,1,0:T(8,128)(2,1)} %get-tuple-element.105), channel_id=1, source_target_pairs={{0,16},{8,24},{16,0},{24,8},{1,17},{9,25},{17,1},{25,9},{2,18},{10... | collective-permute-start | bytes 6291464 | tf_op jit(solution)/shard_map/ppermute | solution.py:822
  416.5 51.5 %collective-permute-start.14 = (bf16[3,1024,512]{2,1,0:T(8,128)(2,1)}, bf16[3,1024,512]{2,1,0:T(8,128)(2,1)}, u32[]{:S(2)}, u32[]{:S(2)}) collective-permute-start(bf16[3,1024,512]{2,1,0:T(8,128)(2,1)} %conv_wgrad_keep.1.conv_ref), channel_id=1, source_target_pairs={{0,8},{8,0},{16,24},{24,16},{1,9},{9,1},{17,25},{25,17},{2,10},{10... | collective-permute-start | bytes 9437192 | tf_op jit(solution)/shard_map/ppermute | solution.py:816
  417.7 5.8 %collective-permute-start.16 = (bf16[864,512]{1,0:T(8,128)(2,1)}, bf16[864,512]{1,0:T(8,128)(2,1)S(1)}, u32[]{:S(2)}, u32[]{:S(2)}) collective-permute-start(bf16[864,512]{1,0:T(8,128)(2,1)} %fusion), channel_id=1, source_target_pairs={{0,8},{8,0},{16,24},{24,16},{1,9},{9,1},{17,25},{25,17},{2,10},{10... | collective-permute-start | bytes 2654216 | tf_op jit(solution)/shard_map/ppermute | solution.py:816
  423.6 13.8 %copy-start.7 = (bf16[864,512]{1,0:T(8,128)(2,1)}, bf16[864,512]{1,0:T(8,128)(2,1)S(1)}, u32[]{:S(2)}) copy-start(bf16[864,512]{1,0:T(8,128)(2,1)S(1)} %collective-permute-done.16) | copy-start | bytes 2654212
  423.6 13.8 %collective-permute-start.11 = (f32[1,26,512]{2,1,0:T(8,128)S(1)}, f32[1,26,512]{2,1,0:T(8,128)S(1)}, u32[]{:S(2)}, u32[]{:S(2)}) collective-permute-start(f32[1,26,512]{2,1,0:T(8,128)S(1)} %slice_bitcast_fusion.1), channel_id=1, source_target_pairs={{0,1},{1,0},{2,3},{3,2},{4,5},{5,4},{6,7},{7,6},{8,9},{9,8},{10,11... | collective-permute-start | bytes 159752 | tf_op jit(solution)/shard_map/ppermute | solution.py:870
  426.9 50.3 %collective-permute-start.17 = (bf16[864,512]{1,0:T(8,128)(2,1)}, bf16[864,512]{1,0:T(8,128)(2,1)}, u32[]{:S(2)}, u32[]{:S(2)}) collective-permute-start(bf16[864,512]{1,0:T(8,128)(2,1)} %fusion.14), channel_id=1, source_target_pairs={{0,16},{8,24},{16,0},{24,8},{1,17},{9,25},{17,1},{25,9},{2,18},{10... | collective-permute-start | bytes 2654216 | tf_op jit(solution)/shard_map/ppermute | solution.py:822
  437.4 17.1 %copy-start.6 = (bf16[1,256,2048]{2,1,0:T(8,128)(2,1)S(1)}, bf16[1,256,2048]{2,1,0:T(8,128)(2,1)}, u32[]{:S(2)}) copy-start(bf16[1,256,2048]{2,1,0:T(8,128)(2,1)} %add_convert_fusion.1) | copy-start | bytes 3145732
  454.8 22.4 %copy-start.2 = (bf16[3,256,2048]{2,1,0:T(8,128)(2,1)}, bf16[3,256,2048]{2,1,0:T(8,128)(2,1)S(1)}, u32[]{:S(2)}) copy-start(bf16[3,256,2048]{2,1,0:T(8,128)(2,1)S(1)} %pad_maximum_fusion.mine_ref) | copy-start | bytes 9437188
  454.8 37.0 %collective-permute-start.19 = (bf16[3,256,2048]{2,1,0:T(8,128)(2,1)S(1)}, bf16[3,256,2048]{2,1,0:T(8,128)(2,1)}, u32[]{:S(2)}, u32[]{:S(2)}) collective-permute-start(bf16[3,256,2048]{2,1,0:T(8,128)(2,1)S(1)} %pad_maximum_fusion.mine_ref), channel_id=1, source_target_pairs={{0,8},{8,0},{16,24},{24,16},{1,9},{9,1},{17,25},{25,17},{2,10},{10... | collective-permute-start | bytes 9437192 | tf_op jit(solution)/shard_map/ppermute | solution.py:816
  454.9 11.1 %collective-permute-start.12 = (f32[2,26,512]{2,1,0:T(8,128)S(1)}, f32[2,26,512]{2,1,0:T(8,128)}, u32[]{:S(2)}, u32[]{:S(2)}) collective-permute-start(f32[2,26,512]{2,1,0:T(8,128)S(1)} %pad_maximum_fusion.3), channel_id=1, source_target_pairs={{0,2},{1,3},{2,0},{3,1},{4,6},{5,7},{6,4},{7,5},{8,10},{9,11},{10,... | collective-permute-start | bytes 319496 | tf_op jit(solution)/shard_map/ppermute | solution.py:870
  466.9 10.2 %copy-start.9 = (f32[2,26,512]{2,1,0:T(8,128)}, f32[2,26,512]{2,1,0:T(8,128)S(1)}, u32[]{:S(2)}) copy-start(f32[2,26,512]{2,1,0:T(8,128)S(1)} %get-tuple-element.115) | copy-start | bytes 319492
  467.7 14.7 %collective-permute-start.13 = (f32[4,26,512]{2,1,0:T(8,128)}, f32[4,26,512]{2,1,0:T(8,128)}, u32[]{:S(2)}, u32[]{:S(2)}) collective-permute-start(f32[4,26,512]{2,1,0:T(8,128)} %pad_maximum_fusion.2), channel_id=1, source_target_pairs={{0,4},{1,5},{2,6},{3,7},{4,0},{5,1},{6,2},{7,3},{8,12},{9,13},{10,... | collective-permute-start | bytes 638984 | tf_op jit(solution)/shard_map/ppermute | solution.py:870
  479.5 2.9 copy-start.10
  485.5 3.1 copy-start.4
  485.5 3.1 copy-start.13
  485.5 3.1 copy-start.15
  488.6 1.7 copy-start.8
  488.6 1.7 copy-start.23
  488.6 1.7 copy-start.24
  491.8 10.2 %copy-start.1 = (f32[16,4096]{1,0:T(8,128)S(1)}, f32[16,4096]{1,0:T(8,128)}, u32[]{:S(2)}) copy-start(f32[16,4096]{1,0:T(8,128)} %param.21) | copy-start | bytes 786436
Sparse Core Ops, SparseCore 0:
  11.8 76.0 all-gather.3
  90.0 84.2 all-gather.5
  177.1 72.4 all-gather.7
  253.7 86.8 reduce-scatter.1

commit v3 on v2

--- a/solution.py
+++ b/solution.py
@@ -381,8 +381,8 @@
 
 
 def scan_fwd_body(pj_ref, act_ref, gate_ref, sp_ref, sb_ref, ld_ref, skip_ref, modc_ref, modr_ref,
-                  delta_ref, sig_ref, gated_ref, scanned_ref, prev_ref, final_ref,
-                  state, pre_s, d_s, u_s, r_s, b_s, c_s, yp_s):
+                  delta_ref, sig_ref, gated_ref, scanned_ref, prev_ref, final_ref, b_s, c_s,
+                  state, pre_s, d_s, u_s, r_s, yp_s):
     span, chans = act_ref.shape
     rank = pj_ref.shape[1] - 64
     tiles = chans // LANES
@@ -446,6 +446,7 @@
     blocks = rows // LANES
     row = pl.BlockSpec((LANES, chans), lambda i: (i, 0))
     full = lambda shape: pl.BlockSpec(shape, lambda i: (0,) * len(shape))
+    wide = pl.BlockSpec((LANES, 16, LANES), lambda i: (i, 0, 0))
     return pl.pallas_call(
         scan_fwd_body,
         grid=(blocks,),
@@ -463,6 +464,8 @@
             row, row, row, row,
             pl.BlockSpec((LANES * 16, chans), lambda i: (i, 0)),
             full((16, chans)),
+            wide,
+            wide,
         ],
         out_shape=[
             jax.ShapeDtypeStruct((rows, chans), bf16),
@@ -471,20 +474,21 @@
             jax.ShapeDtypeStruct((rows, chans), f32),
             jax.ShapeDtypeStruct((rows * 16, chans), f32),
             jax.ShapeDtypeStruct((16, chans), f32),
+            jax.ShapeDtypeStruct((rows, 16, LANES), f32),
+            jax.ShapeDtypeStruct((rows, 16, LANES), f32),
         ],
         scratch_shapes=[pltpu.VMEM((16, chans), f32)] + [pltpu.VMEM((LANES, chans), f32)] * 3
         + [pltpu.VMEM((16, chans), f32)]
-        + [pltpu.VMEM((LANES, 16, LANES), f32)] * 2
         + [pltpu.VMEM((LANES, 8, chans), f32)],
         cost_estimate=cost(40e9, 64 * rows * chans + 20 * rows * chans),
         name="scan_forward",
     )(pj, act, gate, step_proj, step_bias, log_decay, skip, modc, modr)
 
 
-def scan_bwd_body(pj_ref, act_ref, gate_ref, gg_ref, delta_ref, sig_ref, prev_ref, final_ref,
+def scan_bwd_body(pj_ref, act_ref, gate_ref, gg_ref, delta_ref, sig_ref, prev_ref, final_ref, b_s, c_s,
                   sp_ref, ld_ref, skip_ref, modc_ref, modr_ref,
                   gas_ref, gpt_ref, glogd_ref, gskip_ref, gbias_ref, gstep_ref,
-                  carry_w, acc, later, d_s, u_s, gs_s, r_s, b_s, c_s, gp_s, hp_s, p_s, q_s):
+                  carry_w, acc, later, d_s, u_s, gs_s, r_s, gp_s, hp_s, p_s, q_s):
     span, chans = act_ref.shape
     rank = pj_ref.shape[1] - 64
     tiles = chans // LANES
@@ -500,9 +504,6 @@
 
     rates = -jnp.exp(ld_ref[...])
     r_s[...] = rates * log2e
-    b, c = state_vectors(pj_ref, rank)
-    spread(b, b_s)
-    spread(c, c_s)
 
     act = act_ref[...].astype(f32)
     d = delta_ref[...].astype(f32)
@@ -588,7 +589,7 @@
     glogd_ref[...] = acc[...] * rates
 
 
-def scan_backward(pj, act, gate, gg, delta, sig, prev, final, step_proj, log_decay, skip, modc, modr):
+def scan_backward(pj, act, gate, gg, delta, sig, prev, final, b, c, step_proj, log_decay, skip, modc, modr):
     rows, chans = act.shape
     blocks = rows // LANES
     rank = step_proj.shape[0] // M
@@ -596,6 +597,7 @@
     row = pl.BlockSpec((LANES, chans), lambda i: (last - i, 0))
     full = lambda shape: pl.BlockSpec(shape, lambda i: (0,) * len(shape))
     slab = lambda shape: pl.BlockSpec((1,) + shape, lambda i: (last - i, 0, 0))
+    wide = pl.BlockSpec((LANES, 16, LANES), lambda i: (last - i, 0, 0))
     return pl.pallas_call(
         scan_bwd_body,
         grid=(blocks,),
@@ -604,6 +606,8 @@
             row, row, row, row, row,
             pl.BlockSpec((LANES * 16, chans), lambda i: (last - i, 0)),
             full((16, chans)),
+            wide,
+            wide,
             full(step_proj.shape),
             full((16, chans)),
             full((1, chans)),
@@ -629,12 +633,11 @@
         scratch_shapes=[pltpu.VMEM((16, chans), f32)] * 3
         + [pltpu.VMEM((LANES, chans), f32)] * 3
         + [pltpu.VMEM((16, chans), f32)]
-        + [pltpu.VMEM((LANES, 16, LANES), f32)] * 2
         + [pltpu.VMEM((LANES, 8, chans), f32)] * 2
         + [pltpu.VMEM((LANES, 16, LANES), f32)] * 2,
         cost_estimate=cost(60e9, 64 * rows * chans + 20 * rows * chans),
         name="scan_backward",
-    )(pj, act, gate, gg, delta, sig, prev, final, step_proj, log_decay, skip, modc, modr)
+    )(pj, act, gate, gg, delta, sig, prev, final, b, c, step_proj, log_decay, skip, modc, modr)
 
 
 def conv_bwd_body(gp_ref, sp_ref, gas_ref, ci_ref, act_ref, cw_ref, cb_ref, modc_ref, modr_ref,
@@ -839,18 +842,25 @@
     return lax.reduce_precision(value, 8, 7)
 
 
-def batch_total(value, first, second):
-    value = value + after(swap_core(value), first)
-    return y_sum(value, second)
-
-
-def batch_total_rounded(value, first, second):
-    value = rounded(value)
-    value = rounded(value + after(swap_core(value.astype(bf16)), first).astype(f32))
-    total = value
-    for other in y_others(value.astype(bf16)):
-        total = total + after(other, second).astype(f32)
-    return total
+def split(value):
+    high = rounded(value)
+    return jnp.concatenate([high, rounded(value - high)], axis=0).astype(bf16)
+
+
+def joined(value):
+    count = value.shape[0] // 2
+    return value[:count].astype(f32) + value[count:].astype(f32)
+
+
+def small_totals(coarse, fine, first, second):
+    rows = coarse.shape[0]
+    for step, before in ((lambda value: [swap_core(value)], first), (y_others, second)):
+        message = lax.optimization_barrier(jnp.concatenate([rounded(coarse).astype(bf16), split(fine)], axis=0))
+        coarse, fine = message[:rows].astype(f32), joined(message[rows:])
+        for other in step(message):
+            other = after(other, *before)
+            coarse, fine = coarse + other[:rows].astype(f32), fine + joined(other[rows:])
+    return coarse, fine
 
 
 def to_owners(pieces):
@@ -925,28 +935,28 @@
     packed = jnp.concatenate([high, low], axis=1)
     pj = to_all(packed).reshape(blocks, psize + 2 * states, LANES)
     xs = [x] + [lax.all_gather(after(other, pj), "own", axis=0, tiled=True) for other in normed_others]
-    delta, sig, gated, scanned, prev, final = scan_forward(
+    delta, sig, gated, scanned, prev, final, b_wide, c_wide = scan_forward(
         pj, act, gate, step_rows, step_bias, decay, skip, modc, modr
     )
-    gg, ggate = gated_grads(cot, output_proj, modc, scanned, gate)
-    ggates = [ggate] + y_others(ggate)
     branch_part = select_matmul(gated, output_proj, modc, False, bf16, "output_stage")
     branch = lax.psum_scatter(branch_part, "own", scatter_dimension=0, tiled=True)
     block_out = (resid + branch.astype(f32)).astype(bf16)[None]
 
     gated_t = jnp.swapaxes(gated, 0, 1)
-    groups = ((0,), (1, 2))
+    groups = ((0, 1, 2),)
     out_got = [
         swap_core(value) for value in rows_wgrad(other_at, gated_t, cot, modl, [], groups, "output_wgrad_send")
     ]
-    out_half = rows_wgrad(core_at, gated_t, cot, modl, out_got, groups, "output_wgrad_keep")
-    out_total = [y_sum(out_half[0]).astype(bf16)]
-
+    out_half = rows_wgrad(core_at, gated_t, cot, modl, [after(value, branch_part) for value in out_got], groups, "output_wgrad_keep")
+    out_total = y_sum(out_half[0]).astype(bf16)
+
+    gg, ggate = gated_grads(after(cot, *out_half), output_proj, modc, scanned, gate)
+    ggates = [ggate] + y_others(ggate)
     gas, gpt, glogd, gskip, gbias, gstep = scan_backward(
-        after(pj, branch_part, *out_half), act, gate, gg, delta, sig, prev, final, step_rows, decay, skip, modc, modr
+        after(pj, branch_part, *out_half), act, gate, gg, delta, sig, prev, final, b_wide, c_wide, step_rows, decay, skip, modc, modr
     )
-    gpt = after(gpt, out_total[0])
     gp_own = jnp.sum(to_owners(gpt.reshape(own_count, per_owner * psize, LANES)).astype(f32), axis=0).astype(bf16)
+    gp_own = after(gp_own, out_total)
     gp = to_all(gp_own).reshape(blocks, psize, LANES)
 
     ggates = [ggate] + [after(other, gp_own) for other in ggates[1:]]
@@ -959,25 +969,17 @@
     gnormed, gain_part = input_dgrad(gci, ggate, w_in, modc, x, norm_gain.reshape(1, width))
 
     gcis = [gci] + [after(other, gnormed) for other in others]
-    gnormed = to_owners(after(gnormed, *others).reshape(own_count, span, width))
+    gnormed = lax.psum_scatter(gnormed, "own", scatter_dimension=0, tiled=True)
     conv_send = half_wgrad(other_at, xs, gcis, modcs, None, "conv_wgrad_send")
     gate_mine = half_wgrad(core_at, xs, ggates, modcs, after(gate_got, conv_send, branch), "gate_wgrad_keep")
     gate_recv = swap_core(gate_mine)
-    gain_rows = width // chans
-    small = batch_total(
-        jnp.concatenate([glogd, gcw[:5], gskip, gain_part.reshape(gain_rows, chans), gbias], axis=0),
-        conv_send, gate_mine,
-    )
-    conv_got = after(swap_core(conv_send), gate_mine, small)
+    conv_got = after(swap_core(conv_send), gate_mine)
     conv_mine = half_wgrad(core_at, xs, gcis, modcs, conv_got, "conv_wgrad_keep")
     conv_recv = swap_core(conv_mine)
-    half_placed = place_input_grad(core_at, conv_mine, gate_mine, None)
-    grad_input = place_input_grad(other_at, conv_recv, gate_recv, half_placed)
-    gnormed = after(gnormed, half_placed)
-    out_total.append(y_sum(after(out_half[1], small), half_placed).astype(bf16))
-    out_total = jnp.concatenate(out_total, axis=0)
-    grad_output = join_halves(core_at, after(out_total, gnormed), swap_core(out_total))
-    gnormed = jnp.sum(gnormed.astype(f32), axis=0)
+    grad_output = join_halves(core_at, out_total, swap_core(out_total))
+    half_placed = place_input_grad(core_at, after(conv_mine, grad_output), gate_mine, None)
+    grad_input = place_input_grad(other_at, after(conv_recv, gnormed), gate_recv, half_placed)
+    gnormed = gnormed.astype(f32)
 
     weighted = norm_gain * gnormed
     coupled = jnp.mean(resid * weighted, axis=-1, keepdims=True)
@@ -985,13 +987,16 @@
         grad_out[0].astype(f32) + inverse * weighted - resid * (inverse * inverse * inverse) * coupled
     )[None]
 
-    weights = batch_total_rounded(
-        jnp.concatenate([gstep, gstate.reshape(M * psize, chans)], axis=0), conv_send, grad_input
+    gain_rows = width // chans
+    weights, small = small_totals(
+        jnp.concatenate([gstep, gstate.reshape(M * psize, chans)], axis=0),
+        jnp.concatenate([glogd, gcw[:5], gskip, gain_part.reshape(gain_rows, chans), gbias], axis=0),
+        (conv_send,), (half_placed,),
     )
     grad_step = weights[: M * rank].reshape(M, rank, chans)
     grad_state = jnp.swapaxes(weights[M * rank :].reshape(M, psize, chans), 1, 2)
     grad_bias = small[states + 6 + gain_rows :]
-    wide = gather_small(small[: states + 6 + gain_rows], conv_mine, half_placed, grad_input)
+    wide = gather_small(small[: states + 6 + gain_rows], half_placed, half_placed, grad_input)
     grad_gain = jnp.sum(wide[:, states + 6 :], axis=0).reshape(width)
     wide = jnp.swapaxes(wide[:, : states + 6], 0, 1).reshape(states + 6, own_count * chans)
     grad_input = input_grad_layout(grad_input, width, chans)

time: 511 us -> 481 us (0.941)
  waiting for transfers between devices: 100 us -> 89.6 us
  starting transfers between devices: 29.6 us -> 19.2 us
    ppermute x9 -> x7, waiting for transfers between devices: 9.42 us -> 3.19 us  [swap_core(): return lax.ppermute(value, 'batch', [(i, i ^ 1) for i in range(count)])]
    all_to_all x3 -> x2, starting transfers between devices: 13 us -> 6.96 us  [to_owners(): lax.all_to_all(pieces, 'own', split_axis=0, concat_axis=0, tiled=False)]
    pallas_call x1, Pallas kernels: 52.1 us -> 46.3 us  [scan_backward(): pl.pallas_call(scan_bwd_body, grid=(blocks,), in_specs=[slab(pj.shape[1:]...]
    ppermute x8 -> x6, waiting for transfers between devices: 20.1 us -> 16.5 us  [y_others(): lax.ppermute(value, 'batch', [(i, (i + shift) % count) for i in range(cou...]
  transfers between devices with their start and end apart: 27 -> 23, of which waited for: 8 -> 8; matrix products, arithmetic and copies ran while one was open for 11% -> 10% of each run, Pallas kernels for 48% -> 52%
where the time goes in v3:
time: 481 us; the launch traced here: 479 us
  Pallas kernels  248 us (52%)
  waiting for transfers between devices  89.6 us (19%)
  blocking collectives  48.8 us (10%)
  local copies, waits for them, and re-layouts  39.3 us (8%)
  starting transfers between devices  19.2 us (4%)
  other arithmetic  18.9 us (4%)
  between operations  14.3 us (3%)
    all_gather x1, waiting for transfers between devices, per_device(): x = lax.all_gather(normed, 'own', axis=0, tiled=True)  52.1 us
    pallas_call x4, Pallas kernels, half_wgrad(): pl.pallas_call(functools.partial(wgrad_body, sets=sets, add=got is not No...  50.9 us
    all_to_all x2, blocking collectives, to_owners(): lax.all_to_all(pieces, 'own', split_axis=0, concat_axis=0, tiled=False)  48.8 us
    pallas_call x1, Pallas kernels, scan_backward(): pl.pallas_call(scan_bwd_body, grid=(blocks,), in_specs=[slab(pj.shape[1:]...  46.3 us
    pallas_call x1, Pallas kernels, input_stage(): pl.pallas_call(functools.partial(in_body, rows=rows, block=min(256, rows)...  27.1 us
    pallas_call x1, Pallas kernels, scan_forward(): pl.pallas_call(scan_fwd_body, grid=(blocks,), in_specs=[pl.BlockSpec((1,)...  26.5 us
    reshape x1, local copies, waits for them, and re-layouts, per_device(): w_in = input_proj.reshape(M, width, 2 * chans)  20.9 us
    pallas_call x2, Pallas kernels, place_input_grad(): pl.pallas_call(body, grid_spec=pltpu.PrefetchScalarGridSpec(num_scalar_pr...  18.4 us
  transfers between devices with their start and end apart: 23, of which 8 were waited for; matrix products, arithmetic and copies ran while one was open for 10% of the time, Pallas kernels for 52%

profile of v3, /device:TPU:0, one launch (start us, length us, event | category | flops | bytes accessed | tf_op | source)
XLA Modules:
  0.0 478.5 jit_solution(14550114853064713735)
XLA Ops:
  7.2 1.3 fusion.1
  9.0 2.0 fusion.3
  11.2 3.0 collective-permute-start.1
  14.3 20.9 %reshape.117.wc_ref.wg_ref.w_ref = bf16[3,2048,1024]{2,1,0:T(8,128)(2,1)} reshape(bf16[3,2048,2,512]{3,2,1,0:T(2,128)(2,1)} %param.15) | data formatting | bytes 25165824 | tf_op jit(solution)/shard_map/reshape | solution.py:911
  35.2 52.1 %all-gather.4.cloned.1.call-done.x_ref.refs_1_ = bf16[1024,2048]{1,0:T(8,128)(2,1)} async-done(((bf16[128,2048]{1,0:T(8,128)(2,1)}), bf16[1024,2048]{1,0:T(8,128)(2,1)}) %all-gather.4.cloned.1.call-update) | async-done | bytes 4194320 | tf_op jit(solution)/shard_map/all_gather | solution.py:924
  87.4 1.0 copy.47.modc_ref.refs_5_
  88.5 1.3 dynamic_slice.13
  89.8 1.3 constant_dynamic-slice_fusion.1.cw_ref
  91.1 27.1 %input_stage.1 = (bf16[1024,512]{1,0:T(8,128)(2,1)}, bf16[1024,512]{1,0:T(8,128)(2,1)}, bf16[1024,512]{1,0:T(8,128)(2,1)}, bf16[8,160,128]{2,1,0:T(8,128)(2,1)}) custom-call(bf16[1024,2048]{1,0:T(8,128)(2,1)} %all-gather.4.cloned.1.call-done.x_ref.refs_1_, bf16[3,2048,1024]{2,1,0:T(8,128)(2,1)} %reshape.117.wc_ref.wg_ref.w_ref, ...), custom_call_target="tpu_custom_call" | custom-call | flops 12884901888 | bytes 16777216 | tf_op jit(solution)/shard_map/input_stage/pallas_call | solution.py:112
  118.2 22.8 %all_to_all.20 = bf16[8,160,128]{2,1,0:T(8,128)(2,1)S(1)} all-to-all(bf16[8,160,128]{2,1,0:T(8,128)(2,1)} %get-tuple-element.55), channel_id=1, replica_groups=mesh['batch'=4,'own'=8] {'own'}, dimensions={0} | all-to-all | bytes 655360 | tf_op jit(solution)/shard_map/all_to_all | solution.py:867
  141.1 26.1 %all_to_all.21 = bf16[8,1,192,128]{3,2,1,0:T(8,128)(2,1)} all-to-all(bf16[8,1,192,128]{3,2,1,0:T(8,128)(2,1)S(1)} %broadcast_in_dim.30), channel_id=1, replica_groups=mesh['batch'=4,'own'=8] {'own'}, dimensions={0} | all-to-all | bytes 786432 | tf_op jit(solution)/shard_map/all_to_all | solution.py:867
  167.3 1.3 dynamic_slice.15
  168.6 0.6 constant_dynamic-slice_fusion.ld_ref
  169.3 26.5 %scan_forward.1 = (bf16[1024,512]{1,0:T(8,128)(2,1)}, f32[1024,512]{1,0:T(8,128)}, bf16[1024,512]{1,0:T(8,128)(2,1)}, f32[1024,512]{1,0:T(8,128)}, f32[16384,512...) custom-call(bf16[8,192,128]{2,1,0:T(8,128)(2,1)} %bitcast.64, ...), custom_call_target="tpu_custom_call" | custom-call | flops 40000000000 | bytes 44040192 | tf_op jit(solution)/shard_map/scan_forward/pallas_call | solution.py:450
  195.8 2.3 copy.50
  198.1 6.9 %output_wgrad_send.1 = bf16[3,256,2048]{2,1,0:T(8,128)(2,1)} custom-call(s32[1]{0:T(128)} %bitcast.15.pos_ref.refs_0_, bf16[512,1024]{1,0:T(8,128)(2,1)} %bitcast.58, bf16[1024,2048]{1,0:T(8,128)(2,1)} %all-gather.6.cloned.1.call-done.g_ref.x_ref, s32[1,1024]{1,0:T(1,128)} %modl_ref.3), custom_call_target="tpu_custom_call" | custom-call | flops 3221225472 | bytes 11010048 | tf_op jit(solution)/shard_map/output_wgrad_send/pallas_call | solution.py:320
  205.0 12.5 %output_stage.1 = bf16[1024,2048]{1,0:T(8,128)(2,1)} custom-call(bf16[1024,512]{1,0:T(8,128)(2,1)} %get-tuple-element.58.x_ref, bf16[3,512,2048]{2,1,0:T(8,128)(2,1)} %w_ref.3, s32[1024,1]{1,0:T(8,128)} %copy.47.modc_ref.refs_5_), custom_call_target="tpu_custom_call" | custom-call | flops 6442450944 | bytes 11534336 | tf_op jit(solution)/shard_map/output_stage/pallas_call | solution.py:160
  217.5 1.7 copy-done.20
  219.1 7.4 %output_wgrad_keep.1 = bf16[3,256,2048]{2,1,0:T(8,128)(2,1)} custom-call(s32[1]{0:T(128)} %bitcast.13.pos_ref.refs_0_, bf16[512,1024]{1,0:T(8,128)(2,1)} %bitcast.59, bf16[1024,2048]{1,0:T(8,128)(2,1)} %all-gather.6.cloned.1.call-done.g_ref.x_ref, s32[1,1024]{1,0:T(1,128)} %modl_ref.3, bf16[3,256,2048]{2,1,0:T(8,128)(2,1)} %copy-done.20), custom_call_target="tpu_custom_call" | custom-call | flops 3221225472 | bytes 11010048 | tf_op jit(solution)/shard_map/output_wgrad_keep/pallas_call | solution.py:320
  226.6 1.6 collective-permute-start.3
  228.2 12.5 %gated_grads.1 = (bf16[1024,512]{1,0:T(8,128)(2,1)}, bf16[1024,512]{1,0:T(8,128)(2,1)}) custom-call(bf16[1024,2048]{1,0:T(8,128)(2,1)} %all-gather.6.cloned.1.call-done.g_ref.x_ref, bf16[3,512,2048]{2,1,0:T(8,128)(2,1)} %w_ref.3, s32[1024,1]{1,0:T(8,128)} %copy.47.modc_ref.refs_5_, f32[1024,512]{1,0:T(8,128)} %get-tuple-element.63.scanned_ref, ...), custom_call_target="tpu_custom_call" | custom-call | flops 6442450944 | bytes 15728640 | tf_op jit(solution)/shard_map/gated_grads/pallas_call | solution.py:196
  240.6 46.3 %scan_backward.1 = (bf16[1024,512]{1,0:T(8,128)(2,1)}, bf16[8,160,128]{2,1,0:T(8,128)(2,1)}, f32[16,512]{1,0:T(8,128)}, f32[1,512]{1,0:T(1,128)}, f32[3,512]{1,0:T(4,128)}, /*index=5*/f32[384,512]{1,0:T(8,128)}) custom-call(bf16[8,192,128]{2,1,0:T(8,128)(2,1)} %bitcast.65, bf16[1024,512]{1,0:T(8,128)(2,1)} %get-tuple-element.56.act_ref, ...), custom_call_target="tpu_custom_call" | custom-call | flops 60000002048 | bytes 44040192 | tf_op jit(solution)/shard_map/scan_backward/pallas_call | solution.py:601
  286.9 3.4 all-to-all-start.2
  290.9 1.1 copy.54.refs_6_
  291.9 9.8 %all-to-all-done.2 = bf16[8,160,128]{2,1,0:T(8,128)(2,1)S(1)} async-done(((bf16[8,160,128]{2,1,0:T(8,128)(2,1)}), bf16[8,160,128]{2,1,0:T(8,128)(2,1)S(1)}, u32[]{:S(2)}, u32[]{:S(2)}) %all-to-all-start.2) | async-done | bytes 327712 | tf_op jit(solution)/shard_map/all_to_all | solution.py:867
  301.8 4.5 add_convert_fusion.mine_ref
  306.3 0.8 broadcast_in_dim.32
  307.1 3.5 all-to-all-start.3
  310.9 9.0 %collective-permute-done.4.refs_4_ = bf16[1024,512]{1,0:T(8,128)(2,1)} collective-permute-done((bf16[1024,512]{1,0:T(8,128)(2,1)}, bf16[1024,512]{1,0:T(8,128)(2,1)}, u32[]{:S(2)}, u32[]{:S(2)}) %collective-permute-start.4) | collective-permute-done | bytes 1048608 | tf_op jit(solution)/shard_map/ppermute | solution.py:825
  319.8 12.3 %gate_wgrad_send.1 = bf16[3,1024,512]{2,1,0:T(8,128)(2,1)} custom-call(s32[1]{0:T(128)} %bitcast.15.pos_ref.refs_0_, bf16[1024,2048]{1,0:T(8,128)(2,1)} %all-gather.4.cloned.1.call-done.x_ref.refs_1_, bf16[1024,2048]{1,0:T(8,128)(2,1)} %all-gather.8.cloned.1.call-done.refs_2_, bf16[1024,512]{1,0:T(8,128)(2,1)} %get-tuple-element.74.refs_3_.gg_ref, ...), custom_call_target="tpu_custom_call" | custom-call | flops 6442450944 | bytes 12582912 | tf_op jit(solution)/shard_map/gate_wgrad_send/pallas_call | solution.py:286
  332.1 0.7 copy-done.9
  332.8 11.6 %conv_backward.1 = (bf16[1024,512]{1,0:T(8,128)(2,1)}, f32[3,160,512]{2,1,0:T(8,128)}, f32[8,512]{1,0:T(8,128)}) custom-call(bf16[8,160,128]{2,1,0:T(8,128)(2,1)} %copy-done.9, bf16[3,160,512]{2,1,0:T(8,128)(2,1)} %bitcast.85, bf16[1024,512]{1,0:T(8,128)(2,1)} %get-tuple-element.77.gas_ref, bf16[1024,512]{1,0:T(8,128)(2,1)} %get-tuple-element.78.ci_ref, ...), custom_call_target="tpu_custom_call" | custom-call | flops 2013265920 | bytes 5242880 | tf_op jit(solution)/shard_map/conv_backward/pallas_call | solution.py:699
  344.4 1.6 collective-permute-start.6
  346.0 18.2 %input_dgrad.1 = (bf16[1024,2048]{1,0:T(8,128)(2,1)}, f32[1,2048]{1,0:T(1,128)}) custom-call(bf16[1024,512]{1,0:T(8,128)(2,1)} %get-tuple-element.79.gc_ref.refs_3_, bf16[1024,512]{1,0:T(8,128)(2,1)} %get-tuple-element.74.refs_3_.gg_ref, bf16[3,2048,1024]{2,1,0:T(8,128)(2,1)} %reshape.117.wc_ref.wg_ref.w_ref, s32[1024,1]{1,0:T(8,128)} %copy.47.modc_ref.refs_5_, ...), custom_call_target="tpu_custom_call" | custom-call | flops 12884901888 | bytes 23068672 | tf_op jit(solution)/shard_map/input_dgrad/pallas_call | solution.py:235
  364.3 5.2 %collective-permute-done.6.refs_4_ = bf16[1024,512]{1,0:T(8,128)(2,1)} collective-permute-done((bf16[1024,512]{1,0:T(8,128)(2,1)}, bf16[1024,512]{1,0:T(8,128)(2,1)}, u32[]{:S(2)}, u32[]{:S(2)}) %collective-permute-start.6) | collective-permute-done | bytes 1048608 | tf_op jit(solution)/shard_map/ppermute | solution.py:825
  369.5 12.2 %conv_wgrad_send.1 = bf16[3,1024,512]{2,1,0:T(8,128)(2,1)} custom-call(s32[1]{0:T(128)} %bitcast.15.pos_ref.refs_0_, bf16[1024,2048]{1,0:T(8,128)(2,1)} %all-gather.4.cloned.1.call-done.x_ref.refs_1_, bf16[1024,2048]{1,0:T(8,128)(2,1)} %all-gather.8.cloned.1.call-done.refs_2_, bf16[1024,512]{1,0:T(8,128)(2,1)} %get-tuple-element.79.gc_ref.refs_3_, ...), custom_call_target="tpu_custom_call" | custom-call | flops 6442450944 | bytes 12582912 | tf_op jit(solution)/shard_map/conv_wgrad_send/pallas_call | solution.py:286
  382.3 0.7 reduce.4
  383.1 1.6 fusion
  384.8 0.6 collective-permute-start.5
  385.7 3.2 collective-permute-done.5
  388.9 13.2 %gate_wgrad_keep.1.gate_ref = bf16[3,1024,512]{2,1,0:T(8,128)(2,1)} custom-call(s32[1]{0:T(128)} %bitcast.13.pos_ref.refs_0_, bf16[1024,2048]{1,0:T(8,128)(2,1)} %all-gather.4.cloned.1.call-done.x_ref.refs_1_, bf16[1024,2048]{1,0:T(8,128)(2,1)} %all-gather.8.cloned.1.call-done.refs_2_, bf16[1024,512]{1,0:T(8,128)(2,1)} %get-tuple-element.74.refs_3_.gg_ref, ...), custom_call_target="tpu_custom_call" | custom-call | flops 6442450944 | bytes 12582912 | tf_op jit(solution)/shard_map/gate_wgrad_keep/pallas_call | solution.py:286
  402.2 13.2 %conv_wgrad_keep.1.conv_ref = bf16[3,1024,512]{2,1,0:T(8,128)(2,1)} custom-call(s32[1]{0:T(128)} %bitcast.13.pos_ref.refs_0_, bf16[1024,2048]{1,0:T(8,128)(2,1)} %all-gather.4.cloned.1.call-done.x_ref.refs_1_, bf16[1024,2048]{1,0:T(8,128)(2,1)} %all-gather.8.cloned.1.call-done.refs_2_, bf16[1024,512]{1,0:T(8,128)(2,1)} %get-tuple-element.79.gc_ref.refs_3_, ...), custom_call_target="tpu_custom_call" | custom-call | flops 6442450944 | bytes 12582912 | tf_op jit(solution)/shard_map/conv_wgrad_keep/pallas_call | solution.py:286
  415.8 0.9 reduce-precision_convert_fusion.1
  416.7 1.7 reduce-precision_convert_fusion
  418.4 1.0 pad_maximum_fusion.1
  419.4 1.5 collective-permute-start.7
  420.9 10.2 %join_halves.1 = f32[3,512,2048]{2,1,0:T(8,128)} custom-call(s32[1]{0:T(128)} %bitcast.13.pos_ref.refs_0_, bf16[3,256,2048]{2,1,0:T(8,128)(2,1)} %copy-done.2, bf16[3,256,2048]{2,1,0:T(8,128)(2,1)} %collective-permute-done.10.got_ref), custom_call_target="tpu_custom_call" | custom-call | bytes 18874368 | tf_op jit(solution)/shard_map/join_halves/pallas_call | solution.py:799
  431.1 9.2 %place_input_grad.2.rest_0_ = f32[3,16384,128]{2,1,0:T(8,128)} custom-call(s32[1]{0:T(128)} %bitcast.13.pos_ref.refs_0_, bf16[3,1024,512]{2,1,0:T(8,128)(2,1)} %conv_wgrad_keep.1.conv_ref, bf16[3,1024,512]{2,1,0:T(8,128)(2,1)} %gate_wgrad_keep.1.gate_ref), custom_call_target="tpu_custom_call" | custom-call | bytes 18874368 | tf_op jit(solution)/shard_map/place_input_grad/pallas_call | solution.py:763
  440.3 2.4 collective-permute-done.7
  442.7 0.9 add_add_fusion
  443.6 1.4 collective-permute-start.11
  445.0 2.9 collective-permute-done.11
  448.0 4.9 %collective-permute-done.12 = f32[2,26,512]{2,1,0:T(8,128)S(1)} collective-permute-done((f32[2,26,512]{2,1,0:T(8,128)S(1)}, f32[2,26,512]{2,1,0:T(8,128)S(1)}, u32[]{:S(2)}, u32[]{:S(2)}) %collective-permute-start.12) | collective-permute-done | bytes 106528 | tf_op jit(solution)/shard_map/ppermute | solution.py:880
  453.0 0.7 collective-permute-start.13
  453.8 1.7 convert_add_fusion.1
  455.5 1.0 slice.133
  456.5 0.9 slice.134
  457.4 0.6 slice.135
  458.0 9.2 %place_input_grad.3 = f32[3,16384,128]{2,1,0:T(8,128)} custom-call(s32[1]{0:T(128)} %bitcast.15.pos_ref.refs_0_, bf16[3,1024,512]{2,1,0:T(8,128)(2,1)} %collective-permute-done.14.conv_ref, bf16[3,1024,512]{2,1,0:T(8,128)(2,1)} %collective-permute-done.15.gate_ref, f32[3,16384,128]{2,1,0:T(8,128)} %place_input_grad.2.rest_0_), custom_call_target="tpu_custom_call", output_to_operand_aliasing={{}: (3, {})} | custom-call | bytes 18874368 | tf_op jit(solution)/shard_map/place_input_grad/pallas_call | solution.py:763
  467.4 0.6 slice.130
  468.1 0.6 fusion.16
  469.0 0.6 copy.66
  469.6 0.7 copy.65
  470.4 1.6 fusion.7
  (97 shorter events, 4.1 us)
Async XLA Ops:
  7.2 161.5 %copy-start = (f32[16,4096]{1,0:T(8,128)S(1)}, f32[16,4096]{1,0:T(8,128)}, u32[]{:S(2)}) copy-start(f32[16,4096]{1,0:T(8,128)} %param.21) | copy-start | bytes 786436
  7.2 80.1 %all-gather.4.cloned.1.call-start = ((), (), s32[]{:S(2)}) async-start(), calls=%async_computation.6 | async-start | bytes 4718592 | tf_op jit(solution)/shard_map/all_gather | solution.py:924
  9.0 26.1 %copy-start.17 = (f32[128]{0:T(128)}, f32[128]{0:T(128)S(1)}, u32[]{:S(2)}) copy-start(f32[128]{0:T(128)S(1)} %get-tuple-element.113) | copy-start | bytes 1540
  11.1 76.3 %copy-start.15 = (s32[1,1024]{1,0:T(1,128)S(1)}, s32[1,1024]{1,0:T(1,128)}, u32[]{:S(2)}) copy-start(s32[1,1024]{1,0:T(1,128)} %modl_ref.3) | copy-start | bytes 12292
  11.1 187.0 %all-gather.6.cloned.1.call-start = ((), (), s32[]{:S(2)}) async-start(), calls=%async_computation.8 | async-start | bytes 4718592 | tf_op jit(solution)/shard_map/all_gather | solution.py:925
  11.2 24.0 %collective-permute-start.1 = (bf16[128,2048]{1,0:T(8,128)(2,1)}, bf16[128,2048]{1,0:T(8,128)(2,1)S(1)}, u32[]{:S(2)}, u32[]{:S(2)}) collective-permute-start(bf16[128,2048]{1,0:T(8,128)(2,1)} %fusion.3), channel_id=1, source_target_pairs={{0,16},{8,24},{16,0},{24,8},{1,17},{9,25},{17,1},{25,9},{2,18},{10... | collective-permute-start | bytes 1572872 | tf_op jit(solution)/shard_map/ppermute | solution.py:825
  14.2 21.0 %collective-permute-start = (s32[1,1024]{1,0:T(1,128)}, s32[1,1024]{1,0:T(1,128)S(1)}, u32[]{:S(2)}, u32[]{:S(2)}) collective-permute-start(s32[1,1024]{1,0:T(1,128)} %modl_ref.3), channel_id=1, source_target_pairs={{0,16},{8,24},{16,0},{24,8},{1,17},{9,25},{17,1},{25,9},{2,18},{10... | collective-permute-start | bytes 12296 | tf_op jit(solution)/shard_map/ppermute | solution.py:825
  35.2 83.0 %copy-start.7 = (bf16[128,2048]{1,0:T(8,128)(2,1)}, bf16[128,2048]{1,0:T(8,128)(2,1)S(1)}, u32[]{:S(2)}) copy-start(bf16[128,2048]{1,0:T(8,128)(2,1)S(1)} %collective-permute-done.1) | copy-start | bytes 1572868
  87.4 232.5 %all-gather.8.cloned.1.call-start = ((), (), s32[]{:S(2)}) async-start(), calls=%async_computation.9 | async-start | bytes 4718592 | tf_op jit(solution)/shard_map/all_gather | solution.py:937
  167.2 221.6 %reduce-scatter.3.cloned.1.call-start = ((), (), s32[]{:S(2)}) async-start(), calls=%async_computation.7 | async-start | bytes 4718592 | tf_op jit(solution)/shard_map/reduce_scatter | solution.py:942
  205.0 12.5 %collective-permute-start.2 = (bf16[3,256,2048]{2,1,0:T(8,128)(2,1)}, bf16[3,256,2048]{2,1,0:T(8,128)(2,1)S(1)}, u32[]{:S(2)}, u32[]{:S(2)}) collective-permute-start(bf16[3,256,2048]{2,1,0:T(8,128)(2,1)} %output_wgrad_send.1), channel_id=1, source_target_pairs={{0,8},{8,0},{16,24},{24,16},{1,9},{9,1},{17,25},{25,17},{2,10},{10... | collective-permute-start | bytes 9437192 | tf_op jit(solution)/shard_map/ppermute | solution.py:819
  217.5 1.7 copy-start.20
  226.6 75.2 %collective-permute-start.3 = (bf16[3,256,2048]{2,1,0:T(8,128)(2,1)}, bf16[3,256,2048]{2,1,0:T(8,128)(2,1)}, u32[]{:S(2)}, u32[]{:S(2)}) collective-permute-start(bf16[3,256,2048]{2,1,0:T(8,128)(2,1)} %output_wgrad_keep.1), channel_id=1, source_target_pairs={{0,16},{8,24},{16,0},{24,8},{1,17},{9,25},{17,1},{25,9},{2,18},{10... | collective-permute-start | bytes 9437192 | tf_op jit(solution)/shard_map/ppermute | solution.py:825
  286.9 14.9 %all-to-all-start.2 = ((bf16[8,160,128]{2,1,0:T(8,128)(2,1)}), bf16[8,160,128]{2,1,0:T(8,128)(2,1)S(1)}, u32[]{:S(2)}, u32[]{:S(2)}) async-start(bf16[8,160,128]{2,1,0:T(8,128)(2,1)} %get-tuple-element.71), calls=%async_computation.3 | async-start | bytes 655360 | tf_op jit(solution)/shard_map/all_to_all | solution.py:867
  290.3 29.5 %collective-permute-start.4 = (bf16[1024,512]{1,0:T(8,128)(2,1)}, bf16[1024,512]{1,0:T(8,128)(2,1)}, u32[]{:S(2)}, u32[]{:S(2)}) collective-permute-start(bf16[1024,512]{1,0:T(8,128)(2,1)} %get-tuple-element.74.refs_3_.gg_ref), channel_id=1, source_target_pairs={{0,16},{8,24},{16,0},{24,8},{1,17},{9,25},{17,1},{25,9},{2,18},{10... | collective-permute-start | bytes 3145736 | tf_op jit(solution)/shard_map/ppermute | solution.py:825
  306.3 79.1 %copy-start.2 = (bf16[3,256,2048]{2,1,0:T(8,128)(2,1)}, bf16[3,256,2048]{2,1,0:T(8,128)(2,1)S(1)}, u32[]{:S(2)}) copy-start(bf16[3,256,2048]{2,1,0:T(8,128)(2,1)S(1)} %add_convert_fusion.mine_ref) | copy-start | bytes 9437188
  307.1 25.0 %all-to-all-start.3 = ((bf16[8,160,128]{2,1,0:T(8,128)(2,1)}), bf16[8,160,128]{2,1,0:T(8,128)(2,1)S(1)}, u32[]{:S(2)}, u32[]{:S(2)}) async-start(bf16[8,160,128]{2,1,0:T(8,128)(2,1)} %broadcast_in_dim.32), calls=%async_computation.4 | async-start | bytes 655360 | tf_op jit(solution)/shard_map/all_to_all | solution.py:867
  310.6 147.4 %reduce-scatter.5.cloned.1.call-start = ((), (), s32[]{:S(2)}) async-start(), calls=%async_computation.10 | async-start | bytes 4718592 | tf_op jit(solution)/shard_map/reduce_scatter | solution.py:972
  332.1 0.7 copy-start.9
  344.4 25.1 %collective-permute-start.6 = (bf16[1024,512]{1,0:T(8,128)(2,1)}, bf16[1024,512]{1,0:T(8,128)(2,1)}, u32[]{:S(2)}, u32[]{:S(2)}) collective-permute-start(bf16[1024,512]{1,0:T(8,128)(2,1)} %get-tuple-element.79.gc_ref.refs_3_), channel_id=1, source_target_pairs={{0,16},{8,24},{16,0},{24,8},{1,17},{9,25},{17,1},{25,9},{2,18},{10... | collective-permute-start | bytes 3145736 | tf_op jit(solution)/shard_map/ppermute | solution.py:825
  364.2 18.1 %copy-start.14 = (f32[1,2048]{1,0:T(1,128)S(1)}, f32[1,2048]{1,0:T(1,128)}, u32[]{:S(2)}) copy-start(f32[1,2048]{1,0:T(1,128)} %get-tuple-element.86) | copy-start | bytes 24580
  364.2 18.7 %copy-start.11 = (f32[16,512]{1,0:T(8,128)S(1)}, f32[16,512]{1,0:T(8,128)}, u32[]{:S(2)}) copy-start(f32[16,512]{1,0:T(8,128)} %get-tuple-element.83) | copy-start | bytes 98308
  364.2 18.7 %copy-start.12 = (f32[8,512]{1,0:T(8,128)S(1)}, f32[8,512]{1,0:T(8,128)}, u32[]{:S(2)}) copy-start(f32[8,512]{1,0:T(8,128)} %get-tuple-element.84) | copy-start | bytes 49156
  364.2 18.7 %copy-start.13 = (f32[3,512]{1,0:T(4,128)S(1)}, f32[3,512]{1,0:T(4,128)}, u32[]{:S(2)}) copy-start(f32[3,512]{1,0:T(4,128)} %get-tuple-element.87) | copy-start | bytes 18436
  364.2 18.7 %copy-start.16 = (f32[1,512]{1,0:T(1,128)S(1)}, f32[1,512]{1,0:T(1,128)}, u32[]{:S(2)}) copy-start(f32[1,512]{1,0:T(1,128)} %get-tuple-element.85) | copy-start | bytes 6148
  364.3 24.6 %collective-permute-start.9 = (bf16[3,1024,512]{2,1,0:T(8,128)(2,1)}, bf16[3,1024,512]{2,1,0:T(8,128)(2,1)}, u32[]{:S(2)}, u32[]{:S(2)}) collective-permute-start(bf16[3,1024,512]{2,1,0:T(8,128)(2,1)} %gate_wgrad_send.1), channel_id=1, source_target_pairs={{0,8},{8,0},{16,24},{24,16},{1,9},{9,1},{17,25},{25,17},{2,10},{10... | collective-permute-start | bytes 9437192 | tf_op jit(solution)/shard_map/ppermute | solution.py:819
  381.7 20.4 %collective-permute-start.8 = (bf16[3,1024,512]{2,1,0:T(8,128)(2,1)}, bf16[3,1024,512]{2,1,0:T(8,128)(2,1)}, u32[]{:S(2)}, u32[]{:S(2)}) collective-permute-start(bf16[3,1024,512]{2,1,0:T(8,128)(2,1)} %conv_wgrad_send.1), channel_id=1, source_target_pairs={{0,8},{8,0},{16,24},{24,16},{1,9},{9,1},{17,25},{25,17},{2,10},{10... | collective-permute-start | bytes 9437192 | tf_op jit(solution)/shard_map/ppermute | solution.py:819
  384.8 0.9 copy-start.4
  384.8 4.1 collective-permute-start.5
  385.4 35.6 %collective-permute-start.10 = (bf16[3,256,2048]{2,1,0:T(8,128)(2,1)S(1)}, bf16[3,256,2048]{2,1,0:T(8,128)(2,1)}, u32[]{:S(2)}, u32[]{:S(2)}) collective-permute-start(bf16[3,256,2048]{2,1,0:T(8,128)(2,1)S(1)} %add_convert_fusion.mine_ref), channel_id=1, source_target_pairs={{0,8},{8,0},{16,24},{24,16},{1,9},{9,1},{17,25},{25,17},{2,10},{10... | collective-permute-start | bytes 9437192 | tf_op jit(solution)/shard_map/ppermute | solution.py:819
  402.1 55.9 %collective-permute-start.15 = (bf16[3,1024,512]{2,1,0:T(8,128)(2,1)}, bf16[3,1024,512]{2,1,0:T(8,128)(2,1)}, u32[]{:S(2)}, u32[]{:S(2)}) collective-permute-start(bf16[3,1024,512]{2,1,0:T(8,128)(2,1)} %gate_wgrad_keep.1.gate_ref), channel_id=1, source_target_pairs={{0,8},{8,0},{16,24},{24,16},{1,9},{9,1},{17,25},{25,17},{2,10},{10... | collective-permute-start | bytes 9437192 | tf_op jit(solution)/shard_map/ppermute | solution.py:819
  415.3 42.7 %collective-permute-start.14 = (bf16[3,1024,512]{2,1,0:T(8,128)(2,1)}, bf16[3,1024,512]{2,1,0:T(8,128)(2,1)}, u32[]{:S(2)}, u32[]{:S(2)}) collective-permute-start(bf16[3,1024,512]{2,1,0:T(8,128)(2,1)} %conv_wgrad_keep.1.conv_ref), channel_id=1, source_target_pairs={{0,8},{8,0},{16,24},{24,16},{1,9},{9,1},{17,25},{25,17},{2,10},{10... | collective-permute-start | bytes 9437192 | tf_op jit(solution)/shard_map/ppermute | solution.py:819
  419.4 23.3 %collective-permute-start.7 = (bf16[922,512]{1,0:T(8,128)(2,1)}, bf16[922,512]{1,0:T(8,128)(2,1)}, u32[]{:S(2)}, u32[]{:S(2)}) collective-permute-start(bf16[922,512]{1,0:T(8,128)(2,1)} %pad_maximum_fusion.1), channel_id=1, source_target_pairs={{0,16},{8,24},{16,0},{24,8},{1,17},{9,25},{17,1},{25,9},{2,18},{10... | collective-permute-start | bytes 2832392 | tf_op jit(solution)/shard_map/ppermute | solution.py:825
  443.6 4.3 collective-permute-start.11
  448.0 5.0 %collective-permute-start.12 = (f32[2,26,512]{2,1,0:T(8,128)S(1)}, f32[2,26,512]{2,1,0:T(8,128)S(1)}, u32[]{:S(2)}, u32[]{:S(2)}) collective-permute-start(f32[2,26,512]{2,1,0:T(8,128)S(1)} %pad_maximum_fusion.4), channel_id=1, source_target_pairs={{0,2},{1,3},{2,0},{3,1},{4,6},{5,7},{6,4},{7,5},{8,10},{9,11},{10,... | collective-permute-start | bytes 319496 | tf_op jit(solution)/shard_map/ppermute | solution.py:880
  453.0 14.2 %collective-permute-start.13 = (f32[4,26,512]{2,1,0:T(8,128)S(1)}, f32[4,26,512]{2,1,0:T(8,128)S(1)}, u32[]{:S(2)}, u32[]{:S(2)}) collective-permute-start(f32[4,26,512]{2,1,0:T(8,128)S(1)} %pad_maximum_fusion.3), channel_id=1, source_target_pairs={{0,4},{1,5},{2,6},{3,7},{4,0},{5,1},{6,2},{7,3},{8,12},{9,13},{10,... | collective-permute-start | bytes 638984 | tf_op jit(solution)/shard_map/ppermute | solution.py:880
  467.2 1.5 copy-start.3
  467.2 1.5 copy-start.6
  467.2 1.5 copy-start.10
  467.2 3.1 copy-start.5
  467.2 3.1 copy-start.8
  467.3 3.1 copy-start.18
  467.3 3.1 copy-start.19
  467.4 4.6 copy-start.1
Sparse Core Ops, SparseCore 0:
  11.2 76.0 all-gather.3
  89.5 84.3 all-gather.5
  176.6 72.4 all-gather.7
  252.6 89.9 reduce-scatter.2
  364.3 85.3 reduce-scatter.4

commit v4 on v3

--- a/solution.py
+++ b/solution.py
@@ -110,7 +110,7 @@
     full = lambda shape: pl.BlockSpec(shape, lambda j: (0,) * len(shape))
     col = lambda r: pl.BlockSpec((r, tc), lambda j: (0, j))
     return pl.pallas_call(
-        functools.partial(in_body, rows=rows, block=min(256, rows)),
+        functools.partial(in_body, rows=rows, block=min(512, rows)),
         grid=(tiles,),
         in_specs=[
             full((rows, width)),
@@ -158,7 +158,7 @@
         else pl.BlockSpec((M, depth, tn), lambda j: (0, 0, j))
     )
     return pl.pallas_call(
-        functools.partial(mm_body, rows=rows, block=min(512, rows), rhs_dim=1 if transposed else 0),
+        functools.partial(mm_body, rows=rows, block=min(1024, rows), rhs_dim=1 if transposed else 0),
         grid=(cols // tn,),
         in_specs=[
             pl.BlockSpec((rows, depth), lambda j: (0, 0)),
@@ -942,28 +942,27 @@
     branch = lax.psum_scatter(branch_part, "own", scatter_dimension=0, tiled=True)
     block_out = (resid + branch.astype(f32)).astype(bf16)[None]
 
+    gg, ggate = gated_grads(cot, output_proj, modc, scanned, gate)
+    ggates = [ggate] + y_others(ggate)
     gated_t = jnp.swapaxes(gated, 0, 1)
     groups = ((0, 1, 2),)
     out_got = [
         swap_core(value) for value in rows_wgrad(other_at, gated_t, cot, modl, [], groups, "output_wgrad_send")
     ]
-    out_half = rows_wgrad(core_at, gated_t, cot, modl, [after(value, branch_part) for value in out_got], groups, "output_wgrad_keep")
+    out_half = rows_wgrad(core_at, gated_t, cot, modl, [after(value, branch_part, ggate) for value in out_got], groups, "output_wgrad_keep")
     out_total = y_sum(out_half[0]).astype(bf16)
 
-    gg, ggate = gated_grads(after(cot, *out_half), output_proj, modc, scanned, gate)
-    ggates = [ggate] + y_others(ggate)
     gas, gpt, glogd, gskip, gbias, gstep = scan_backward(
         after(pj, branch_part, *out_half), act, gate, gg, delta, sig, prev, final, b_wide, c_wide, step_rows, decay, skip, modc, modr
     )
     gp_own = jnp.sum(to_owners(gpt.reshape(own_count, per_owner * psize, LANES)).astype(f32), axis=0).astype(bf16)
-    gp_own = after(gp_own, out_total)
     gp = to_all(gp_own).reshape(blocks, psize, LANES)
 
     ggates = [ggate] + [after(other, gp_own) for other in ggates[1:]]
     gate_send = half_wgrad(other_at, xs, ggates, modcs, None, "gate_wgrad_send")
     gate_got = swap_core(gate_send)
 
-    gp = after(gp, gate_send)
+    gp = after(gp, gate_send, out_total)
     gci, gstate, gcw = conv_backward(gp, sp_t, gas, conv_in, act, cw, cb, modc, modr)
     others = y_others(gci)
     gnormed, gain_part = input_dgrad(gci, ggate, w_in, modc, x, norm_gain.reshape(1, width))

time: 481 us -> 475 us (0.988)
    ppermute x6, waiting for transfers between devices: 16.5 us -> 11.3 us  [y_others(): lax.ppermute(value, 'batch', [(i, (i + shift) % count) for i in range(cou...]
where the time goes in v4:
time: 475 us; the launch traced here: 473 us
  Pallas kernels  248 us (52%)
  waiting for transfers between devices  85.1 us (18%)
  blocking collectives  48.7 us (10%)
  local copies, waits for them, and re-layouts  39.3 us (8%)
  starting transfers between devices  19.6 us (4%)
  other arithmetic  18.9 us (4%)
  between operations  14.3 us (3%)
    all_gather x1, waiting for transfers between devices, per_device(): x = lax.all_gather(normed, 'own', axis=0, tiled=True)  52.1 us
    pallas_call x4, Pallas kernels, half_wgrad(): pl.pallas_call(functools.partial(wgrad_body, sets=sets, add=got is not No...  51 us
    all_to_all x2, blocking collectives, to_owners(): lax.all_to_all(pieces, 'own', split_axis=0, concat_axis=0, tiled=False)  48.7 us
    pallas_call x1, Pallas kernels, scan_backward(): pl.pallas_call(scan_bwd_body, grid=(blocks,), in_specs=[slab(pj.shape[1:]...  46.3 us
    pallas_call x1, Pallas kernels, scan_forward(): pl.pallas_call(scan_fwd_body, grid=(blocks,), in_specs=[pl.BlockSpec((1,)...  26.5 us
    pallas_call x1, Pallas kernels, input_stage(): pl.pallas_call(functools.partial(in_body, rows=rows, block=min(512, rows)...  26.4 us
    reshape x1, local copies, waits for them, and re-layouts, per_device(): w_in = input_proj.reshape(M, width, 2 * chans)  20.9 us
    pallas_call x2, Pallas kernels, place_input_grad(): pl.pallas_call(body, grid_spec=pltpu.PrefetchScalarGridSpec(num_scalar_pr...  18.4 us
  transfers between devices with their start and end apart: 23, of which 8 were waited for; matrix products, arithmetic and copies ran while one was open for 10% of the time, Pallas kernels for 52%

profile of v4, /device:TPU:0, one launch (start us, length us, event | category | flops | bytes accessed | tf_op | source)
XLA Modules:
  0.0 473.2 jit_solution(13508393143645624225)
XLA Ops:
  7.2 1.3 fusion.1
  9.0 2.0 fusion.3
  11.2 3.0 collective-permute-start.1
  14.3 20.9 %reshape.117.wc_ref.wg_ref.w_ref = bf16[3,2048,1024]{2,1,0:T(8,128)(2,1)} reshape(bf16[3,2048,2,512]{3,2,1,0:T(2,128)(2,1)} %param.15) | data formatting | bytes 25165824 | tf_op jit(solution)/shard_map/reshape | solution.py:911
  35.2 52.1 %all-gather.4.cloned.1.call-done.x_ref.refs_1_ = bf16[1024,2048]{1,0:T(8,128)(2,1)} async-done(((bf16[128,2048]{1,0:T(8,128)(2,1)}), bf16[1024,2048]{1,0:T(8,128)(2,1)}) %all-gather.4.cloned.1.call-update) | async-done | bytes 4194320 | tf_op jit(solution)/shard_map/all_gather | solution.py:924
  87.4 1.0 copy.47.modc_ref.refs_5_
  88.5 1.3 dynamic_slice.13
  89.8 1.3 constant_dynamic-slice_fusion.1.cw_ref
  91.1 26.4 %input_stage.1 = (bf16[1024,512]{1,0:T(8,128)(2,1)}, bf16[1024,512]{1,0:T(8,128)(2,1)}, bf16[1024,512]{1,0:T(8,128)(2,1)}, bf16[8,160,128]{2,1,0:T(8,128)(2,1)}) custom-call(bf16[1024,2048]{1,0:T(8,128)(2,1)} %all-gather.4.cloned.1.call-done.x_ref.refs_1_, bf16[3,2048,1024]{2,1,0:T(8,128)(2,1)} %reshape.117.wc_ref.wg_ref.w_ref, ...), custom_call_target="tpu_custom_call" | custom-call | flops 12884901888 | bytes 16777216 | tf_op jit(solution)/shard_map/input_stage/pallas_call | solution.py:112
  117.5 22.2 %all_to_all.20 = bf16[8,160,128]{2,1,0:T(8,128)(2,1)S(1)} all-to-all(bf16[8,160,128]{2,1,0:T(8,128)(2,1)} %get-tuple-element.53), channel_id=1, replica_groups=mesh['batch'=4,'own'=8] {'own'}, dimensions={0} | all-to-all | bytes 655360 | tf_op jit(solution)/shard_map/all_to_all | solution.py:867
  139.9 26.4 %all_to_all.21 = bf16[8,1,192,128]{3,2,1,0:T(8,128)(2,1)} all-to-all(bf16[8,1,192,128]{3,2,1,0:T(8,128)(2,1)S(1)} %broadcast_in_dim.30), channel_id=1, replica_groups=mesh['batch'=4,'own'=8] {'own'}, dimensions={0} | all-to-all | bytes 786432 | tf_op jit(solution)/shard_map/all_to_all | solution.py:867
  166.5 1.3 dynamic_slice.15
  167.9 0.6 constant_dynamic-slice_fusion.ld_ref
  168.5 26.5 %scan_forward.1 = (bf16[1024,512]{1,0:T(8,128)(2,1)}, f32[1024,512]{1,0:T(8,128)}, bf16[1024,512]{1,0:T(8,128)(2,1)}, f32[1024,512]{1,0:T(8,128)}, f32[16384,512...) custom-call(bf16[8,192,128]{2,1,0:T(8,128)(2,1)} %bitcast.64, ...), custom_call_target="tpu_custom_call" | custom-call | flops 40000000000 | bytes 44040192 | tf_op jit(solution)/shard_map/scan_forward/pallas_call | solution.py:450
  195.0 2.3 copy.50
  197.3 6.9 %output_wgrad_send.1 = bf16[3,256,2048]{2,1,0:T(8,128)(2,1)} custom-call(s32[1]{0:T(128)} %bitcast.15.pos_ref.refs_0_, bf16[512,1024]{1,0:T(8,128)(2,1)} %bitcast.58, bf16[1024,2048]{1,0:T(8,128)(2,1)} %all-gather.6.cloned.1.call-done.g_ref.x_ref, s32[1,1024]{1,0:T(1,128)} %modl_ref.3), custom_call_target="tpu_custom_call" | custom-call | flops 3221225472 | bytes 11010048 | tf_op jit(solution)/shard_map/output_wgrad_send/pallas_call | solution.py:320
  204.2 11.8 %output_stage.1 = bf16[1024,2048]{1,0:T(8,128)(2,1)} custom-call(bf16[1024,512]{1,0:T(8,128)(2,1)} %get-tuple-element.56.x_ref, bf16[3,512,2048]{2,1,0:T(8,128)(2,1)} %w_ref.3, s32[1024,1]{1,0:T(8,128)} %copy.47.modc_ref.refs_5_), custom_call_target="tpu_custom_call" | custom-call | flops 6442450944 | bytes 11534336 | tf_op jit(solution)/shard_map/output_stage/pallas_call | solution.py:160
  216.0 12.5 %gated_grads.1 = (bf16[1024,512]{1,0:T(8,128)(2,1)}, bf16[1024,512]{1,0:T(8,128)(2,1)}) custom-call(bf16[1024,2048]{1,0:T(8,128)(2,1)} %all-gather.6.cloned.1.call-done.g_ref.x_ref, bf16[3,512,2048]{2,1,0:T(8,128)(2,1)} %w_ref.3, s32[1024,1]{1,0:T(8,128)} %copy.47.modc_ref.refs_5_, f32[1024,512]{1,0:T(8,128)} %get-tuple-element.58.scanned_ref, ...), custom_call_target="tpu_custom_call" | custom-call | flops 6442450944 | bytes 15728640 | tf_op jit(solution)/shard_map/gated_grads/pallas_call | solution.py:196
  228.5 1.4 collective-permute-start.3
  229.9 1.7 copy-done.20
  231.6 7.4 %output_wgrad_keep.1 = bf16[3,256,2048]{2,1,0:T(8,128)(2,1)} custom-call(s32[1]{0:T(128)} %bitcast.13.pos_ref.refs_0_, bf16[512,1024]{1,0:T(8,128)(2,1)} %bitcast.59, bf16[1024,2048]{1,0:T(8,128)(2,1)} %all-gather.6.cloned.1.call-done.g_ref.x_ref, s32[1,1024]{1,0:T(1,128)} %modl_ref.3, bf16[3,256,2048]{2,1,0:T(8,128)(2,1)} %copy-done.20), custom_call_target="tpu_custom_call" | custom-call | flops 3221225472 | bytes 11010048 | tf_op jit(solution)/shard_map/output_wgrad_keep/pallas_call | solution.py:320
  239.0 0.6 collective-permute-start.4
  239.7 46.3 %scan_backward.1 = (bf16[1024,512]{1,0:T(8,128)(2,1)}, bf16[8,160,128]{2,1,0:T(8,128)(2,1)}, f32[16,512]{1,0:T(8,128)}, f32[1,512]{1,0:T(1,128)}, f32[3,512]{1,0:T(4,128)}, /*index=5*/f32[384,512]{1,0:T(8,128)}) custom-call(bf16[8,192,128]{2,1,0:T(8,128)(2,1)} %bitcast.65, bf16[1024,512]{1,0:T(8,128)(2,1)} %get-tuple-element.54.act_ref, ...), custom_call_target="tpu_custom_call" | custom-call | flops 60000002048 | bytes 44040192 | tf_op jit(solution)/shard_map/scan_backward/pallas_call | solution.py:601
  285.9 3.4 all-to-all-start.2
  289.4 1.0 copy.54.refs_6_
  290.4 10.5 %all-to-all-done.2 = bf16[8,160,128]{2,1,0:T(8,128)(2,1)S(1)} async-done(((bf16[8,160,128]{2,1,0:T(8,128)(2,1)}), bf16[8,160,128]{2,1,0:T(8,128)(2,1)S(1)}, u32[]{:S(2)}, u32[]{:S(2)}) %all-to-all-start.2) | async-done | bytes 327712 | tf_op jit(solution)/shard_map/all_to_all | solution.py:867
  300.9 0.8 broadcast_in_dim.32
  301.7 3.6 all-to-all-start.3
  305.6 12.4 %gate_wgrad_send.1 = bf16[3,1024,512]{2,1,0:T(8,128)(2,1)} custom-call(s32[1]{0:T(128)} %bitcast.15.pos_ref.refs_0_, bf16[1024,2048]{1,0:T(8,128)(2,1)} %all-gather.4.cloned.1.call-done.x_ref.refs_1_, bf16[1024,2048]{1,0:T(8,128)(2,1)} %all-gather.8.cloned.1.call-done.refs_2_, bf16[1024,512]{1,0:T(8,128)(2,1)} %get-tuple-element.59.refs_3_.gg_ref, ...), custom_call_target="tpu_custom_call" | custom-call | flops 6442450944 | bytes 12582912 | tf_op jit(solution)/shard_map/gate_wgrad_send/pallas_call | solution.py:286
  318.0 3.8 collective-permute-done.4
  321.8 4.4 add_convert_fusion.mine_ref
  326.2 0.8 copy-done.9
  327.0 11.9 %conv_backward.1 = (bf16[1024,512]{1,0:T(8,128)(2,1)}, f32[3,160,512]{2,1,0:T(8,128)}, f32[8,512]{1,0:T(8,128)}) custom-call(bf16[8,160,128]{2,1,0:T(8,128)(2,1)} %copy-done.9, bf16[3,160,512]{2,1,0:T(8,128)(2,1)} %bitcast.85, bf16[1024,512]{1,0:T(8,128)(2,1)} %get-tuple-element.73.gas_ref, bf16[1024,512]{1,0:T(8,128)(2,1)} %get-tuple-element.74.ci_ref, ...), custom_call_target="tpu_custom_call" | custom-call | flops 2013265920 | bytes 5242880 | tf_op jit(solution)/shard_map/conv_backward/pallas_call | solution.py:699
  338.9 1.6 collective-permute-start.6
  340.5 18.3 %input_dgrad.1 = (bf16[1024,2048]{1,0:T(8,128)(2,1)}, f32[1,2048]{1,0:T(1,128)}) custom-call(bf16[1024,512]{1,0:T(8,128)(2,1)} %get-tuple-element.75.gc_ref.refs_3_, bf16[1024,512]{1,0:T(8,128)(2,1)} %get-tuple-element.59.refs_3_.gg_ref, bf16[3,2048,1024]{2,1,0:T(8,128)(2,1)} %reshape.117.wc_ref.wg_ref.w_ref, s32[1024,1]{1,0:T(8,128)} %copy.47.modc_ref.refs_5_, ...), custom_call_target="tpu_custom_call" | custom-call | flops 12884901888 | bytes 23068672 | tf_op jit(solution)/shard_map/input_dgrad/pallas_call | solution.py:235
  358.9 5.2 %collective-permute-done.6.refs_4_ = bf16[1024,512]{1,0:T(8,128)(2,1)} collective-permute-done((bf16[1024,512]{1,0:T(8,128)(2,1)}, bf16[1024,512]{1,0:T(8,128)(2,1)}, u32[]{:S(2)}, u32[]{:S(2)}) %collective-permute-start.6) | collective-permute-done | bytes 1048608 | tf_op jit(solution)/shard_map/ppermute | solution.py:825
  364.1 12.3 %conv_wgrad_send.1 = bf16[3,1024,512]{2,1,0:T(8,128)(2,1)} custom-call(s32[1]{0:T(128)} %bitcast.15.pos_ref.refs_0_, bf16[1024,2048]{1,0:T(8,128)(2,1)} %all-gather.4.cloned.1.call-done.x_ref.refs_1_, bf16[1024,2048]{1,0:T(8,128)(2,1)} %all-gather.8.cloned.1.call-done.refs_2_, bf16[1024,512]{1,0:T(8,128)(2,1)} %get-tuple-element.75.gc_ref.refs_3_, ...), custom_call_target="tpu_custom_call" | custom-call | flops 6442450944 | bytes 12582912 | tf_op jit(solution)/shard_map/conv_wgrad_send/pallas_call | solution.py:286
  376.9 0.7 reduce.4
  377.7 1.6 fusion
  380.3 3.2 collective-permute-done.5
  383.5 13.2 %gate_wgrad_keep.1.gate_ref = bf16[3,1024,512]{2,1,0:T(8,128)(2,1)} custom-call(s32[1]{0:T(128)} %bitcast.13.pos_ref.refs_0_, bf16[1024,2048]{1,0:T(8,128)(2,1)} %all-gather.4.cloned.1.call-done.x_ref.refs_1_, bf16[1024,2048]{1,0:T(8,128)(2,1)} %all-gather.8.cloned.1.call-done.refs_2_, bf16[1024,512]{1,0:T(8,128)(2,1)} %get-tuple-element.59.refs_3_.gg_ref, ...), custom_call_target="tpu_custom_call" | custom-call | flops 6442450944 | bytes 12582912 | tf_op jit(solution)/shard_map/gate_wgrad_keep/pallas_call | solution.py:286
  396.8 13.2 %conv_wgrad_keep.1.conv_ref = bf16[3,1024,512]{2,1,0:T(8,128)(2,1)} custom-call(s32[1]{0:T(128)} %bitcast.13.pos_ref.refs_0_, bf16[1024,2048]{1,0:T(8,128)(2,1)} %all-gather.4.cloned.1.call-done.x_ref.refs_1_, bf16[1024,2048]{1,0:T(8,128)(2,1)} %all-gather.8.cloned.1.call-done.refs_2_, bf16[1024,512]{1,0:T(8,128)(2,1)} %get-tuple-element.75.gc_ref.refs_3_, ...), custom_call_target="tpu_custom_call" | custom-call | flops 6442450944 | bytes 12582912 | tf_op jit(solution)/shard_map/conv_wgrad_keep/pallas_call | solution.py:286
  410.4 0.9 reduce-precision_convert_fusion.1
  411.3 1.7 reduce-precision_convert_fusion
  413.0 1.0 pad_maximum_fusion.1
  414.0 1.6 collective-permute-start.7
  415.6 10.2 %join_halves.1 = f32[3,512,2048]{2,1,0:T(8,128)} custom-call(s32[1]{0:T(128)} %bitcast.13.pos_ref.refs_0_, bf16[3,256,2048]{2,1,0:T(8,128)(2,1)} %copy-done.2, bf16[3,256,2048]{2,1,0:T(8,128)(2,1)} %collective-permute-done.10.got_ref), custom_call_target="tpu_custom_call" | custom-call | bytes 18874368 | tf_op jit(solution)/shard_map/join_halves/pallas_call | solution.py:799
  425.7 9.2 %place_input_grad.2.rest_0_ = f32[3,16384,128]{2,1,0:T(8,128)} custom-call(s32[1]{0:T(128)} %bitcast.13.pos_ref.refs_0_, bf16[3,1024,512]{2,1,0:T(8,128)(2,1)} %conv_wgrad_keep.1.conv_ref, bf16[3,1024,512]{2,1,0:T(8,128)(2,1)} %gate_wgrad_keep.1.gate_ref), custom_call_target="tpu_custom_call" | custom-call | bytes 18874368 | tf_op jit(solution)/shard_map/place_input_grad/pallas_call | solution.py:763
  434.9 2.4 collective-permute-done.7
  437.3 0.9 add_add_fusion
  438.2 1.5 collective-permute-start.11
  439.7 2.8 collective-permute-done.11
  442.6 4.9 %collective-permute-done.12 = f32[2,26,512]{2,1,0:T(8,128)S(1)} collective-permute-done((f32[2,26,512]{2,1,0:T(8,128)S(1)}, f32[2,26,512]{2,1,0:T(8,128)S(1)}, u32[]{:S(2)}, u32[]{:S(2)}) %collective-permute-start.12) | collective-permute-done | bytes 106528 | tf_op jit(solution)/shard_map/ppermute | solution.py:880
  447.6 0.8 collective-permute-start.13
  448.5 1.7 convert_add_fusion.1
  450.2 1.0 slice.133
  451.2 0.9 slice.134
  452.1 0.6 slice.135
  452.7 9.2 %place_input_grad.3 = f32[3,16384,128]{2,1,0:T(8,128)} custom-call(s32[1]{0:T(128)} %bitcast.15.pos_ref.refs_0_, bf16[3,1024,512]{2,1,0:T(8,128)(2,1)} %collective-permute-done.14.conv_ref, bf16[3,1024,512]{2,1,0:T(8,128)(2,1)} %collective-permute-done.15.gate_ref, f32[3,16384,128]{2,1,0:T(8,128)} %place_input_grad.2.rest_0_), custom_call_target="tpu_custom_call", output_to_operand_aliasing={{}: (3, {})} | custom-call | bytes 18874368 | tf_op jit(solution)/shard_map/place_input_grad/pallas_call | solution.py:763
  462.1 0.6 slice.130
  462.8 0.6 fusion.16
  463.7 0.6 copy.66
  464.3 0.7 copy.65
  465.1 1.6 fusion.7
  (97 shorter events, 4.4 us)
Async XLA Ops:
  7.2 160.7 %copy-start = (f32[16,4096]{1,0:T(8,128)S(1)}, f32[16,4096]{1,0:T(8,128)}, u32[]{:S(2)}) copy-start(f32[16,4096]{1,0:T(8,128)} %param.21) | copy-start | bytes 786436
  7.2 80.1 %all-gather.4.cloned.1.call-start = ((), (), s32[]{:S(2)}) async-start(), calls=%async_computation.6 | async-start | bytes 4718592 | tf_op jit(solution)/shard_map/all_gather | solution.py:924
  9.0 26.1 %copy-start.17 = (f32[128]{0:T(128)}, f32[128]{0:T(128)S(1)}, u32[]{:S(2)}) copy-start(f32[128]{0:T(128)S(1)} %get-tuple-element.109) | copy-start | bytes 1540
  11.1 76.3 %copy-start.15 = (s32[1,1024]{1,0:T(1,128)S(1)}, s32[1,1024]{1,0:T(1,128)}, u32[]{:S(2)}) copy-start(s32[1,1024]{1,0:T(1,128)} %modl_ref.3) | copy-start | bytes 12292
  11.1 186.2 %all-gather.6.cloned.1.call-start = ((), (), s32[]{:S(2)}) async-start(), calls=%async_computation.8 | async-start | bytes 4718592 | tf_op jit(solution)/shard_map/all_gather | solution.py:925
  11.2 24.0 %collective-permute-start.1 = (bf16[128,2048]{1,0:T(8,128)(2,1)}, bf16[128,2048]{1,0:T(8,128)(2,1)S(1)}, u32[]{:S(2)}, u32[]{:S(2)}) collective-permute-start(bf16[128,2048]{1,0:T(8,128)(2,1)} %fusion.3), channel_id=1, source_target_pairs={{0,16},{8,24},{16,0},{24,8},{1,17},{9,25},{17,1},{25,9},{2,18},{10... | collective-permute-start | bytes 1572872 | tf_op jit(solution)/shard_map/ppermute | solution.py:825
  14.2 21.0 %collective-permute-start = (s32[1,1024]{1,0:T(1,128)}, s32[1,1024]{1,0:T(1,128)S(1)}, u32[]{:S(2)}, u32[]{:S(2)}) collective-permute-start(s32[1,1024]{1,0:T(1,128)} %modl_ref.3), channel_id=1, source_target_pairs={{0,16},{8,24},{16,0},{24,8},{1,17},{9,25},{17,1},{25,9},{2,18},{10... | collective-permute-start | bytes 12296 | tf_op jit(solution)/shard_map/ppermute | solution.py:825
  35.2 82.3 %copy-start.7 = (bf16[128,2048]{1,0:T(8,128)(2,1)}, bf16[128,2048]{1,0:T(8,128)(2,1)S(1)}, u32[]{:S(2)}) copy-start(bf16[128,2048]{1,0:T(8,128)(2,1)S(1)} %collective-permute-done.1) | copy-start | bytes 1572868
  87.4 218.2 %all-gather.8.cloned.1.call-start = ((), (), s32[]{:S(2)}) async-start(), calls=%async_computation.9 | async-start | bytes 4718592 | tf_op jit(solution)/shard_map/all_gather | solution.py:937
  166.3 217.2 %reduce-scatter.3.cloned.1.call-start = ((), (), s32[]{:S(2)}) async-start(), calls=%async_computation.7 | async-start | bytes 4718592 | tf_op jit(solution)/shard_map/reduce_scatter | solution.py:942
  204.2 25.7 %collective-permute-start.2 = (bf16[3,256,2048]{2,1,0:T(8,128)(2,1)}, bf16[3,256,2048]{2,1,0:T(8,128)(2,1)S(1)}, u32[]{:S(2)}, u32[]{:S(2)}) collective-permute-start(bf16[3,256,2048]{2,1,0:T(8,128)(2,1)} %output_wgrad_send.1), channel_id=1, source_target_pairs={{0,8},{8,0},{16,24},{24,16},{1,9},{9,1},{17,25},{25,17},{2,10},{10... | collective-permute-start | bytes 9437192 | tf_op jit(solution)/shard_map/ppermute | solution.py:819
  228.5 77.0 %collective-permute-start.3 = (bf16[1024,512]{1,0:T(8,128)(2,1)}, bf16[1024,512]{1,0:T(8,128)(2,1)}, u32[]{:S(2)}, u32[]{:S(2)}) collective-permute-start(bf16[1024,512]{1,0:T(8,128)(2,1)} %get-tuple-element.59.refs_3_.gg_ref), channel_id=1, source_target_pairs={{0,16},{8,24},{16,0},{24,8},{1,17},{9,25},{17,1},{25,9},{2,18},{10... | collective-permute-start | bytes 3145736 | tf_op jit(solution)/shard_map/ppermute | solution.py:825
  229.9 1.7 copy-start.20
  239.0 82.8 %collective-permute-start.4 = (bf16[3,256,2048]{2,1,0:T(8,128)(2,1)}, bf16[3,256,2048]{2,1,0:T(8,128)(2,1)}, u32[]{:S(2)}, u32[]{:S(2)}) collective-permute-start(bf16[3,256,2048]{2,1,0:T(8,128)(2,1)} %output_wgrad_keep.1), channel_id=1, source_target_pairs={{0,16},{8,24},{16,0},{24,8},{1,17},{9,25},{17,1},{25,9},{2,18},{10... | collective-permute-start | bytes 9437192 | tf_op jit(solution)/shard_map/ppermute | solution.py:825
  285.9 15.0 %all-to-all-start.2 = ((bf16[8,160,128]{2,1,0:T(8,128)(2,1)}), bf16[8,160,128]{2,1,0:T(8,128)(2,1)S(1)}, u32[]{:S(2)}, u32[]{:S(2)}) async-start(bf16[8,160,128]{2,1,0:T(8,128)(2,1)} %get-tuple-element.69), calls=%async_computation.3 | async-start | bytes 655360 | tf_op jit(solution)/shard_map/all_to_all | solution.py:867
  301.7 24.5 %all-to-all-start.3 = ((bf16[8,160,128]{2,1,0:T(8,128)(2,1)}), bf16[8,160,128]{2,1,0:T(8,128)(2,1)S(1)}, u32[]{:S(2)}, u32[]{:S(2)}) async-start(bf16[8,160,128]{2,1,0:T(8,128)(2,1)} %broadcast_in_dim.32), calls=%async_computation.4 | async-start | bytes 655360 | tf_op jit(solution)/shard_map/all_to_all | solution.py:867
  305.3 147.4 %reduce-scatter.5.cloned.1.call-start = ((), (), s32[]{:S(2)}) async-start(), calls=%async_computation.10 | async-start | bytes 4718592 | tf_op jit(solution)/shard_map/reduce_scatter | solution.py:971
  326.2 53.8 %copy-start.2 = (bf16[3,256,2048]{2,1,0:T(8,128)(2,1)}, bf16[3,256,2048]{2,1,0:T(8,128)(2,1)S(1)}, u32[]{:S(2)}) copy-start(bf16[3,256,2048]{2,1,0:T(8,128)(2,1)S(1)} %add_convert_fusion.mine_ref) | copy-start | bytes 9437188
  326.2 0.8 copy-start.9
  338.9 25.2 %collective-permute-start.6 = (bf16[1024,512]{1,0:T(8,128)(2,1)}, bf16[1024,512]{1,0:T(8,128)(2,1)}, u32[]{:S(2)}, u32[]{:S(2)}) collective-permute-start(bf16[1024,512]{1,0:T(8,128)(2,1)} %get-tuple-element.75.gc_ref.refs_3_), channel_id=1, source_target_pairs={{0,16},{8,24},{16,0},{24,8},{1,17},{9,25},{17,1},{25,9},{2,18},{10... | collective-permute-start | bytes 3145736 | tf_op jit(solution)/shard_map/ppermute | solution.py:825
  358.8 18.1 %copy-start.14 = (f32[1,2048]{1,0:T(1,128)S(1)}, f32[1,2048]{1,0:T(1,128)}, u32[]{:S(2)}) copy-start(f32[1,2048]{1,0:T(1,128)} %get-tuple-element.82) | copy-start | bytes 24580
  358.8 18.7 %copy-start.11 = (f32[16,512]{1,0:T(8,128)S(1)}, f32[16,512]{1,0:T(8,128)}, u32[]{:S(2)}) copy-start(f32[16,512]{1,0:T(8,128)} %get-tuple-element.79) | copy-start | bytes 98308
  358.8 18.7 %copy-start.12 = (f32[8,512]{1,0:T(8,128)S(1)}, f32[8,512]{1,0:T(8,128)}, u32[]{:S(2)}) copy-start(f32[8,512]{1,0:T(8,128)} %get-tuple-element.80) | copy-start | bytes 49156
  358.8 18.7 %copy-start.13 = (f32[3,512]{1,0:T(4,128)S(1)}, f32[3,512]{1,0:T(4,128)}, u32[]{:S(2)}) copy-start(f32[3,512]{1,0:T(4,128)} %get-tuple-element.83) | copy-start | bytes 18436
  358.9 18.7 %copy-start.16 = (f32[1,512]{1,0:T(1,128)S(1)}, f32[1,512]{1,0:T(1,128)}, u32[]{:S(2)}) copy-start(f32[1,512]{1,0:T(1,128)} %get-tuple-element.81) | copy-start | bytes 6148
  358.9 24.6 %collective-permute-start.9 = (bf16[3,1024,512]{2,1,0:T(8,128)(2,1)}, bf16[3,1024,512]{2,1,0:T(8,128)(2,1)}, u32[]{:S(2)}, u32[]{:S(2)}) collective-permute-start(bf16[3,1024,512]{2,1,0:T(8,128)(2,1)} %gate_wgrad_send.1), channel_id=1, source_target_pairs={{0,8},{8,0},{16,24},{24,16},{1,9},{9,1},{17,25},{25,17},{2,10},{10... | collective-permute-start | bytes 9437192 | tf_op jit(solution)/shard_map/ppermute | solution.py:819
  376.3 20.4 %collective-permute-start.8 = (bf16[3,1024,512]{2,1,0:T(8,128)(2,1)}, bf16[3,1024,512]{2,1,0:T(8,128)(2,1)}, u32[]{:S(2)}, u32[]{:S(2)}) collective-permute-start(bf16[3,1024,512]{2,1,0:T(8,128)(2,1)} %conv_wgrad_send.1), channel_id=1, source_target_pairs={{0,8},{8,0},{16,24},{24,16},{1,9},{9,1},{17,25},{25,17},{2,10},{10... | collective-permute-start | bytes 9437192 | tf_op jit(solution)/shard_map/ppermute | solution.py:819
  379.4 0.9 copy-start.4
  379.4 4.1 collective-permute-start.5
  380.0 35.6 %collective-permute-start.10 = (bf16[3,256,2048]{2,1,0:T(8,128)(2,1)S(1)}, bf16[3,256,2048]{2,1,0:T(8,128)(2,1)}, u32[]{:S(2)}, u32[]{:S(2)}) collective-permute-start(bf16[3,256,2048]{2,1,0:T(8,128)(2,1)S(1)} %add_convert_fusion.mine_ref), channel_id=1, source_target_pairs={{0,8},{8,0},{16,24},{24,16},{1,9},{9,1},{17,25},{25,17},{2,10},{10... | collective-permute-start | bytes 9437192 | tf_op jit(solution)/shard_map/ppermute | solution.py:819
  396.7 56.0 %collective-permute-start.15 = (bf16[3,1024,512]{2,1,0:T(8,128)(2,1)}, bf16[3,1024,512]{2,1,0:T(8,128)(2,1)}, u32[]{:S(2)}, u32[]{:S(2)}) collective-permute-start(bf16[3,1024,512]{2,1,0:T(8,128)(2,1)} %gate_wgrad_keep.1.gate_ref), channel_id=1, source_target_pairs={{0,8},{8,0},{16,24},{24,16},{1,9},{9,1},{17,25},{25,17},{2,10},{10... | collective-permute-start | bytes 9437192 | tf_op jit(solution)/shard_map/ppermute | solution.py:819
  409.9 42.8 %collective-permute-start.14 = (bf16[3,1024,512]{2,1,0:T(8,128)(2,1)}, bf16[3,1024,512]{2,1,0:T(8,128)(2,1)}, u32[]{:S(2)}, u32[]{:S(2)}) collective-permute-start(bf16[3,1024,512]{2,1,0:T(8,128)(2,1)} %conv_wgrad_keep.1.conv_ref), channel_id=1, source_target_pairs={{0,8},{8,0},{16,24},{24,16},{1,9},{9,1},{17,25},{25,17},{2,10},{10... | collective-permute-start | bytes 9437192 | tf_op jit(solution)/shard_map/ppermute | solution.py:819
  414.0 23.3 %collective-permute-start.7 = (bf16[922,512]{1,0:T(8,128)(2,1)}, bf16[922,512]{1,0:T(8,128)(2,1)}, u32[]{:S(2)}, u32[]{:S(2)}) collective-permute-start(bf16[922,512]{1,0:T(8,128)(2,1)} %pad_maximum_fusion.1), channel_id=1, source_target_pairs={{0,16},{8,24},{16,0},{24,8},{1,17},{9,25},{17,1},{25,9},{2,18},{10... | collective-permute-start | bytes 2832392 | tf_op jit(solution)/shard_map/ppermute | solution.py:825
  438.2 4.3 collective-permute-start.11
  442.6 5.0 %collective-permute-start.12 = (f32[2,26,512]{2,1,0:T(8,128)S(1)}, f32[2,26,512]{2,1,0:T(8,128)S(1)}, u32[]{:S(2)}, u32[]{:S(2)}) collective-permute-start(f32[2,26,512]{2,1,0:T(8,128)S(1)} %pad_maximum_fusion.4), channel_id=1, source_target_pairs={{0,2},{1,3},{2,0},{3,1},{4,6},{5,7},{6,4},{7,5},{8,10},{9,11},{10,... | collective-permute-start | bytes 319496 | tf_op jit(solution)/shard_map/ppermute | solution.py:880
  447.6 14.3 %collective-permute-start.13 = (f32[4,26,512]{2,1,0:T(8,128)S(1)}, f32[4,26,512]{2,1,0:T(8,128)S(1)}, u32[]{:S(2)}, u32[]{:S(2)}) collective-permute-start(f32[4,26,512]{2,1,0:T(8,128)S(1)} %pad_maximum_fusion.3), channel_id=1, source_target_pairs={{0,4},{1,5},{2,6},{3,7},{4,0},{5,1},{6,2},{7,3},{8,12},{9,13},{10,... | collective-permute-start | bytes 638984 | tf_op jit(solution)/shard_map/ppermute | solution.py:880
  461.9 1.5 copy-start.3
  461.9 1.5 copy-start.6
  461.9 1.5 copy-start.10
  461.9 3.1 copy-start.5
  462.0 3.1 copy-start.8
  462.0 3.1 copy-start.18
  462.0 3.1 copy-start.19
  462.1 4.6 copy-start.1
Sparse Core Ops, SparseCore 0:
  11.2 76.0 all-gather.3
  89.5 83.6 all-gather.5
  175.9 72.3 all-gather.7
  251.8 93.2 reduce-scatter.2
  358.9 85.5 reduce-scatter.4

commit v5 on v4

--- a/solution.py
+++ b/solution.py
@@ -550,13 +550,13 @@
             )
 
     def reads(i, _):
-        for j in range(UNROLL):
-            t = i * UNROLL + j
+        for j in range(8):
+            t = i * 8 + j
             at = pl.multiple_of(jnp.minimum(t + 1, span - 1) * 16, 16)
             read_grad(t, lambda h: prev_ref[pl.ds(at + 8 * h, 8), :])
         return 0
 
-    lax.fori_loop(0, span // UNROLL, reads, 0)
+    lax.fori_loop(0, span // 8, reads, 0)
     read_grad(span - 1, lambda h: later[8 * h : 8 * h + 8, :])
     later[...] = prev_ref[0:16, :]
 
@@ -826,8 +826,7 @@
     ]
 
 
-def y_sum(value, *before):
-    others = [after(other, *before) for other in y_others(value)]
+def y_sum(value, others):
     if len(others) == 1:
         return value.astype(f32) + others[0].astype(f32)
     chips = len(others) + 1
@@ -950,7 +949,7 @@
         swap_core(value) for value in rows_wgrad(other_at, gated_t, cot, modl, [], groups, "output_wgrad_send")
     ]
     out_half = rows_wgrad(core_at, gated_t, cot, modl, [after(value, branch_part, ggate) for value in out_got], groups, "output_wgrad_keep")
-    out_total = y_sum(out_half[0]).astype(bf16)
+    out_others = y_others(out_half[0])
 
     gas, gpt, glogd, gskip, gbias, gstep = scan_backward(
         after(pj, branch_part, *out_half), act, gate, gg, delta, sig, prev, final, b_wide, c_wide, step_rows, decay, skip, modc, modr
@@ -962,7 +961,8 @@
     gate_send = half_wgrad(other_at, xs, ggates, modcs, None, "gate_wgrad_send")
     gate_got = swap_core(gate_send)
 
-    gp = after(gp, gate_send, out_total)
+    gp = after(gp, gate_send, *out_others)
+    out_total = y_sum(out_half[0], out_others).astype(bf16)
     gci, gstate, gcw = conv_backward(gp, sp_t, gas, conv_in, act, cw, cb, modc, modr)
     others = y_others(gci)
     gnormed, gain_part = input_dgrad(gci, ggate, w_in, modc, x, norm_gain.reshape(1, width))

time: 475 us -> 473 us (level)
  transfers between devices with their start and end apart: 23 -> 23, of which waited for: 8 -> 8; matrix products, arithmetic and copies ran while one was open for 10% -> 10% of each run, Pallas kernels for 52% -> 53%
where the time goes in v5:
time: 473 us; the launch traced here: 471 us
  Pallas kernels  248 us (52%)
  waiting for transfers between devices  81 us (17%)
  blocking collectives  48.5 us (10%)
  local copies, waits for them, and re-layouts  39.8 us (8%)
  starting transfers between devices  20.8 us (4%)
  other arithmetic  18.3 us (4%)
  between operations  14.3 us (3%)
    all_gather x1, waiting for transfers between devices, per_device(): x = lax.all_gather(normed, 'own', axis=0, tiled=True)  52.1 us
    pallas_call x4, Pallas kernels, half_wgrad(): pl.pallas_call(functools.partial(wgrad_body, sets=sets, add=got is not No...  51.4 us
    all_to_all x2, blocking collectives, to_owners(): lax.all_to_all(pieces, 'own', split_axis=0, concat_axis=0, tiled=False)  48.5 us
    pallas_call x1, Pallas kernels, scan_backward(): pl.pallas_call(scan_bwd_body, grid=(blocks,), in_specs=[slab(pj.shape[1:]...  45.4 us
    pallas_call x1, Pallas kernels, scan_forward(): pl.pallas_call(scan_fwd_body, grid=(blocks,), in_specs=[pl.BlockSpec((1,)...  26.5 us
    pallas_call x1, Pallas kernels, input_stage(): pl.pallas_call(functools.partial(in_body, rows=rows, block=min(512, rows)...  26.4 us
    reshape x1, local copies, waits for them, and re-layouts, per_device(): w_in = input_proj.reshape(M, width, 2 * chans)  20.9 us
    pallas_call x2, Pallas kernels, place_input_grad(): pl.pallas_call(body, grid_spec=pltpu.PrefetchScalarGridSpec(num_scalar_pr...  18.4 us
  transfers between devices with their start and end apart: 23, of which 8 were waited for; matrix products, arithmetic and copies ran while one was open for 10% of the time, Pallas kernels for 53%

profile of v5, /device:TPU:0, one launch (start us, length us, event | category | flops | bytes accessed | tf_op | source)
XLA Modules:
  0.0 470.6 jit_solution(17906056991667582722)
XLA Ops:
  7.2 1.3 fusion.1
  8.5 0.6 multiply_multiply_fusion
  9.7 2.0 fusion.3
  11.8 3.0 collective-permute-start.1
  14.9 20.9 %reshape.117.wc_ref.wg_ref.w_ref = bf16[3,2048,1024]{2,1,0:T(8,128)(2,1)} reshape(bf16[3,2048,2,512]{3,2,1,0:T(2,128)(2,1)} %param.15) | data formatting | bytes 25165824 | tf_op jit(solution)/shard_map/reshape | solution.py:910
  35.8 52.1 %all-gather.4.cloned.1.call-done.x_ref.refs_1_ = bf16[1024,2048]{1,0:T(8,128)(2,1)} async-done(((bf16[128,2048]{1,0:T(8,128)(2,1)}), bf16[1024,2048]{1,0:T(8,128)(2,1)}) %all-gather.4.cloned.1.call-update) | async-done | bytes 4194320 | tf_op jit(solution)/shard_map/all_gather | solution.py:923
  88.1 1.0 copy.47.modc_ref.refs_5_
  89.1 1.3 dynamic_slice.13
  90.4 1.3 constant_dynamic-slice_fusion.1.cw_ref
  91.7 26.4 %input_stage.1 = (bf16[1024,512]{1,0:T(8,128)(2,1)}, bf16[1024,512]{1,0:T(8,128)(2,1)}, bf16[1024,512]{1,0:T(8,128)(2,1)}, bf16[8,160,128]{2,1,0:T(8,128)(2,1)}) custom-call(bf16[1024,2048]{1,0:T(8,128)(2,1)} %all-gather.4.cloned.1.call-done.x_ref.refs_1_, bf16[3,2048,1024]{2,1,0:T(8,128)(2,1)} %reshape.117.wc_ref.wg_ref.w_ref, ...), custom_call_target="tpu_custom_call" | custom-call | flops 12884901888 | bytes 16777216 | tf_op jit(solution)/shard_map/input_stage/pallas_call | solution.py:112
  118.1 22.2 %all_to_all.20 = bf16[8,160,128]{2,1,0:T(8,128)(2,1)S(1)} all-to-all(bf16[8,160,128]{2,1,0:T(8,128)(2,1)} %get-tuple-element.53), channel_id=1, replica_groups=mesh['batch'=4,'own'=8] {'own'}, dimensions={0} | all-to-all | bytes 655360 | tf_op jit(solution)/shard_map/all_to_all | solution.py:866
  140.5 26.3 %all_to_all.21 = bf16[8,1,192,128]{3,2,1,0:T(8,128)(2,1)} all-to-all(bf16[8,1,192,128]{3,2,1,0:T(8,128)(2,1)S(1)} %broadcast_in_dim.30), channel_id=1, replica_groups=mesh['batch'=4,'own'=8] {'own'}, dimensions={0} | all-to-all | bytes 786432 | tf_op jit(solution)/shard_map/all_to_all | solution.py:866
  167.0 1.3 dynamic_slice.15
  168.4 0.6 constant_dynamic-slice_fusion.ld_ref
  169.0 26.5 %scan_forward.1 = (bf16[1024,512]{1,0:T(8,128)(2,1)}, f32[1024,512]{1,0:T(8,128)}, bf16[1024,512]{1,0:T(8,128)(2,1)}, f32[1024,512]{1,0:T(8,128)}, f32[16384,512...) custom-call(bf16[8,192,128]{2,1,0:T(8,128)(2,1)} %bitcast.64, ...), custom_call_target="tpu_custom_call" | custom-call | flops 40000000000 | bytes 44040192 | tf_op jit(solution)/shard_map/scan_forward/pallas_call | solution.py:450
  195.5 2.3 copy.50
  197.8 6.9 %output_wgrad_send.1 = bf16[3,256,2048]{2,1,0:T(8,128)(2,1)} custom-call(s32[1]{0:T(128)} %bitcast.15.pos_ref.refs_0_, bf16[512,1024]{1,0:T(8,128)(2,1)} %bitcast.58, bf16[1024,2048]{1,0:T(8,128)(2,1)} %all-gather.6.cloned.1.call-done.g_ref.x_ref, s32[1,1024]{1,0:T(1,128)} %modl_ref.3), custom_call_target="tpu_custom_call" | custom-call | flops 3221225472 | bytes 11010048 | tf_op jit(solution)/shard_map/output_wgrad_send/pallas_call | solution.py:320
  204.7 11.7 %output_stage.1 = bf16[1024,2048]{1,0:T(8,128)(2,1)} custom-call(bf16[1024,512]{1,0:T(8,128)(2,1)} %get-tuple-element.56.x_ref, bf16[3,512,2048]{2,1,0:T(8,128)(2,1)} %w_ref.3, s32[1024,1]{1,0:T(8,128)} %copy.47.modc_ref.refs_5_), custom_call_target="tpu_custom_call" | custom-call | flops 6442450944 | bytes 11534336 | tf_op jit(solution)/shard_map/output_stage/pallas_call | solution.py:160
  216.5 12.5 %gated_grads.1 = (bf16[1024,512]{1,0:T(8,128)(2,1)}, bf16[1024,512]{1,0:T(8,128)(2,1)}) custom-call(bf16[1024,2048]{1,0:T(8,128)(2,1)} %all-gather.6.cloned.1.call-done.g_ref.x_ref, bf16[3,512,2048]{2,1,0:T(8,128)(2,1)} %w_ref.3, s32[1024,1]{1,0:T(8,128)} %copy.47.modc_ref.refs_5_, f32[1024,512]{1,0:T(8,128)} %get-tuple-element.58.scanned_ref, ...), custom_call_target="tpu_custom_call" | custom-call | flops 6442450944 | bytes 15728640 | tf_op jit(solution)/shard_map/gated_grads/pallas_call | solution.py:196
  229.0 1.3 collective-permute-start.3
  230.3 1.7 copy-done.22
  232.0 7.4 %output_wgrad_keep.1 = bf16[3,256,2048]{2,1,0:T(8,128)(2,1)} custom-call(s32[1]{0:T(128)} %bitcast.13.pos_ref.refs_0_, bf16[512,1024]{1,0:T(8,128)(2,1)} %bitcast.59, bf16[1024,2048]{1,0:T(8,128)(2,1)} %all-gather.6.cloned.1.call-done.g_ref.x_ref, s32[1,1024]{1,0:T(1,128)} %modl_ref.3, bf16[3,256,2048]{2,1,0:T(8,128)(2,1)} %copy-done.22), custom_call_target="tpu_custom_call" | custom-call | flops 3221225472 | bytes 11010048 | tf_op jit(solution)/shard_map/output_wgrad_keep/pallas_call | solution.py:320
  239.4 0.7 collective-permute-start.4
  240.1 45.4 %scan_backward.1 = (bf16[1024,512]{1,0:T(8,128)(2,1)}, bf16[8,160,128]{2,1,0:T(8,128)(2,1)}, f32[16,512]{1,0:T(8,128)}, f32[1,512]{1,0:T(1,128)}, f32[3,512]{1,0:T(4,128)}, /*index=5*/f32[384,512]{1,0:T(8,128)}) custom-call(bf16[8,192,128]{2,1,0:T(8,128)(2,1)} %bitcast.65, bf16[1024,512]{1,0:T(8,128)(2,1)} %get-tuple-element.54.act_ref, ...), custom_call_target="tpu_custom_call" | custom-call | flops 60000002048 | bytes 44040192 | tf_op jit(solution)/shard_map/scan_backward/pallas_call | solution.py:601
  285.6 4.1 all-to-all-start.2
  289.7 1.0 copy.54.refs_6_
  290.7 10.9 %all-to-all-done.2 = bf16[8,160,128]{2,1,0:T(8,128)(2,1)} async-done(((bf16[8,160,128]{2,1,0:T(8,128)(2,1)}), bf16[8,160,128]{2,1,0:T(8,128)(2,1)}, u32[]{:S(2)}, u32[]{:S(2)}) %all-to-all-start.2) | async-done | bytes 327712 | tf_op jit(solution)/shard_map/all_to_all | solution.py:866
  301.6 1.0 reduce_sum.53
  302.6 0.7 broadcast_in_dim.32
  303.4 4.1 all-to-all-start.3
  307.8 12.3 %gate_wgrad_send.1 = bf16[3,1024,512]{2,1,0:T(8,128)(2,1)} custom-call(s32[1]{0:T(128)} %bitcast.15.pos_ref.refs_0_, bf16[1024,2048]{1,0:T(8,128)(2,1)} %all-gather.4.cloned.1.call-done.x_ref.refs_1_, bf16[1024,2048]{1,0:T(8,128)(2,1)} %all-gather.8.cloned.1.call-done.refs_2_, bf16[1024,512]{1,0:T(8,128)(2,1)} %get-tuple-element.59.refs_3_.gg_ref, ...), custom_call_target="tpu_custom_call" | custom-call | flops 6442450944 | bytes 12582912 | tf_op jit(solution)/shard_map/gate_wgrad_send/pallas_call | solution.py:286
  320.1 2.1 collective-permute-done.4
  322.1 12.8 %conv_backward.1 = (bf16[1024,512]{1,0:T(8,128)(2,1)}, f32[3,160,512]{2,1,0:T(8,128)}, f32[8,512]{1,0:T(8,128)}) custom-call(bf16[8,160,128]{2,1,0:T(8,128)(2,1)} %all-to-all-done.3.gp_ref, bf16[3,160,512]{2,1,0:T(8,128)(2,1)} %bitcast.85, bf16[1024,512]{1,0:T(8,128)(2,1)} %get-tuple-element.73.gas_ref, bf16[1024,512]{1,0:T(8,128)(2,1)} %get-tuple-element.74.ci_ref, ...), custom_call_target="tpu_custom_call" | custom-call | flops 2013265920 | bytes 5242880 | tf_op jit(solution)/shard_map/conv_backward/pallas_call | solution.py:699
  335.0 1.4 collective-permute-start.6
  336.4 18.2 %input_dgrad.1 = (bf16[1024,2048]{1,0:T(8,128)(2,1)}, f32[1,2048]{1,0:T(1,128)}) custom-call(bf16[1024,512]{1,0:T(8,128)(2,1)} %get-tuple-element.75.gc_ref.refs_3_, bf16[1024,512]{1,0:T(8,128)(2,1)} %get-tuple-element.59.refs_3_.gg_ref, bf16[3,2048,1024]{2,1,0:T(8,128)(2,1)} %reshape.117.wc_ref.wg_ref.w_ref, s32[1024,1]{1,0:T(8,128)} %copy.47.modc_ref.refs_5_, ...), custom_call_target="tpu_custom_call" | custom-call | flops 12884901888 | bytes 23068672 | tf_op jit(solution)/shard_map/input_dgrad/pallas_call | solution.py:235
  354.8 5.1 %collective-permute-done.6.refs_4_ = bf16[1024,512]{1,0:T(8,128)(2,1)S(1)} collective-permute-done((bf16[1024,512]{1,0:T(8,128)(2,1)}, bf16[1024,512]{1,0:T(8,128)(2,1)S(1)}, u32[]{:S(2)}, u32[]{:S(2)}) %collective-permute-start.6) | collective-permute-done | bytes 1048608 | tf_op jit(solution)/shard_map/ppermute | solution.py:825
  359.9 1.0 copy-done.23
  360.8 12.2 %conv_wgrad_send.1 = bf16[3,1024,512]{2,1,0:T(8,128)(2,1)} custom-call(s32[1]{0:T(128)} %bitcast.15.pos_ref.refs_0_, bf16[1024,2048]{1,0:T(8,128)(2,1)} %all-gather.4.cloned.1.call-done.x_ref.refs_1_, bf16[1024,2048]{1,0:T(8,128)(2,1)} %all-gather.8.cloned.1.call-done.refs_2_, bf16[1024,512]{1,0:T(8,128)(2,1)} %get-tuple-element.75.gc_ref.refs_3_, ...), custom_call_target="tpu_custom_call" | custom-call | flops 6442450944 | bytes 12582912 | tf_op jit(solution)/shard_map/conv_wgrad_send/pallas_call | solution.py:286
  373.6 0.7 reduce.4
  375.3 4.3 add_convert_fusion.mine_ref
  380.2 13.6 %gate_wgrad_keep.1.gate_ref = bf16[3,1024,512]{2,1,0:T(8,128)(2,1)} custom-call(s32[1]{0:T(128)} %bitcast.13.pos_ref.refs_0_, bf16[1024,2048]{1,0:T(8,128)(2,1)} %all-gather.4.cloned.1.call-done.x_ref.refs_1_, bf16[1024,2048]{1,0:T(8,128)(2,1)} %all-gather.8.cloned.1.call-done.refs_2_, bf16[1024,512]{1,0:T(8,128)(2,1)} %get-tuple-element.59.refs_3_.gg_ref, ...), custom_call_target="tpu_custom_call" | custom-call | flops 6442450944 | bytes 12582912 | tf_op jit(solution)/shard_map/gate_wgrad_keep/pallas_call | solution.py:286
  394.2 13.2 %conv_wgrad_keep.1.conv_ref = bf16[3,1024,512]{2,1,0:T(8,128)(2,1)} custom-call(s32[1]{0:T(128)} %bitcast.13.pos_ref.refs_0_, bf16[1024,2048]{1,0:T(8,128)(2,1)} %all-gather.4.cloned.1.call-done.x_ref.refs_1_, bf16[1024,2048]{1,0:T(8,128)(2,1)} %all-gather.8.cloned.1.call-done.refs_2_, bf16[1024,512]{1,0:T(8,128)(2,1)} %get-tuple-element.75.gc_ref.refs_3_, ...), custom_call_target="tpu_custom_call" | custom-call | flops 6442450944 | bytes 12582912 | tf_op jit(solution)/shard_map/conv_wgrad_keep/pallas_call | solution.py:286
  407.6 0.9 reduce-precision_convert_fusion.1
  408.5 1.7 reduce-precision_convert_fusion
  410.1 1.0 pad_maximum_fusion.1
  411.1 1.6 collective-permute-start.7
  412.7 10.2 %join_halves.1 = f32[3,512,2048]{2,1,0:T(8,128)} custom-call(s32[1]{0:T(128)} %bitcast.13.pos_ref.refs_0_, bf16[3,256,2048]{2,1,0:T(8,128)(2,1)} %copy-done.2, bf16[3,256,2048]{2,1,0:T(8,128)(2,1)} %collective-permute-done.10.got_ref), custom_call_target="tpu_custom_call" | custom-call | bytes 18874368 | tf_op jit(solution)/shard_map/join_halves/pallas_call | solution.py:799
  422.9 9.2 %place_input_grad.2.rest_0_ = f32[3,16384,128]{2,1,0:T(8,128)} custom-call(s32[1]{0:T(128)} %bitcast.13.pos_ref.refs_0_, bf16[3,1024,512]{2,1,0:T(8,128)(2,1)} %conv_wgrad_keep.1.conv_ref, bf16[3,1024,512]{2,1,0:T(8,128)(2,1)} %gate_wgrad_keep.1.gate_ref), custom_call_target="tpu_custom_call" | custom-call | bytes 18874368 | tf_op jit(solution)/shard_map/place_input_grad/pallas_call | solution.py:763
  432.1 2.7 collective-permute-done.7
  434.8 0.9 add_add_fusion
  435.7 1.5 collective-permute-start.11
  437.2 2.8 collective-permute-done.11
  440.1 4.9 %collective-permute-done.12 = f32[2,26,512]{2,1,0:T(8,128)S(1)} collective-permute-done((f32[2,26,512]{2,1,0:T(8,128)S(1)}, f32[2,26,512]{2,1,0:T(8,128)S(1)}, u32[]{:S(2)}, u32[]{:S(2)}) %collective-permute-start.12) | collective-permute-done | bytes 106528 | tf_op jit(solution)/shard_map/ppermute | solution.py:879
  445.1 0.8 collective-permute-start.13
  445.9 1.7 convert_add_fusion.1
  447.6 1.0 slice.133
  448.6 0.9 slice.134
  449.5 0.6 slice.135
  450.1 9.2 %place_input_grad.3 = f32[3,16384,128]{2,1,0:T(8,128)} custom-call(s32[1]{0:T(128)} %bitcast.15.pos_ref.refs_0_, bf16[3,1024,512]{2,1,0:T(8,128)(2,1)} %collective-permute-done.14.conv_ref, bf16[3,1024,512]{2,1,0:T(8,128)(2,1)} %collective-permute-done.15.gate_ref, f32[3,16384,128]{2,1,0:T(8,128)} %place_input_grad.2.rest_0_), custom_call_target="tpu_custom_call", output_to_operand_aliasing={{}: (3, {})} | custom-call | bytes 18874368 | tf_op jit(solution)/shard_map/place_input_grad/pallas_call | solution.py:763
  459.5 0.6 slice.130
  460.2 0.6 fusion.16
  461.1 0.6 copy.66
  461.7 0.7 copy.65
  462.5 1.6 fusion.7
  (103 shorter events, 4.8 us)
Async XLA Ops:
  7.2 161.2 %copy-start = (f32[16,4096]{1,0:T(8,128)S(1)}, f32[16,4096]{1,0:T(8,128)}, u32[]{:S(2)}) copy-start(f32[16,4096]{1,0:T(8,128)} %param.21) | copy-start | bytes 786436
  7.2 80.8 %all-gather.4.cloned.1.call-start = ((), (), s32[]{:S(2)}) async-start(), calls=%async_computation.6 | async-start | bytes 4718592 | tf_op jit(solution)/shard_map/all_gather | solution.py:923
  9.1 0.6 copy-start.19
  11.7 76.3 %copy-start.17 = (s32[1,1024]{1,0:T(1,128)S(1)}, s32[1,1024]{1,0:T(1,128)}, u32[]{:S(2)}) copy-start(s32[1,1024]{1,0:T(1,128)} %modl_ref.3) | copy-start | bytes 12292
  11.7 186.1 %all-gather.6.cloned.1.call-start = ((), (), s32[]{:S(2)}) async-start(), calls=%async_computation.8 | async-start | bytes 4718592 | tf_op jit(solution)/shard_map/all_gather | solution.py:924
  11.8 24.0 %collective-permute-start.1 = (bf16[128,2048]{1,0:T(8,128)(2,1)}, bf16[128,2048]{1,0:T(8,128)(2,1)S(1)}, u32[]{:S(2)}, u32[]{:S(2)}) collective-permute-start(bf16[128,2048]{1,0:T(8,128)(2,1)} %fusion.3), channel_id=1, source_target_pairs={{0,16},{8,24},{16,0},{24,8},{1,17},{9,25},{17,1},{25,9},{2,18},{10... | collective-permute-start | bytes 1572872 | tf_op jit(solution)/shard_map/ppermute | solution.py:825
  14.8 21.0 %collective-permute-start = (s32[1,1024]{1,0:T(1,128)}, s32[1,1024]{1,0:T(1,128)S(1)}, u32[]{:S(2)}, u32[]{:S(2)}) collective-permute-start(s32[1,1024]{1,0:T(1,128)} %modl_ref.3), channel_id=1, source_target_pairs={{0,16},{8,24},{16,0},{24,8},{1,17},{9,25},{17,1},{25,9},{2,18},{10... | collective-permute-start | bytes 12296 | tf_op jit(solution)/shard_map/ppermute | solution.py:825
  35.8 82.3 %copy-start.10 = (bf16[128,2048]{1,0:T(8,128)(2,1)}, bf16[128,2048]{1,0:T(8,128)(2,1)S(1)}, u32[]{:S(2)}) copy-start(bf16[128,2048]{1,0:T(8,128)(2,1)S(1)} %collective-permute-done.1) | copy-start | bytes 1572868
  88.0 219.8 %all-gather.8.cloned.1.call-start = ((), (), s32[]{:S(2)}) async-start(), calls=%async_computation.9 | async-start | bytes 4718592 | tf_op jit(solution)/shard_map/all_gather | solution.py:936
  166.8 213.4 %reduce-scatter.3.cloned.1.call-start = ((), (), s32[]{:S(2)}) async-start(), calls=%async_computation.7 | async-start | bytes 4718592 | tf_op jit(solution)/shard_map/reduce_scatter | solution.py:941
  204.7 25.6 %collective-permute-start.2 = (bf16[3,256,2048]{2,1,0:T(8,128)(2,1)}, bf16[3,256,2048]{2,1,0:T(8,128)(2,1)S(1)}, u32[]{:S(2)}, u32[]{:S(2)}) collective-permute-start(bf16[3,256,2048]{2,1,0:T(8,128)(2,1)} %output_wgrad_send.1), channel_id=1, source_target_pairs={{0,8},{8,0},{16,24},{24,16},{1,9},{9,1},{17,25},{25,17},{2,10},{10... | collective-permute-start | bytes 9437192 | tf_op jit(solution)/shard_map/ppermute | solution.py:819
  229.0 78.8 %collective-permute-start.3 = (bf16[1024,512]{1,0:T(8,128)(2,1)}, bf16[1024,512]{1,0:T(8,128)(2,1)}, u32[]{:S(2)}, u32[]{:S(2)}) collective-permute-start(bf16[1024,512]{1,0:T(8,128)(2,1)} %get-tuple-element.59.refs_3_.gg_ref), channel_id=1, source_target_pairs={{0,16},{8,24},{16,0},{24,8},{1,17},{9,25},{17,1},{25,9},{2,18},{10... | collective-permute-start | bytes 3145736 | tf_op jit(solution)/shard_map/ppermute | solution.py:825
  230.3 1.7 copy-start.22
  239.4 82.7 %collective-permute-start.4 = (bf16[3,256,2048]{2,1,0:T(8,128)(2,1)}, bf16[3,256,2048]{2,1,0:T(8,128)(2,1)S(1)}, u32[]{:S(2)}, u32[]{:S(2)}) collective-permute-start(bf16[3,256,2048]{2,1,0:T(8,128)(2,1)} %output_wgrad_keep.1), channel_id=1, source_target_pairs={{0,16},{8,24},{16,0},{24,8},{1,17},{9,25},{17,1},{25,9},{2,18},{10... | collective-permute-start | bytes 9437192 | tf_op jit(solution)/shard_map/ppermute | solution.py:825
  285.6 16.1 %all-to-all-start.2 = ((bf16[8,160,128]{2,1,0:T(8,128)(2,1)}), bf16[8,160,128]{2,1,0:T(8,128)(2,1)}, u32[]{:S(2)}, u32[]{:S(2)}) async-start(bf16[8,160,128]{2,1,0:T(8,128)(2,1)} %get-tuple-element.69), calls=%async_computation.3 | async-start | bytes 655360 | tf_op jit(solution)/shard_map/all_to_all | solution.py:866
  303.4 16.7 %all-to-all-start.3 = ((bf16[8,160,128]{2,1,0:T(8,128)(2,1)}), bf16[8,160,128]{2,1,0:T(8,128)(2,1)}, u32[]{:S(2)}, u32[]{:S(2)}) async-start(bf16[8,160,128]{2,1,0:T(8,128)(2,1)} %broadcast_in_dim.32), calls=%async_computation.4 | async-start | bytes 655360 | tf_op jit(solution)/shard_map/all_to_all | solution.py:866
  307.5 142.7 %reduce-scatter.5.cloned.1.call-start = ((), (), s32[]{:S(2)}) async-start(), calls=%async_computation.10 | async-start | bytes 4718592 | tf_op jit(solution)/shard_map/reduce_scatter | solution.py:971
  322.1 12.9 %copy-start.5 = (bf16[3,256,2048]{2,1,0:T(8,128)(2,1)}, bf16[3,256,2048]{2,1,0:T(8,128)(2,1)S(1)}, u32[]{:S(2)}) copy-start(bf16[3,256,2048]{2,1,0:T(8,128)(2,1)S(1)} %collective-permute-done.4) | copy-start | bytes 9437188
  335.0 24.9 %collective-permute-start.6 = (bf16[1024,512]{1,0:T(8,128)(2,1)}, bf16[1024,512]{1,0:T(8,128)(2,1)S(1)}, u32[]{:S(2)}, u32[]{:S(2)}) collective-permute-start(bf16[1024,512]{1,0:T(8,128)(2,1)} %get-tuple-element.75.gc_ref.refs_3_), channel_id=1, source_target_pairs={{0,16},{8,24},{16,0},{24,8},{1,17},{9,25},{17,1},{25,9},{2,18},{10... | collective-permute-start | bytes 3145736 | tf_op jit(solution)/shard_map/ppermute | solution.py:825
  354.6 19.0 %copy-start.16 = (f32[1,2048]{1,0:T(1,128)S(1)}, f32[1,2048]{1,0:T(1,128)}, u32[]{:S(2)}) copy-start(f32[1,2048]{1,0:T(1,128)} %get-tuple-element.82) | copy-start | bytes 24580
  354.6 19.7 %copy-start.13 = (f32[16,512]{1,0:T(8,128)S(1)}, f32[16,512]{1,0:T(8,128)}, u32[]{:S(2)}) copy-start(f32[16,512]{1,0:T(8,128)} %get-tuple-element.79) | copy-start | bytes 98308
  354.6 19.7 %copy-start.14 = (f32[8,512]{1,0:T(8,128)S(1)}, f32[8,512]{1,0:T(8,128)}, u32[]{:S(2)}) copy-start(f32[8,512]{1,0:T(8,128)} %get-tuple-element.80) | copy-start | bytes 49156
  354.7 19.7 %copy-start.15 = (f32[3,512]{1,0:T(4,128)S(1)}, f32[3,512]{1,0:T(4,128)}, u32[]{:S(2)}) copy-start(f32[3,512]{1,0:T(4,128)} %get-tuple-element.83) | copy-start | bytes 18436
  354.7 19.7 %copy-start.18 = (f32[1,512]{1,0:T(1,128)S(1)}, f32[1,512]{1,0:T(1,128)}, u32[]{:S(2)}) copy-start(f32[1,512]{1,0:T(1,128)} %get-tuple-element.81) | copy-start | bytes 6148
  354.7 19.8 %copy-start.8 = (f32[3,160,512]{2,1,0:T(8,128)S(1)}, f32[3,160,512]{2,1,0:T(8,128)}, u32[]{:S(2)}) copy-start(f32[3,160,512]{2,1,0:T(8,128)} %get-tuple-element.78) | copy-start | bytes 2949124
  354.7 19.8 %copy-start.9 = (f32[384,512]{1,0:T(8,128)S(1)}, f32[384,512]{1,0:T(8,128)}, u32[]{:S(2)}) copy-start(f32[384,512]{1,0:T(8,128)} %get-tuple-element.77) | copy-start | bytes 2359300
  354.7 25.5 %collective-permute-start.9 = (bf16[3,1024,512]{2,1,0:T(8,128)(2,1)}, bf16[3,1024,512]{2,1,0:T(8,128)(2,1)}, u32[]{:S(2)}, u32[]{:S(2)}) collective-permute-start(bf16[3,1024,512]{2,1,0:T(8,128)(2,1)} %gate_wgrad_send.1), channel_id=1, source_target_pairs={{0,8},{8,0},{16,24},{24,16},{1,9},{9,1},{17,25},{25,17},{2,10},{10... | collective-permute-start | bytes 9437192 | tf_op jit(solution)/shard_map/ppermute | solution.py:819
  359.9 1.0 copy-start.23
  373.1 21.1 %collective-permute-start.8 = (bf16[3,1024,512]{2,1,0:T(8,128)(2,1)}, bf16[3,1024,512]{2,1,0:T(8,128)(2,1)}, u32[]{:S(2)}, u32[]{:S(2)}) collective-permute-start(bf16[3,1024,512]{2,1,0:T(8,128)(2,1)} %conv_wgrad_send.1), channel_id=1, source_target_pairs={{0,8},{8,0},{16,24},{24,16},{1,9},{9,1},{17,25},{25,17},{2,10},{10... | collective-permute-start | bytes 9437192 | tf_op jit(solution)/shard_map/ppermute | solution.py:819
  374.7 4.9 %copy-start.4 = (bf16[922,512]{1,0:T(8,128)(2,1)}, bf16[922,512]{1,0:T(8,128)(2,1)S(1)}, u32[]{:S(2)}) copy-start(bf16[922,512]{1,0:T(8,128)(2,1)S(1)} %pad_maximum_fusion) | copy-start | bytes 2832388
  374.7 5.5 %collective-permute-start.5 = (bf16[922,512]{1,0:T(8,128)(2,1)S(1)}, bf16[922,512]{1,0:T(8,128)(2,1)}, u32[]{:S(2)}, u32[]{:S(2)}) collective-permute-start(bf16[922,512]{1,0:T(8,128)(2,1)S(1)} %pad_maximum_fusion), channel_id=1, source_target_pairs={{0,8},{8,0},{16,24},{24,16},{1,9},{9,1},{17,25},{25,17},{2,10},{10... | collective-permute-start | bytes 2832392 | tf_op jit(solution)/shard_map/ppermute | solution.py:819
  379.6 14.3 %copy-start.2 = (bf16[3,256,2048]{2,1,0:T(8,128)(2,1)}, bf16[3,256,2048]{2,1,0:T(8,128)(2,1)S(1)}, u32[]{:S(2)}) copy-start(bf16[3,256,2048]{2,1,0:T(8,128)(2,1)S(1)} %add_convert_fusion.mine_ref) | copy-start | bytes 9437188
  379.6 33.1 %collective-permute-start.10 = (bf16[3,256,2048]{2,1,0:T(8,128)(2,1)S(1)}, bf16[3,256,2048]{2,1,0:T(8,128)(2,1)}, u32[]{:S(2)}, u32[]{:S(2)}) collective-permute-start(bf16[3,256,2048]{2,1,0:T(8,128)(2,1)S(1)} %add_convert_fusion.mine_ref), channel_id=1, source_target_pairs={{0,8},{8,0},{16,24},{24,16},{1,9},{9,1},{17,25},{25,17},{2,10},{10... | collective-permute-start | bytes 9437192 | tf_op jit(solution)/shard_map/ppermute | solution.py:819
  393.9 56.3 %collective-permute-start.15 = (bf16[3,1024,512]{2,1,0:T(8,128)(2,1)}, bf16[3,1024,512]{2,1,0:T(8,128)(2,1)}, u32[]{:S(2)}, u32[]{:S(2)}) collective-permute-start(bf16[3,1024,512]{2,1,0:T(8,128)(2,1)} %gate_wgrad_keep.1.gate_ref), channel_id=1, source_target_pairs={{0,8},{8,0},{16,24},{24,16},{1,9},{9,1},{17,25},{25,17},{2,10},{10... | collective-permute-start | bytes 9437192 | tf_op jit(solution)/shard_map/ppermute | solution.py:819
  407.4 42.7 %collective-permute-start.14 = (bf16[3,1024,512]{2,1,0:T(8,128)(2,1)}, bf16[3,1024,512]{2,1,0:T(8,128)(2,1)}, u32[]{:S(2)}, u32[]{:S(2)}) collective-permute-start(bf16[3,1024,512]{2,1,0:T(8,128)(2,1)} %conv_wgrad_keep.1.conv_ref), channel_id=1, source_target_pairs={{0,8},{8,0},{16,24},{24,16},{1,9},{9,1},{17,25},{25,17},{2,10},{10... | collective-permute-start | bytes 9437192 | tf_op jit(solution)/shard_map/ppermute | solution.py:819
  411.1 23.6 %collective-permute-start.7 = (bf16[922,512]{1,0:T(8,128)(2,1)}, bf16[922,512]{1,0:T(8,128)(2,1)}, u32[]{:S(2)}, u32[]{:S(2)}) collective-permute-start(bf16[922,512]{1,0:T(8,128)(2,1)} %pad_maximum_fusion.1), channel_id=1, source_target_pairs={{0,16},{8,24},{16,0},{24,8},{1,17},{9,25},{17,1},{25,9},{2,18},{10... | collective-permute-start | bytes 2832392 | tf_op jit(solution)/shard_map/ppermute | solution.py:825
  435.7 4.3 collective-permute-start.11
  440.0 5.0 %collective-permute-start.12 = (f32[2,26,512]{2,1,0:T(8,128)S(1)}, f32[2,26,512]{2,1,0:T(8,128)S(1)}, u32[]{:S(2)}, u32[]{:S(2)}) collective-permute-start(f32[2,26,512]{2,1,0:T(8,128)S(1)} %pad_maximum_fusion.4), channel_id=1, source_target_pairs={{0,2},{1,3},{2,0},{3,1},{4,6},{5,7},{6,4},{7,5},{8,10},{9,11},{10,... | collective-permute-start | bytes 319496 | tf_op jit(solution)/shard_map/ppermute | solution.py:879
  445.1 14.3 %collective-permute-start.13 = (f32[4,26,512]{2,1,0:T(8,128)S(1)}, f32[4,26,512]{2,1,0:T(8,128)S(1)}, u32[]{:S(2)}, u32[]{:S(2)}) collective-permute-start(f32[4,26,512]{2,1,0:T(8,128)S(1)} %pad_maximum_fusion.3), channel_id=1, source_target_pairs={{0,4},{1,5},{2,6},{3,7},{4,0},{5,1},{6,2},{7,3},{8,12},{9,13},{10,... | collective-permute-start | bytes 638984 | tf_op jit(solution)/shard_map/ppermute | solution.py:879
  459.3 1.5 copy-start.3
  459.3 1.5 copy-start.7
  459.3 1.5 copy-start.12
  459.3 3.1 copy-start.6
  459.4 3.1 copy-start.11
  459.4 3.1 copy-start.20
  459.4 3.1 copy-start.21
  459.5 4.6 copy-start.1
Sparse Core Ops, SparseCore 0:
  11.8 76.0 all-gather.3
  90.1 83.6 all-gather.5
  176.5 72.3 all-gather.7
  252.4 92.8 reduce-scatter.2
  354.7 86.0 reduce-scatter.4

commit v6 on v5

--- a/solution.py
+++ b/solution.py
@@ -411,8 +411,8 @@
 
     def positions(i, carry):
         st = list(carry)
-        for j in range(UNROLL):
-            t = i * UNROLL + j
+        for j in range(8):
+            t = i * 8 + j
             at = pl.multiple_of(t * 16, 16)
             d_row, u_row = row_of(d_s, t), row_of(u_s, t)
             for k in range(tiles):
@@ -430,7 +430,7 @@
     first = tuple(
         state[8 * h : 8 * h + 8, k * LANES : (k + 1) * LANES] for k in range(tiles) for h in range(2)
     )
-    st = lax.fori_loop(0, span // UNROLL, positions, first)
+    st = lax.fori_loop(0, span // 8, positions, first)
     for k in range(tiles):
         for h in range(2):
             state[8 * h : 8 * h + 8, k * LANES : (k + 1) * LANES] = st[2 * k + h]

time: 473 us -> 473 us (level)
  transfers between devices with their start and end apart: 23 -> 23, of which waited for: 8 -> 8; matrix products, arithmetic and copies ran while one was open for 10% -> 10% of each run, Pallas kernels for 53% -> 52%
where the time goes in v6:
time: 473 us; the launch traced here: 471 us
  Pallas kernels  247 us (52%)
  waiting for transfers between devices  80.4 us (17%)
  blocking collectives  48.5 us (10%)
  local copies, waits for them, and re-layouts  39.8 us (8%)
  starting transfers between devices  22.3 us (5%)
  other arithmetic  18.3 us (4%)
  between operations  14.3 us (3%)
    all_gather x1, waiting for transfers between devices, per_device(): x = lax.all_gather(normed, 'own', axis=0, tiled=True)  52.1 us
    pallas_call x4, Pallas kernels, half_wgrad(): pl.pallas_call(functools.partial(wgrad_body, sets=sets, add=got is not No...  51.5 us
    all_to_all x2, blocking collectives, to_owners(): lax.all_to_all(pieces, 'own', split_axis=0, concat_axis=0, tiled=False)  48.5 us
    pallas_call x1, Pallas kernels, scan_backward(): pl.pallas_call(scan_bwd_body, grid=(blocks,), in_specs=[slab(pj.shape[1:]...  45.4 us
    pallas_call x1, Pallas kernels, input_stage(): pl.pallas_call(functools.partial(in_body, rows=rows, block=min(512, rows)...  26.4 us
    pallas_call x1, Pallas kernels, scan_forward(): pl.pallas_call(scan_fwd_body, grid=(blocks,), in_specs=[pl.BlockSpec((1,)...  26 us
    reshape x1, local copies, waits for them, and re-layouts, per_device(): w_in = input_proj.reshape(M, width, 2 * chans)  20.9 us
    pallas_call x2, Pallas kernels, place_input_grad(): pl.pallas_call(body, grid_spec=pltpu.PrefetchScalarGridSpec(num_scalar_pr...  18.4 us
  transfers between devices with their start and end apart: 23, of which 8 were waited for; matrix products, arithmetic and copies ran while one was open for 10% of the time, Pallas kernels for 52%

profile of v6, /device:TPU:0, one launch (start us, length us, event | category | flops | bytes accessed | tf_op | source)
XLA Modules:
  0.0 470.7 jit_solution(12879142226502484508)
XLA Ops:
  7.2 1.3 fusion.1
  9.7 2.0 fusion.3
  11.8 3.0 collective-permute-start.1
  14.9 20.9 %reshape.117.wc_ref.wg_ref.w_ref = bf16[3,2048,1024]{2,1,0:T(8,128)(2,1)} reshape(bf16[3,2048,2,512]{3,2,1,0:T(2,128)(2,1)} %param.15) | data formatting | bytes 25165824 | tf_op jit(solution)/shard_map/reshape | solution.py:910
  35.8 52.1 %all-gather.4.cloned.1.call-done.x_ref.refs_1_ = bf16[1024,2048]{1,0:T(8,128)(2,1)} async-done(((bf16[128,2048]{1,0:T(8,128)(2,1)}), bf16[1024,2048]{1,0:T(8,128)(2,1)}) %all-gather.4.cloned.1.call-update) | async-done | bytes 4194320 | tf_op jit(solution)/shard_map/all_gather | solution.py:923
  88.1 1.0 copy.47.modc_ref.refs_5_
  89.1 1.3 dynamic_slice.13
  90.4 1.3 constant_dynamic-slice_fusion.1.cw_ref
  91.7 26.4 %input_stage.1 = (bf16[1024,512]{1,0:T(8,128)(2,1)}, bf16[1024,512]{1,0:T(8,128)(2,1)}, bf16[1024,512]{1,0:T(8,128)(2,1)}, bf16[8,160,128]{2,1,0:T(8,128)(2,1)}) custom-call(bf16[1024,2048]{1,0:T(8,128)(2,1)} %all-gather.4.cloned.1.call-done.x_ref.refs_1_, bf16[3,2048,1024]{2,1,0:T(8,128)(2,1)} %reshape.117.wc_ref.wg_ref.w_ref, ...), custom_call_target="tpu_custom_call" | custom-call | flops 12884901888 | bytes 16777216 | tf_op jit(solution)/shard_map/input_stage/pallas_call | solution.py:112
  118.1 22.2 %all_to_all.20 = bf16[8,160,128]{2,1,0:T(8,128)(2,1)S(1)} all-to-all(bf16[8,160,128]{2,1,0:T(8,128)(2,1)} %get-tuple-element.53), channel_id=1, replica_groups=mesh['batch'=4,'own'=8] {'own'}, dimensions={0} | all-to-all | bytes 655360 | tf_op jit(solution)/shard_map/all_to_all | solution.py:866
  140.5 26.3 %all_to_all.21 = bf16[8,1,192,128]{3,2,1,0:T(8,128)(2,1)} all-to-all(bf16[8,1,192,128]{3,2,1,0:T(8,128)(2,1)S(1)} %broadcast_in_dim.30), channel_id=1, replica_groups=mesh['batch'=4,'own'=8] {'own'}, dimensions={0} | all-to-all | bytes 786432 | tf_op jit(solution)/shard_map/all_to_all | solution.py:866
  167.0 1.3 dynamic_slice.15
  168.4 0.6 constant_dynamic-slice_fusion.ld_ref
  169.0 26.0 %scan_forward.1 = (bf16[1024,512]{1,0:T(8,128)(2,1)}, f32[1024,512]{1,0:T(8,128)}, bf16[1024,512]{1,0:T(8,128)(2,1)}, f32[1024,512]{1,0:T(8,128)}, f32[16384,512...) custom-call(bf16[8,192,128]{2,1,0:T(8,128)(2,1)} %bitcast.64, ...), custom_call_target="tpu_custom_call" | custom-call | flops 40000000000 | bytes 44040192 | tf_op jit(solution)/shard_map/scan_forward/pallas_call | solution.py:450
  195.0 2.3 copy.50
  197.2 6.9 %output_wgrad_send.1 = bf16[3,256,2048]{2,1,0:T(8,128)(2,1)} custom-call(s32[1]{0:T(128)} %bitcast.15.pos_ref.refs_0_, bf16[512,1024]{1,0:T(8,128)(2,1)} %bitcast.58, bf16[1024,2048]{1,0:T(8,128)(2,1)} %all-gather.6.cloned.1.call-done.g_ref.x_ref, s32[1,1024]{1,0:T(1,128)} %modl_ref.3), custom_call_target="tpu_custom_call" | custom-call | flops 3221225472 | bytes 11010048 | tf_op jit(solution)/shard_map/output_wgrad_send/pallas_call | solution.py:320
  204.1 11.6 %output_stage.1 = bf16[1024,2048]{1,0:T(8,128)(2,1)} custom-call(bf16[1024,512]{1,0:T(8,128)(2,1)} %get-tuple-element.56.x_ref, bf16[3,512,2048]{2,1,0:T(8,128)(2,1)} %w_ref.3, s32[1024,1]{1,0:T(8,128)} %copy.47.modc_ref.refs_5_), custom_call_target="tpu_custom_call" | custom-call | flops 6442450944 | bytes 11534336 | tf_op jit(solution)/shard_map/output_stage/pallas_call | solution.py:160
  215.7 12.5 %gated_grads.1 = (bf16[1024,512]{1,0:T(8,128)(2,1)}, bf16[1024,512]{1,0:T(8,128)(2,1)}) custom-call(bf16[1024,2048]{1,0:T(8,128)(2,1)} %all-gather.6.cloned.1.call-done.g_ref.x_ref, bf16[3,512,2048]{2,1,0:T(8,128)(2,1)} %w_ref.3, s32[1024,1]{1,0:T(8,128)} %copy.47.modc_ref.refs_5_, f32[1024,512]{1,0:T(8,128)} %get-tuple-element.58.scanned_ref, ...), custom_call_target="tpu_custom_call" | custom-call | flops 6442450944 | bytes 15728640 | tf_op jit(solution)/shard_map/gated_grads/pallas_call | solution.py:196
  228.2 1.5 collective-permute-start.3
  229.7 1.7 copy-done.22
  231.4 7.4 %output_wgrad_keep.1 = bf16[3,256,2048]{2,1,0:T(8,128)(2,1)} custom-call(s32[1]{0:T(128)} %bitcast.13.pos_ref.refs_0_, bf16[512,1024]{1,0:T(8,128)(2,1)} %bitcast.59, bf16[1024,2048]{1,0:T(8,128)(2,1)} %all-gather.6.cloned.1.call-done.g_ref.x_ref, s32[1,1024]{1,0:T(1,128)} %modl_ref.3, bf16[3,256,2048]{2,1,0:T(8,128)(2,1)} %copy-done.22), custom_call_target="tpu_custom_call" | custom-call | flops 3221225472 | bytes 11010048 | tf_op jit(solution)/shard_map/output_wgrad_keep/pallas_call | solution.py:320
  238.8 0.6 collective-permute-start.4
  239.5 45.4 %scan_backward.1 = (bf16[1024,512]{1,0:T(8,128)(2,1)}, bf16[8,160,128]{2,1,0:T(8,128)(2,1)}, f32[16,512]{1,0:T(8,128)}, f32[1,512]{1,0:T(1,128)}, f32[3,512]{1,0:T(4,128)}, /*index=5*/f32[384,512]{1,0:T(8,128)}) custom-call(bf16[8,192,128]{2,1,0:T(8,128)(2,1)} %bitcast.65, bf16[1024,512]{1,0:T(8,128)(2,1)} %get-tuple-element.54.act_ref, ...), custom_call_target="tpu_custom_call" | custom-call | flops 60000002048 | bytes 44040192 | tf_op jit(solution)/shard_map/scan_backward/pallas_call | solution.py:601
  284.9 4.1 all-to-all-start.2
  289.0 1.0 copy.54.refs_6_
  290.1 11.6 %all-to-all-done.2 = bf16[8,160,128]{2,1,0:T(8,128)(2,1)} async-done(((bf16[8,160,128]{2,1,0:T(8,128)(2,1)}), bf16[8,160,128]{2,1,0:T(8,128)(2,1)}, u32[]{:S(2)}, u32[]{:S(2)}) %all-to-all-start.2) | async-done | bytes 327712 | tf_op jit(solution)/shard_map/all_to_all | solution.py:866
  301.6 1.0 reduce_sum.53
  302.7 0.7 broadcast_in_dim.32
  303.4 4.1 all-to-all-start.3
  307.8 12.3 %gate_wgrad_send.1 = bf16[3,1024,512]{2,1,0:T(8,128)(2,1)} custom-call(s32[1]{0:T(128)} %bitcast.15.pos_ref.refs_0_, bf16[1024,2048]{1,0:T(8,128)(2,1)} %all-gather.4.cloned.1.call-done.x_ref.refs_1_, bf16[1024,2048]{1,0:T(8,128)(2,1)} %all-gather.8.cloned.1.call-done.refs_2_, bf16[1024,512]{1,0:T(8,128)(2,1)} %get-tuple-element.59.refs_3_.gg_ref, ...), custom_call_target="tpu_custom_call" | custom-call | flops 6442450944 | bytes 12582912 | tf_op jit(solution)/shard_map/gate_wgrad_send/pallas_call | solution.py:286
  320.1 1.4 collective-permute-done.4
  321.4 12.7 %conv_backward.1 = (bf16[1024,512]{1,0:T(8,128)(2,1)}, f32[3,160,512]{2,1,0:T(8,128)}, f32[8,512]{1,0:T(8,128)}) custom-call(bf16[8,160,128]{2,1,0:T(8,128)(2,1)} %all-to-all-done.3.gp_ref, bf16[3,160,512]{2,1,0:T(8,128)(2,1)} %bitcast.85, bf16[1024,512]{1,0:T(8,128)(2,1)} %get-tuple-element.73.gas_ref, bf16[1024,512]{1,0:T(8,128)(2,1)} %get-tuple-element.74.ci_ref, ...), custom_call_target="tpu_custom_call" | custom-call | flops 2013265920 | bytes 5242880 | tf_op jit(solution)/shard_map/conv_backward/pallas_call | solution.py:699
  334.1 1.5 collective-permute-start.6
  335.6 18.2 %input_dgrad.1 = (bf16[1024,2048]{1,0:T(8,128)(2,1)}, f32[1,2048]{1,0:T(1,128)}) custom-call(bf16[1024,512]{1,0:T(8,128)(2,1)} %get-tuple-element.75.gc_ref.refs_3_, bf16[1024,512]{1,0:T(8,128)(2,1)} %get-tuple-element.59.refs_3_.gg_ref, bf16[3,2048,1024]{2,1,0:T(8,128)(2,1)} %reshape.117.wc_ref.wg_ref.w_ref, s32[1024,1]{1,0:T(8,128)} %copy.47.modc_ref.refs_5_, ...), custom_call_target="tpu_custom_call" | custom-call | flops 12884901888 | bytes 23068672 | tf_op jit(solution)/shard_map/input_dgrad/pallas_call | solution.py:235
  354.1 5.1 %collective-permute-done.6.refs_4_ = bf16[1024,512]{1,0:T(8,128)(2,1)S(1)} collective-permute-done((bf16[1024,512]{1,0:T(8,128)(2,1)}, bf16[1024,512]{1,0:T(8,128)(2,1)S(1)}, u32[]{:S(2)}, u32[]{:S(2)}) %collective-permute-start.6) | collective-permute-done | bytes 1048608 | tf_op jit(solution)/shard_map/ppermute | solution.py:825
  359.2 1.0 copy-done.23
  360.2 12.3 %conv_wgrad_send.1 = bf16[3,1024,512]{2,1,0:T(8,128)(2,1)} custom-call(s32[1]{0:T(128)} %bitcast.15.pos_ref.refs_0_, bf16[1024,2048]{1,0:T(8,128)(2,1)} %all-gather.4.cloned.1.call-done.x_ref.refs_1_, bf16[1024,2048]{1,0:T(8,128)(2,1)} %all-gather.8.cloned.1.call-done.refs_2_, bf16[1024,512]{1,0:T(8,128)(2,1)} %get-tuple-element.75.gc_ref.refs_3_, ...), custom_call_target="tpu_custom_call" | custom-call | flops 6442450944 | bytes 12582912 | tf_op jit(solution)/shard_map/conv_wgrad_send/pallas_call | solution.py:286
  372.9 0.7 reduce.4
  374.6 4.3 add_convert_fusion.mine_ref
  379.6 13.8 %gate_wgrad_keep.1.gate_ref = bf16[3,1024,512]{2,1,0:T(8,128)(2,1)} custom-call(s32[1]{0:T(128)} %bitcast.13.pos_ref.refs_0_, bf16[1024,2048]{1,0:T(8,128)(2,1)} %all-gather.4.cloned.1.call-done.x_ref.refs_1_, bf16[1024,2048]{1,0:T(8,128)(2,1)} %all-gather.8.cloned.1.call-done.refs_2_, bf16[1024,512]{1,0:T(8,128)(2,1)} %get-tuple-element.59.refs_3_.gg_ref, ...), custom_call_target="tpu_custom_call" | custom-call | flops 6442450944 | bytes 12582912 | tf_op jit(solution)/shard_map/gate_wgrad_keep/pallas_call | solution.py:286
  393.5 13.2 %conv_wgrad_keep.1.conv_ref = bf16[3,1024,512]{2,1,0:T(8,128)(2,1)} custom-call(s32[1]{0:T(128)} %bitcast.13.pos_ref.refs_0_, bf16[1024,2048]{1,0:T(8,128)(2,1)} %all-gather.4.cloned.1.call-done.x_ref.refs_1_, bf16[1024,2048]{1,0:T(8,128)(2,1)} %all-gather.8.cloned.1.call-done.refs_2_, bf16[1024,512]{1,0:T(8,128)(2,1)} %get-tuple-element.75.gc_ref.refs_3_, ...), custom_call_target="tpu_custom_call" | custom-call | flops 6442450944 | bytes 12582912 | tf_op jit(solution)/shard_map/conv_wgrad_keep/pallas_call | solution.py:286
  407.0 0.9 reduce-precision_convert_fusion.1
  407.9 1.7 reduce-precision_convert_fusion
  409.6 1.0 pad_maximum_fusion.1
  410.6 1.5 collective-permute-start.7
  412.1 10.2 %join_halves.1 = f32[3,512,2048]{2,1,0:T(8,128)} custom-call(s32[1]{0:T(128)} %bitcast.13.pos_ref.refs_0_, bf16[3,256,2048]{2,1,0:T(8,128)(2,1)} %copy-done.2, bf16[3,256,2048]{2,1,0:T(8,128)(2,1)} %collective-permute-done.10.got_ref), custom_call_target="tpu_custom_call" | custom-call | bytes 18874368 | tf_op jit(solution)/shard_map/join_halves/pallas_call | solution.py:799
  422.2 9.2 %place_input_grad.2.rest_0_ = f32[3,16384,128]{2,1,0:T(8,128)} custom-call(s32[1]{0:T(128)} %bitcast.13.pos_ref.refs_0_, bf16[3,1024,512]{2,1,0:T(8,128)(2,1)} %conv_wgrad_keep.1.conv_ref, bf16[3,1024,512]{2,1,0:T(8,128)(2,1)} %gate_wgrad_keep.1.gate_ref), custom_call_target="tpu_custom_call" | custom-call | bytes 18874368 | tf_op jit(solution)/shard_map/place_input_grad/pallas_call | solution.py:763
  431.4 2.6 collective-permute-done.7
  434.1 0.9 add_add_fusion
  435.0 1.4 collective-permute-start.11
  436.4 2.9 collective-permute-done.11
  439.3 0.8 collective-permute-start.12
  440.1 4.3 collective-permute-done.12
  444.4 1.6 collective-permute-start.13
  446.0 1.7 convert_add_fusion.1
  447.7 1.0 slice.133
  448.7 0.9 slice.134
  449.6 0.6 slice.135
  450.2 9.2 %place_input_grad.3 = f32[3,16384,128]{2,1,0:T(8,128)} custom-call(s32[1]{0:T(128)} %bitcast.15.pos_ref.refs_0_, bf16[3,1024,512]{2,1,0:T(8,128)(2,1)} %collective-permute-done.14.conv_ref, bf16[3,1024,512]{2,1,0:T(8,128)(2,1)} %collective-permute-done.15.gate_ref, f32[3,16384,128]{2,1,0:T(8,128)} %place_input_grad.2.rest_0_), custom_call_target="tpu_custom_call", output_to_operand_aliasing={{}: (3, {})} | custom-call | bytes 18874368 | tf_op jit(solution)/shard_map/place_input_grad/pallas_call | solution.py:763
  459.6 0.6 slice.130
  460.3 0.6 fusion.16
  461.2 0.6 copy.66
  461.8 0.7 copy.65
  462.6 1.6 fusion.7
  (103 shorter events, 5.3 us)
Async XLA Ops:
  7.2 161.2 %copy-start = (f32[16,4096]{1,0:T(8,128)S(1)}, f32[16,4096]{1,0:T(8,128)}, u32[]{:S(2)}) copy-start(f32[16,4096]{1,0:T(8,128)} %param.21) | copy-start | bytes 786436
  7.2 80.8 %all-gather.4.cloned.1.call-start = ((), (), s32[]{:S(2)}) async-start(), calls=%async_computation.6 | async-start | bytes 4718592 | tf_op jit(solution)/shard_map/all_gather | solution.py:923
  9.1 0.6 copy-start.19
  11.7 76.3 %copy-start.17 = (s32[1,1024]{1,0:T(1,128)S(1)}, s32[1,1024]{1,0:T(1,128)}, u32[]{:S(2)}) copy-start(s32[1,1024]{1,0:T(1,128)} %modl_ref.3) | copy-start | bytes 12292
  11.7 185.5 %all-gather.6.cloned.1.call-start = ((), (), s32[]{:S(2)}) async-start(), calls=%async_computation.8 | async-start | bytes 4718592 | tf_op jit(solution)/shard_map/all_gather | solution.py:924
  11.8 24.0 %collective-permute-start.1 = (bf16[128,2048]{1,0:T(8,128)(2,1)}, bf16[128,2048]{1,0:T(8,128)(2,1)S(1)}, u32[]{:S(2)}, u32[]{:S(2)}) collective-permute-start(bf16[128,2048]{1,0:T(8,128)(2,1)} %fusion.3), channel_id=1, source_target_pairs={{0,16},{8,24},{16,0},{24,8},{1,17},{9,25},{17,1},{25,9},{2,18},{10... | collective-permute-start | bytes 1572872 | tf_op jit(solution)/shard_map/ppermute | solution.py:825
  14.8 21.0 %collective-permute-start = (s32[1,1024]{1,0:T(1,128)}, s32[1,1024]{1,0:T(1,128)S(1)}, u32[]{:S(2)}, u32[]{:S(2)}) collective-permute-start(s32[1,1024]{1,0:T(1,128)} %modl_ref.3), channel_id=1, source_target_pairs={{0,16},{8,24},{16,0},{24,8},{1,17},{9,25},{17,1},{25,9},{2,18},{10... | collective-permute-start | bytes 12296 | tf_op jit(solution)/shard_map/ppermute | solution.py:825
  35.8 82.3 %copy-start.10 = (bf16[128,2048]{1,0:T(8,128)(2,1)}, bf16[128,2048]{1,0:T(8,128)(2,1)S(1)}, u32[]{:S(2)}) copy-start(bf16[128,2048]{1,0:T(8,128)(2,1)S(1)} %collective-permute-done.1) | copy-start | bytes 1572868
  88.0 219.8 %all-gather.8.cloned.1.call-start = ((), (), s32[]{:S(2)}) async-start(), calls=%async_computation.9 | async-start | bytes 4718592 | tf_op jit(solution)/shard_map/all_gather | solution.py:936
  166.8 212.8 %reduce-scatter.3.cloned.1.call-start = ((), (), s32[]{:S(2)}) async-start(), calls=%async_computation.7 | async-start | bytes 4718592 | tf_op jit(solution)/shard_map/reduce_scatter | solution.py:941
  204.1 25.6 %collective-permute-start.2 = (bf16[3,256,2048]{2,1,0:T(8,128)(2,1)}, bf16[3,256,2048]{2,1,0:T(8,128)(2,1)S(1)}, u32[]{:S(2)}, u32[]{:S(2)}) collective-permute-start(bf16[3,256,2048]{2,1,0:T(8,128)(2,1)} %output_wgrad_send.1), channel_id=1, source_target_pairs={{0,8},{8,0},{16,24},{24,16},{1,9},{9,1},{17,25},{25,17},{2,10},{10... | collective-permute-start | bytes 9437192 | tf_op jit(solution)/shard_map/ppermute | solution.py:819
  228.2 79.5 %collective-permute-start.3 = (bf16[1024,512]{1,0:T(8,128)(2,1)}, bf16[1024,512]{1,0:T(8,128)(2,1)}, u32[]{:S(2)}, u32[]{:S(2)}) collective-permute-start(bf16[1024,512]{1,0:T(8,128)(2,1)} %get-tuple-element.59.refs_3_.gg_ref), channel_id=1, source_target_pairs={{0,16},{8,24},{16,0},{24,8},{1,17},{9,25},{17,1},{25,9},{2,18},{10... | collective-permute-start | bytes 3145736 | tf_op jit(solution)/shard_map/ppermute | solution.py:825
  229.7 1.7 copy-start.22
  238.8 82.6 %collective-permute-start.4 = (bf16[3,256,2048]{2,1,0:T(8,128)(2,1)}, bf16[3,256,2048]{2,1,0:T(8,128)(2,1)S(1)}, u32[]{:S(2)}, u32[]{:S(2)}) collective-permute-start(bf16[3,256,2048]{2,1,0:T(8,128)(2,1)} %output_wgrad_keep.1), channel_id=1, source_target_pairs={{0,16},{8,24},{16,0},{24,8},{1,17},{9,25},{17,1},{25,9},{2,18},{10... | collective-permute-start | bytes 9437192 | tf_op jit(solution)/shard_map/ppermute | solution.py:825
  284.9 16.7 %all-to-all-start.2 = ((bf16[8,160,128]{2,1,0:T(8,128)(2,1)}), bf16[8,160,128]{2,1,0:T(8,128)(2,1)}, u32[]{:S(2)}, u32[]{:S(2)}) async-start(bf16[8,160,128]{2,1,0:T(8,128)(2,1)} %get-tuple-element.69), calls=%async_computation.3 | async-start | bytes 655360 | tf_op jit(solution)/shard_map/all_to_all | solution.py:866
  303.4 16.7 %all-to-all-start.3 = ((bf16[8,160,128]{2,1,0:T(8,128)(2,1)}), bf16[8,160,128]{2,1,0:T(8,128)(2,1)}, u32[]{:S(2)}, u32[]{:S(2)}) async-start(bf16[8,160,128]{2,1,0:T(8,128)(2,1)} %broadcast_in_dim.32), calls=%async_computation.4 | async-start | bytes 655360 | tf_op jit(solution)/shard_map/all_to_all | solution.py:866
  307.5 142.8 %reduce-scatter.5.cloned.1.call-start = ((), (), s32[]{:S(2)}) async-start(), calls=%async_computation.10 | async-start | bytes 4718592 | tf_op jit(solution)/shard_map/reduce_scatter | solution.py:971
  321.4 12.7 %copy-start.5 = (bf16[3,256,2048]{2,1,0:T(8,128)(2,1)}, bf16[3,256,2048]{2,1,0:T(8,128)(2,1)S(1)}, u32[]{:S(2)}) copy-start(bf16[3,256,2048]{2,1,0:T(8,128)(2,1)S(1)} %collective-permute-done.4) | copy-start | bytes 9437188
  334.1 25.1 %collective-permute-start.6 = (bf16[1024,512]{1,0:T(8,128)(2,1)}, bf16[1024,512]{1,0:T(8,128)(2,1)S(1)}, u32[]{:S(2)}, u32[]{:S(2)}) collective-permute-start(bf16[1024,512]{1,0:T(8,128)(2,1)} %get-tuple-element.75.gc_ref.refs_3_), channel_id=1, source_target_pairs={{0,16},{8,24},{16,0},{24,8},{1,17},{9,25},{17,1},{25,9},{2,18},{10... | collective-permute-start | bytes 3145736 | tf_op jit(solution)/shard_map/ppermute | solution.py:825
  353.9 19.0 %copy-start.16 = (f32[1,2048]{1,0:T(1,128)S(1)}, f32[1,2048]{1,0:T(1,128)}, u32[]{:S(2)}) copy-start(f32[1,2048]{1,0:T(1,128)} %get-tuple-element.82) | copy-start | bytes 24580
  353.9 19.7 %copy-start.13 = (f32[16,512]{1,0:T(8,128)S(1)}, f32[16,512]{1,0:T(8,128)}, u32[]{:S(2)}) copy-start(f32[16,512]{1,0:T(8,128)} %get-tuple-element.79) | copy-start | bytes 98308
  353.9 19.7 %copy-start.14 = (f32[8,512]{1,0:T(8,128)S(1)}, f32[8,512]{1,0:T(8,128)}, u32[]{:S(2)}) copy-start(f32[8,512]{1,0:T(8,128)} %get-tuple-element.80) | copy-start | bytes 49156
  353.9 19.7 %copy-start.15 = (f32[3,512]{1,0:T(4,128)S(1)}, f32[3,512]{1,0:T(4,128)}, u32[]{:S(2)}) copy-start(f32[3,512]{1,0:T(4,128)} %get-tuple-element.83) | copy-start | bytes 18436
  353.9 19.7 %copy-start.18 = (f32[1,512]{1,0:T(1,128)S(1)}, f32[1,512]{1,0:T(1,128)}, u32[]{:S(2)}) copy-start(f32[1,512]{1,0:T(1,128)} %get-tuple-element.81) | copy-start | bytes 6148
  353.9 19.9 %copy-start.8 = (f32[3,160,512]{2,1,0:T(8,128)S(1)}, f32[3,160,512]{2,1,0:T(8,128)}, u32[]{:S(2)}) copy-start(f32[3,160,512]{2,1,0:T(8,128)} %get-tuple-element.78) | copy-start | bytes 2949124
  354.0 19.9 %copy-start.9 = (f32[384,512]{1,0:T(8,128)S(1)}, f32[384,512]{1,0:T(8,128)}, u32[]{:S(2)}) copy-start(f32[384,512]{1,0:T(8,128)} %get-tuple-element.77) | copy-start | bytes 2359300
  354.0 25.6 %collective-permute-start.9 = (bf16[3,1024,512]{2,1,0:T(8,128)(2,1)}, bf16[3,1024,512]{2,1,0:T(8,128)(2,1)}, u32[]{:S(2)}, u32[]{:S(2)}) collective-permute-start(bf16[3,1024,512]{2,1,0:T(8,128)(2,1)} %gate_wgrad_send.1), channel_id=1, source_target_pairs={{0,8},{8,0},{16,24},{24,16},{1,9},{9,1},{17,25},{25,17},{2,10},{10... | collective-permute-start | bytes 9437192 | tf_op jit(solution)/shard_map/ppermute | solution.py:819
  359.2 1.0 copy-start.23
  372.4 21.1 %collective-permute-start.8 = (bf16[3,1024,512]{2,1,0:T(8,128)(2,1)}, bf16[3,1024,512]{2,1,0:T(8,128)(2,1)}, u32[]{:S(2)}, u32[]{:S(2)}) collective-permute-start(bf16[3,1024,512]{2,1,0:T(8,128)(2,1)} %conv_wgrad_send.1), channel_id=1, source_target_pairs={{0,8},{8,0},{16,24},{24,16},{1,9},{9,1},{17,25},{25,17},{2,10},{10... | collective-permute-start | bytes 9437192 | tf_op jit(solution)/shard_map/ppermute | solution.py:819
  374.0 4.9 %copy-start.4 = (bf16[922,512]{1,0:T(8,128)(2,1)}, bf16[922,512]{1,0:T(8,128)(2,1)S(1)}, u32[]{:S(2)}) copy-start(bf16[922,512]{1,0:T(8,128)(2,1)S(1)} %pad_maximum_fusion) | copy-start | bytes 2832388
  374.1 5.5 %collective-permute-start.5 = (bf16[922,512]{1,0:T(8,128)(2,1)S(1)}, bf16[922,512]{1,0:T(8,128)(2,1)}, u32[]{:S(2)}, u32[]{:S(2)}) collective-permute-start(bf16[922,512]{1,0:T(8,128)(2,1)S(1)} %pad_maximum_fusion), channel_id=1, source_target_pairs={{0,8},{8,0},{16,24},{24,16},{1,9},{9,1},{17,25},{25,17},{2,10},{10... | collective-permute-start | bytes 2832392 | tf_op jit(solution)/shard_map/ppermute | solution.py:819
  378.9 14.4 %copy-start.2 = (bf16[3,256,2048]{2,1,0:T(8,128)(2,1)}, bf16[3,256,2048]{2,1,0:T(8,128)(2,1)S(1)}, u32[]{:S(2)}) copy-start(bf16[3,256,2048]{2,1,0:T(8,128)(2,1)S(1)} %add_convert_fusion.mine_ref) | copy-start | bytes 9437188
  379.0 33.1 %collective-permute-start.10 = (bf16[3,256,2048]{2,1,0:T(8,128)(2,1)S(1)}, bf16[3,256,2048]{2,1,0:T(8,128)(2,1)}, u32[]{:S(2)}, u32[]{:S(2)}) collective-permute-start(bf16[3,256,2048]{2,1,0:T(8,128)(2,1)S(1)} %add_convert_fusion.mine_ref), channel_id=1, source_target_pairs={{0,8},{8,0},{16,24},{24,16},{1,9},{9,1},{17,25},{25,17},{2,10},{10... | collective-permute-start | bytes 9437192 | tf_op jit(solution)/shard_map/ppermute | solution.py:819
  393.4 56.9 %collective-permute-start.15 = (bf16[3,1024,512]{2,1,0:T(8,128)(2,1)}, bf16[3,1024,512]{2,1,0:T(8,128)(2,1)}, u32[]{:S(2)}, u32[]{:S(2)}) collective-permute-start(bf16[3,1024,512]{2,1,0:T(8,128)(2,1)} %gate_wgrad_keep.1.gate_ref), channel_id=1, source_target_pairs={{0,8},{8,0},{16,24},{24,16},{1,9},{9,1},{17,25},{25,17},{2,10},{10... | collective-permute-start | bytes 9437192 | tf_op jit(solution)/shard_map/ppermute | solution.py:819
  406.7 43.5 %collective-permute-start.14 = (bf16[3,1024,512]{2,1,0:T(8,128)(2,1)}, bf16[3,1024,512]{2,1,0:T(8,128)(2,1)}, u32[]{:S(2)}, u32[]{:S(2)}) collective-permute-start(bf16[3,1024,512]{2,1,0:T(8,128)(2,1)} %conv_wgrad_keep.1.conv_ref), channel_id=1, source_target_pairs={{0,8},{8,0},{16,24},{24,16},{1,9},{9,1},{17,25},{25,17},{2,10},{10... | collective-permute-start | bytes 9437192 | tf_op jit(solution)/shard_map/ppermute | solution.py:819
  410.6 23.4 %collective-permute-start.7 = (bf16[922,512]{1,0:T(8,128)(2,1)}, bf16[922,512]{1,0:T(8,128)(2,1)}, u32[]{:S(2)}, u32[]{:S(2)}) collective-permute-start(bf16[922,512]{1,0:T(8,128)(2,1)} %pad_maximum_fusion.1), channel_id=1, source_target_pairs={{0,16},{8,24},{16,0},{24,8},{1,17},{9,25},{17,1},{25,9},{2,18},{10... | collective-permute-start | bytes 2832392 | tf_op jit(solution)/shard_map/ppermute | solution.py:825
  435.0 4.3 collective-permute-start.11
  439.3 5.0 %collective-permute-start.12 = (f32[2,26,512]{2,1,0:T(8,128)S(1)}, f32[2,26,512]{2,1,0:T(8,128)S(1)}, u32[]{:S(2)}, u32[]{:S(2)}) collective-permute-start(f32[2,26,512]{2,1,0:T(8,128)S(1)} %pad_maximum_fusion.4), channel_id=1, source_target_pairs={{0,2},{1,3},{2,0},{3,1},{4,6},{5,7},{6,4},{7,5},{8,10},{9,11},{10,... | collective-permute-start | bytes 319496 | tf_op jit(solution)/shard_map/ppermute | solution.py:879
  444.4 15.1 %collective-permute-start.13 = (f32[4,26,512]{2,1,0:T(8,128)S(1)}, f32[4,26,512]{2,1,0:T(8,128)S(1)}, u32[]{:S(2)}, u32[]{:S(2)}) collective-permute-start(f32[4,26,512]{2,1,0:T(8,128)S(1)} %pad_maximum_fusion.3), channel_id=1, source_target_pairs={{0,4},{1,5},{2,6},{3,7},{4,0},{5,1},{6,2},{7,3},{8,12},{9,13},{10,... | collective-permute-start | bytes 638984 | tf_op jit(solution)/shard_map/ppermute | solution.py:879
  459.4 1.5 copy-start.3
  459.4 1.5 copy-start.7
  459.4 1.5 copy-start.12
  459.4 3.1 copy-start.6
  459.5 3.1 copy-start.11
  459.5 3.1 copy-start.20
  459.5 3.1 copy-start.21
  459.6 4.6 copy-start.1
Sparse Core Ops, SparseCore 0:
  11.8 76.0 all-gather.3
  90.1 83.6 all-gather.5
  176.5 72.3 all-gather.7
  252.4 92.4 reduce-scatter.2
  354.0 86.8 reduce-scatter.4
